TPU v7x, 256 devices: a whole 4x4x8 slice. The times are simulated.
256 devices in a mesh: ctx: 8 (over y, core), exp: 32 (over x, z).
Axes of the slice: x: 4, y: 4, z: 8, core: 2. Of those that a mesh axis runs over, the one named last changes fastest.
Arguments:
- hidden: bfloat16 [32, 1024, 2048], P('exp', 'ctx'), may hold values from -6 to 6
- queries: bfloat16 [32, 1024, 1536], P('exp', 'ctx'), may hold values from -48 to 48
- latent: bfloat16 [32, 1024, 576], P('exp', 'ctx'), may hold values from -48 to 48
- group_order: int32 [16], replicated, may hold values from 0 to 15, each once
- w_uk: bfloat16 [512, 1024], replicated, may hold values from -0.25 to 0.25
- w_uv: bfloat16 [512, 1024], replicated, may hold values from -0.25 to 0.25
- w_out: bfloat16 [1024, 2048], replicated, may hold values from -0.1875 to 0.1875
- norm_gain: float32 [2048], replicated, may hold values from 0.5 to 1.5
- expert_ids: int32 [32, 1024, 6], P('exp', 'ctx'), may hold values from 0 to 63, all different within a row; in each aligned block of 128 rows (0 to 127, 128 to 255, ..., all dimensions but the last counted through in order) at most 13 rows name the same one
- gate_weights: float32 [32, 1024, 6], P('exp', 'ctx'), may hold values from 0.05 to 0.5
- w_gate: bfloat16 [64, 2048, 1024], P('exp', None, 'ctx'), may hold values from -0.125 to 0.125
- w_up: bfloat16 [64, 2048, 1024], P('exp', None, 'ctx'), may hold values from -0.125 to 0.125
- w_down: bfloat16 [64, 2048, 1024], P('exp', None, 'ctx'), may hold values from -0.1875 to 0.1875
Outputs:
- mixed: bfloat16 [32, 1024, 2048], P('exp', 'ctx')
Inputs may be any that keep to these rules, and one draw needn't show every extreme that they name: `expert_ids`: within each aligned block of 128 rows of a sequence (the rows of one device), each expert is named by at most 13 rows, a bound that some block reaches; each row names 6 different experts. A permutation; stored half-block i of 64 rows holds the positions of half-block group_order[i], in increasing order.
All inputs are finite; a program needn't handle non-finite values.
Results may differ from a plain program's by a relative error of at most 0.011.
Values may be sent and summed in bfloat16 or wider, within the bound.
No kernel may reach another device: no remote copies, remote signals or barrier semaphores. Data moves between devices by JAX's collectives and lax.ppermute only.
A program may use at most 192 MiB of HBM per device.

v0:
```python
import jax
import jax.numpy as jnp
from jax import lax
from jax.sharding import PartitionSpec as P

D = 2048
HEADS = 8
NOPE = 128
ROPE = 64
VDIM = 128
KVR = 512
EXPERTS = 64
TOPK = 6
CAP = 13


EPSILON = 1e-06


def joined_along(blocks, dim):
    blocks = jnp.moveaxis(blocks, 0, dim)
    dims = blocks.shape
    return blocks.reshape(*dims[:dim], dims[dim] * dims[dim + 1], *dims[dim + 2 :])


def from_everyone(shard, axis):
    length = lax.axis_size(axis)
    return lax.all_to_all(
        jnp.broadcast_to(shard[None], (length, *shard.shape)), axis, 0, 0, tiled=True
    )


def gather_directly(shard, axis, dim):
    return joined_along(from_everyone(shard, axis), dim)


def sent_together(arrays, axis, dim, along):
    both = jnp.concatenate(arrays, axis=along)
    out, at, gathered = (lax.all_gather(both, axis, axis=dim, tiled=True), 0, [])
    for a in arrays:
        gathered.append(lax.slice_in_dim(out, at, at + a.shape[along], axis=along))
        at += a.shape[along]
    return tuple(gathered)


def block_slots(block_ids):
    flat_ids = block_ids.reshape(-1)
    onehot = (flat_ids[:, None] == jnp.arange(EXPERTS, dtype=jnp.int32)[None, :]).astype(jnp.int32)
    before = jnp.sum((jnp.cumsum(onehot, axis=0) - onehot) * onehot, axis=1)
    return flat_ids * CAP + before


def expert_block(rows, gate_slice, up_slice, down_slice):
    gate_part = jnp.einsum("sjcd,jdf->sjcf", rows, gate_slice, preferred_element_type=jnp.float32)
    up_part = jnp.einsum("sjcd,jdf->sjcf", rows, up_slice, preferred_element_type=jnp.float32)
    inner = (jax.nn.silu(gate_part) * up_part).astype(jnp.bfloat16)
    return jnp.einsum("sjcf,jdf->sjcd", inner, down_slice, preferred_element_type=jnp.float32)


def body(
    hidden,
    queries,
    latent,
    group_order,
    w_uk,
    w_uv,
    w_out,
    norm_gain,
    expert_ids,
    gate_weights,
    w_gate,
    w_up,
    w_down,
):
    block_rows = hidden.shape[1]
    half_rows = block_rows // 2
    seq_rows = block_rows * lax.axis_size("ctx")
    row_index = jnp.arange(seq_rows, dtype=jnp.int32)
    positions = group_order[row_index // half_rows] * half_rows + row_index % half_rows
    own_positions = lax.dynamic_slice_in_dim(
        positions, lax.axis_index("ctx") * block_rows, block_rows
    )
    own_latent = latent[0]
    whole = gather_directly(own_latent, "ctx", 0)
    content = whole[:, :KVR]
    key_rope = whole[:, KVR:]
    key_nope = jnp.dot(content, w_uk, preferred_element_type=jnp.float32).astype(jnp.bfloat16)
    values = jnp.dot(content, w_uv, preferred_element_type=jnp.float32).astype(jnp.bfloat16)
    query_full = queries[0].reshape(block_rows, HEADS, NOPE + ROPE)
    scores = jnp.einsum(
        "qhd,khd->hqk",
        query_full[:, :, :NOPE],
        key_nope.reshape(seq_rows, HEADS, NOPE),
        preferred_element_type=jnp.float32,
    )
    scores = scores + jnp.einsum(
        "qhr,kr->hqk", query_full[:, :, NOPE:], key_rope, preferred_element_type=jnp.float32
    )
    scores = scores * (NOPE + ROPE) ** (-0.5)
    visible = positions[None, :] <= own_positions[:, None]
    scores = jnp.where(visible[None], scores, -jnp.inf)
    peak = jnp.max(scores, axis=2, keepdims=True)
    expo = jnp.exp(scores - peak)
    totals = jnp.sum(expo, axis=2)
    heads_out = jnp.einsum(
        "hqk,khv->qhv",
        expo.astype(jnp.bfloat16),
        values.reshape(seq_rows, HEADS, VDIM),
        preferred_element_type=jnp.float32,
    )
    heads_out = heads_out / jnp.transpose(totals)[:, :, None]
    attended = heads_out.astype(jnp.bfloat16).reshape(block_rows, HEADS * VDIM)
    residual = (
        hidden[0].astype(jnp.float32) + jnp.dot(attended, w_out, preferred_element_type=jnp.float32)
    ).astype(jnp.bfloat16)
    stream = residual.astype(jnp.float32)
    factor = lax.rsqrt(jnp.mean(stream * stream, axis=1, keepdims=True) + EPSILON)
    normed = (stream * factor * norm_gain).astype(jnp.bfloat16)
    slot_index = block_slots(expert_ids[0])
    slot_count = EXPERTS * CAP
    matches = jnp.arange(slot_count, dtype=jnp.int32)[:, None] == slot_index[None, :]
    selector = jnp.sum(
        matches.reshape(slot_count, block_rows, TOPK).astype(jnp.int32), axis=2
    ).astype(jnp.bfloat16)
    outgoing = jnp.dot(selector, normed, preferred_element_type=jnp.float32).astype(jnp.bfloat16)
    outgoing = outgoing.reshape(lax.axis_size("exp"), w_gate.shape[0], CAP, D)
    received = lax.all_to_all(outgoing, "exp", split_axis=0, concat_axis=0, tiled=True)
    pieces = sent_together((w_gate, w_up, w_down), "ctx", 2, 0)
    expert_out = expert_block(received, pieces[0], pieces[1], pieces[2]).astype(jnp.bfloat16)
    returned = lax.all_to_all(expert_out, "exp", split_axis=0, concat_axis=0, tiled=True).reshape(
        slot_count, D
    )
    picked = jnp.take(returned, slot_index, axis=0).reshape(block_rows, TOPK, D)
    mixture = jnp.sum(gate_weights[0][:, :, None] * picked.astype(jnp.float32), axis=1)
    mixed = (stream + mixture).astype(jnp.bfloat16)
    return mixed[None]


def solution(mesh):
    return jax.shard_map(
        body,
        mesh=mesh,
        in_specs=(
            P("exp", "ctx", None),
            P("exp", "ctx", None),
            P("exp", "ctx", None),
            P(),
            P(),
            P(),
            P(),
            P(),
            P("exp", "ctx", None),
            P("exp", "ctx", None),
            P("exp", None, "ctx"),
            P("exp", None, "ctx"),
            P("exp", None, "ctx"),
        ),
        out_specs=P("exp", "ctx", None),
        check_vma=False,
    )
```

profile of v0, /device:TPU:32, one launch (start us, length us, event | category | flops | bytes accessed | tf_op | source)
XLA Modules:
  0.0 293.1 jit_solution(10620134687416112936)
XLA Ops:
  6.5 3.3 %pad_maximum_fusion = bf16[6,2048,128]{2,1,0:T(8,128)(2,1)} fusion(bf16[2,2048,128]{2,1,0:T(8,128)(2,1)} %param.25, bf16[2,2048,128]{2,1,0:T(8,128)(2,1)} %param.24, bf16[2,2048,128]{2,1,0:T(8,128)(2,1)} %param.23), kind=kLoop, calls=%fused_computation.23 | loop fusion | flops 3145728 | bytes 6291456 | tf_op jit(solution)/shard_map/concatenate | solution.py:38
  9.9 1.3 broadcast_in_dim.44
  11.2 4.5 %all-to-all-start = ((bf16[8,128,576]{1,2,0:T(8,128)(2,1)}), bf16[8,128,576]{1,2,0:T(8,128)(2,1)S(1)}, u32[]{:S(2)}, u32[]{:S(2)}) async-start(bf16[8,128,576]{1,2,0:T(8,128)(2,1)} %broadcast_in_dim.44), calls=%async_computation | async-start | bytes 2359296 | tf_op jit(solution)/shard_map/all_to_all | solution.py:28
  16.3 1.8 reduce-window.6
  19.1 0.7 fusion.49
  19.8 4.3 %compare_select_fusion.2 = s32[1024,1]{0,1:T(1,128)S(1)} fusion(s32[]{:T(128)} %bitcast.12, s32[]{:T(128)} %bitcast.13, s32[]{:T(128)} %bitcast.14, s32[]{:T(128)} %bitcast.15, s32[]{:T(128)} %bitcast.16, s32[]{:T(128)} %bitcast.18, s32[]{:T(128)} %bitcast.17), kind=kLoop, calls=%fused_computation.74 | loop fusion | flops 23552 | bytes 4124 | tf_op jit(solution)/shard_map/gather | solution.py:79
  24.1 5.7 %fusion.44 = s32[1024]{0:T(1024)S(1)} fusion(pred[1024]{0:T(1024)(128)(4,1)S(1)} %compare_reduce_fusion, pred[1024]{0:T(1024)(128)(4,1)S(1)} %compare_reduce_fusion.1, pred[1024]{0:T(1024)(128)(4,1)S(1)} %compare_reduce_fusion.2, pred[1024]{0:T(1024)(128)(4,1)S(1)} %compare_reduce_fusion.3, pred[1024]{0:T(1024)(128)(4,1)S(1)} %compare_reduce_fusion.4, ...), kind=kLoop, calls=%fused_computation.86 | loop fusion | flops 17408 | bytes 17444 | tf_op jit(solution)/shard_map/add | solution.py:79
  30.0 1.1 convert_reduce_fusion
  31.2 3.1 %all-to-all-done = bf16[8,128,576]{1,2,0:T(8,128)(2,1)S(1)} async-done(((bf16[8,128,576]{1,2,0:T(8,128)(2,1)}), bf16[8,128,576]{1,2,0:T(8,128)(2,1)S(1)}, u32[]{:S(2)}, u32[]{:S(2)}) %all-to-all-start) | async-done | bytes 1179680 | tf_op jit(solution)/shard_map/all_to_all | solution.py:28
  34.6 1.3 convolution_convert_fusion.1
  35.9 0.8 fusion.36
  36.7 0.9 fusion.50
  38.9 1.3 convolution_convert_fusion.2
  40.2 0.9 fusion.28
  41.2 1.3 copy-done.4
  42.6 0.8 multiply_reduce_fusion.1
  43.4 1.0 copy-done.2
  44.4 1.1 convolution_convert_fusion
  45.6 3.0 %reshape.199 = bf16[32,2,13,2048]{3,2,1,0:T(8,128)(2,1)} reshape(bf16[832,2048]{1,0:T(8,128)(2,1)S(1)} %convolution_convert_fusion) | data formatting | bytes 6815744 | tf_op jit(solution)/shard_map/reshape | solution.py:126
  48.5 5.9 %copy.88 = bf16[32,2,13,2048]{3,1,2,0:T(2,128)(2,1)S(1)} copy(bf16[32,2,13,2048]{3,2,1,0:T(8,128)(2,1)} %reshape.199) | data formatting | bytes 6815744 | tf_op jit(solution)/shard_map/reshape | solution.py:126
  54.4 90.6 %all_to_all.15 = bf16[32,2,13,2048]{3,1,2,0:T(2,128)(2,1)S(1)} all-to-all(bf16[32,2,13,2048]{3,1,2,0:T(2,128)(2,1)S(1)} %copy.88), channel_id=1, replica_groups=mesh['ctx'=8,'exp'=32] {'exp'}, dimensions={0} | all-to-all | bytes 6815744 | tf_op jit(solution)/shard_map/all_to_all | solution.py:127
  145.0 9.1 %fusion = f32[2,1024,32,13]{1,2,3,0:T(8,128)} fusion(bf16[6,2048,1024]{2,1,0:T(8,128)(2,1)} %all-gather.2.cloned.1.call-done, bf16[32,2,13,2048]{3,1,2,0:T(2,128)(2,1)S(1)} %all_to_all.15), kind=kOutput, calls=%fused_computation.2 | convolution fusion | flops 3489660928 | bytes 15204352 | tf_op jit(solution)/shard_map/sjcd,jdf->sjcf/dot_general | solution.py:55
  154.2 13.2 %fusion.12 = bf16[32,2,13,2048]{3,0,2,1:T(8,128)(2,1)} fusion(bf16[6,2048,1024]{2,1,0:T(8,128)(2,1)} %all-gather.2.cloned.1.call-done, f32[2,1024,32,13]{1,2,3,0:T(8,128)} %fusion, bf16[32,2,13,2048]{3,1,2,0:T(2,128)(2,1)S(1)} %all_to_all.15), kind=kOutput, calls=%fused_computation.24 | convolution fusion | flops 6986137600 | bytes 27000832 | tf_op jit(solution)/shard_map/sjcf,jdf->sjcd/dot_general | solution.py:57
  167.3 7.2 %copy.91 = bf16[32,2,13,2048]{3,1,2,0:T(2,128)(2,1)} copy(bf16[32,2,13,2048]{3,0,2,1:T(8,128)(2,1)} %fusion.12) | data formatting | bytes 6815744 | tf_op jit(solution)/shard_map/convert_element_type | solution.py:129
  174.5 9.5 %all-to-all-start.2 = ((bf16[32,2,13,2048]{3,1,2,0:T(2,128)(2,1)}), bf16[32,2,13,2048]{3,1,2,0:T(2,128)(2,1)S(1)}, u32[]{:S(2)}, u32[]{:S(2)}) async-start(bf16[32,2,13,2048]{3,1,2,0:T(2,128)(2,1)} %copy.91), calls=%async_computation.2 | async-start | bytes 6815744 | tf_op jit(solution)/shard_map/all_to_all | solution.py:130
  184.6 77.0 %all-to-all-done.2 = bf16[32,2,13,2048]{3,1,2,0:T(2,128)(2,1)S(1)} async-done(((bf16[32,2,13,2048]{3,1,2,0:T(2,128)(2,1)}), bf16[32,2,13,2048]{3,1,2,0:T(2,128)(2,1)S(1)}, u32[]{:S(2)}, u32[]{:S(2)}) %all-to-all-start.2) | async-done | bytes 3407904 | tf_op jit(solution)/shard_map/all_to_all | solution.py:130
  261.6 3.6 %copy.92 = bf16[32,2,13,2048]{3,2,1,0:T(8,128)(2,1)} copy(bf16[32,2,13,2048]{3,1,2,0:T(2,128)(2,1)S(1)} %all-to-all-done.2) | data formatting | bytes 6815744 | tf_op jit(solution)/shard_map/all_to_all | solution.py:130
  265.3 3.4 %reshape.200 = bf16[832,2048]{1,0:T(8,128)(2,1)S(1)} reshape(bf16[32,2,13,2048]{3,2,1,0:T(8,128)(2,1)} %copy.92) | data formatting | bytes 6815744 | tf_op jit(solution)/shard_map/reshape | solution.py:130
  268.7 4.3 %gather_fusion = bf16[768,2048]{1,0:T(8,128)(2,1)} fusion(bf16[832,2048]{1,0:T(8,128)(2,1)S(1)} %reshape.200, s32[1024]{0:T(1024)S(1)} %pad_clamp_fusion), kind=kCustom, calls=%fused_computation | custom fusion | bytes 6294528 | tf_op jit(solution)/shard_map/jit(_take)/gather | solution.py:133
  273.0 6.3 %gather.11 = bf16[128,6,2048]{2,1,0:T(8,128)(2,1)} reshape(bf16[768,2048]{1,0:T(8,128)(2,1)} %gather_fusion) | data formatting | bytes 6291456 | tf_op jit(solution)/shard_map/jit(_take)/gather | solution.py:133
  279.2 6.1 %multiply_reduce_fusion = f32[128,2048]{1,0:T(8,128)S(1)} fusion(bf16[128,6,2048]{2,1,0:T(8,128)(2,1)} %gather.11, f32[128,6]{1,0:T(8,128)S(1)} %bitcast.139, pred[128,6]{1,0:T(8,128)(4,1)S(1)} %copy.87), kind=kLoop, calls=%fused_computation.7 | loop fusion | flops 6029312 | bytes 4198144 | tf_op jit(solution)/shard_map/reduce_sum | solution.py:134
  285.4 0.9 fusion.33
  (61 shorter events, 4.0 us)
Async XLA Ops:
  6.5 28.0 %copy-start = (bf16[512,1024]{1,0:T(8,128)(2,1)S(1)}, bf16[512,1024]{1,0:T(8,128)(2,1)}, u32[]{:S(2)}) copy-start(bf16[512,1024]{1,0:T(8,128)(2,1)} %param.17) | copy-start | bytes 3145732
  6.5 3.4 %copy-start.8 = (bf16[1,128,576]{1,2,0:T(8,128)(2,1)S(1)}, bf16[1,128,576]{1,2,0:T(8,128)(2,1)}, u32[]{:S(2)}) copy-start(bf16[1,128,576]{1,2,0:T(8,128)(2,1)} %param.15) | copy-start | bytes 442372
  6.5 138.5 %all-gather.2.cloned.1.call-start = ((), (), s32[]{:S(2)}) async-start(), calls=%async_computation.3 | async-start | bytes 28311552 | tf_op jit(solution)/shard_map/all_gather | solution.py:39
  9.9 5.8 %copy-start.10 = (s32[1,128,6]{1,0,2:T(1,128)S(1)}, s32[1,128,6]{1,0,2:T(1,128)}, u32[]{:S(2)}) copy-start(s32[1,128,6]{1,0,2:T(1,128)} %param.21) | copy-start | bytes 9220
  9.9 6.2 %copy-start.7 = (bf16[1,128,1536]{2,1,0:T(8,128)(2,1)S(1)}, bf16[1,128,1536]{2,1,0:T(8,128)(2,1)}, u32[]{:S(2)}) copy-start(bf16[1,128,1536]{2,1,0:T(8,128)(2,1)} %param.14) | copy-start | bytes 1179652
  9.9 9.2 %copy-start.9 = (s32[16]{0:T(128)S(1)}, s32[16]{0:T(128)}, u32[]{:S(2)}) copy-start(s32[16]{0:T(128)} %param.16) | copy-start | bytes 196
  11.2 23.2 %all-to-all-start = ((bf16[8,128,576]{1,2,0:T(8,128)(2,1)}), bf16[8,128,576]{1,2,0:T(8,128)(2,1)S(1)}, u32[]{:S(2)}, u32[]{:S(2)}) async-start(bf16[8,128,576]{1,2,0:T(8,128)(2,1)} %broadcast_in_dim.44), calls=%async_computation | async-start | bytes 2359296 | tf_op jit(solution)/shard_map/all_to_all | solution.py:28
  37.6 1.2 copy-start.13
  40.2 2.3 copy-start.4
  40.2 2.4 copy-start.6
  41.2 3.3 %copy-start.5 = (s32[832,128]{1,0:T(8,128)S(1)}, s32[832,128]{1,0:T(8,128)}, u32[]{:S(2)}) copy-start(s32[832,128]{1,0:T(8,128)} %convert_reduce_fusion) | copy-start | bytes 1277956
  41.2 3.2 %copy-start.11 = (f32[2048]{0:T(1024)S(1)}, f32[2048]{0:T(1024)}, u32[]{:S(2)}) copy-start(f32[2048]{0:T(1024)} %param.20) | copy-start | bytes 24580
  43.4 1.0 copy-start.2
  174.5 9.9 %copy-start.12 = (f32[1,128,6]{1,0,2:T(1,128)S(1)}, f32[1,128,6]{1,0,2:T(1,128)}, u32[]{:S(2)}) copy-start(f32[1,128,6]{1,0,2:T(1,128)} %param.22) | copy-start | bytes 9220
  174.5 87.1 %all-to-all-start.2 = ((bf16[32,2,13,2048]{3,1,2,0:T(2,128)(2,1)}), bf16[32,2,13,2048]{3,1,2,0:T(2,128)(2,1)S(1)}, u32[]{:S(2)}, u32[]{:S(2)}) async-start(bf16[32,2,13,2048]{3,1,2,0:T(2,128)(2,1)} %copy.91), calls=%async_computation.2 | async-start | bytes 6815744 | tf_op jit(solution)/shard_map/all_to_all | solution.py:130
  279.2 6.1 %copy-start.3 = (f32[128,2048]{1,0:T(8,128)S(1)}, f32[128,2048]{1,0:T(8,128)}, u32[]{:S(2)}) copy-start(f32[128,2048]{1,0:T(8,128)} %copy-done.2) | copy-start | bytes 3145732
  279.2 7.1 %copy-start.1 = (bf16[512,1024]{1,0:T(8,128)(2,1)S(1)}, bf16[512,1024]{1,0:T(8,128)(2,1)}, u32[]{:S(2)}) copy-start(bf16[512,1024]{1,0:T(8,128)(2,1)} %param.17) | copy-start | bytes 3145732
Sparse Core Ops, SparseCore 0:
  10.0 133.1 all-gather.1
where the time goes:
time: 297 us; the launch traced here: 293 us
  blocking collectives  90.6 us (31%)
  waiting for transfers between devices  80.2 us (27%)
  local copies, waits for them, and re-layouts  40.6 us (14%)
  matrix products  29.6 us (10%)
  other arithmetic  24.6 us (8%)
  starting transfers between devices  14 us (5%)
  between operations  13.7 us (5%)
    all_to_all x1, blocking collectives, body(): lax.all_to_all(outgoing, 'exp', split_axis=0, concat_axis=0, tiled=True)  90.6 us
    all_to_all x1, waiting for transfers between devices, body(): lax.all_to_all(expert_out, 'exp', split_axis=0, concat_axis=0, tiled=True)  77 us
    dot_general x1, matrix products, expert_block(): jnp.einsum('sjcf,jdf->sjcd', inner, down_slice, preferred_element_type=jn...  13.2 us
    gather x2, local copies, waits for them, and re-layouts, body(): picked = jnp.take(returned, slot_index, axis=0).reshape(block_rows, TOPK, D)  10.5 us
    all_to_all x1, starting transfers between devices, body(): lax.all_to_all(expert_out, 'exp', split_axis=0, concat_axis=0, tiled=True)  9.5 us
    dot_general x1, matrix products, expert_block(): jnp.einsum('sjcd,jdf->sjcf', rows, up_slice, preferred_element_type=jnp.f...  9.14 us
    reshape x2, local copies, waits for them, and re-layouts, body(): outgoing = outgoing.reshape(lax.axis_size('exp'), w_gate.shape[0], CAP, D)  8.86 us
    convert_element_type x1, local copies, waits for them, and re-layouts, body(): expert_block(received, pieces[0], pieces[1], pieces[2]).astype(jnp.bfloat16)  7.19 us
  transfers between devices with their start and end apart: 3, of which 2 were waited for; matrix products, arithmetic and copies ran while one was open for 12% of the time, Pallas kernels for 0%

commit v1 on v0

v1 whole, which is shorter than its diff:
```python
import jax
import jax.numpy as jnp
from jax import lax
from jax.experimental import pallas as pl
from jax.experimental.pallas import tpu as pltpu
from jax.sharding import PartitionSpec as P

D = 2048
HEADS = 8
NOPE = 128
ROPE = 64
VDIM = 128
KVR = 512
EXPERTS = 64
TOPK = 6
CAP = 13
EPSILON = 1e-06

CHUNKS = 4
WIDTH = D // CHUNKS
LOCAL = 2
GROUP = LOCAL * CHUNKS
BLOCK = CAP * GROUP
PACK = 16
FF_BLOCK = 512
MIB = 1 << 20


def whole_vmem():
    return pl.BlockSpec(memory_space=pltpu.VMEM)


def gather_directly(shard, axis):
    length = lax.axis_size(axis)
    return lax.all_to_all(
        jnp.broadcast_to(shard[None], (length, *shard.shape)), axis, 0, 0, tiled=True
    ).reshape(length * shard.shape[0], *shard.shape[1:])


def routing(ids, gates):
    rows = ids.shape[0]
    chosen = ids[:, :, None] == jnp.arange(EXPERTS, dtype=jnp.int32)[None, None, :]
    named = jnp.any(chosen, axis=1)
    gate_of = jnp.sum(jnp.where(chosen, gates[:, :, None], 0.0), axis=1)
    order = jnp.arange(rows, dtype=jnp.int32)
    earlier = (order[None, :] < order[:, None]).astype(jnp.bfloat16)
    before = jnp.dot(earlier, named.astype(jnp.bfloat16), preferred_element_type=jnp.float32)
    rank_of = jnp.where(named, before, -1.0).astype(jnp.bfloat16)
    return rank_of, gate_of


def selectors(ids, gates, peers):
    rank_of, gate_of = routing(ids, gates)
    total = peers * BLOCK
    row = jnp.arange(total, dtype=jnp.int32)
    expert = (row // BLOCK) * LOCAL + (row // CHUNKS) % LOCAL
    rank = ((row % BLOCK) // GROUP).astype(jnp.float32)
    onehot = (expert[:, None] == jnp.arange(EXPERTS, dtype=jnp.int32)[None, :]).astype(jnp.bfloat16)
    at_rows = lax.dot_general(
        onehot, rank_of, (((1,), (1,)), ((), ())), preferred_element_type=jnp.float32
    )
    send = (at_rows == rank[:, None]).astype(jnp.bfloat16)
    at_cols = lax.dot_general(
        rank_of, onehot, (((1,), (1,)), ((), ())), preferred_element_type=jnp.float32
    )
    gate_cols = lax.dot_general(
        gate_of.astype(jnp.bfloat16),
        onehot,
        (((1,), (1,)), ((), ())),
        preferred_element_type=jnp.float32,
    )
    combine = jnp.where(at_cols == rank[None, :], gate_cols, 0.0).astype(jnp.bfloat16)
    return send, combine


def send_kernel(select_ref, rows_ref, out_ref):
    select = select_ref[...]
    which = lax.broadcasted_iota(jnp.int32, select.shape, 0) % CHUNKS
    parts = [jnp.where(which == j, select, jnp.zeros_like(select)) for j in range(CHUNKS)]
    left = jnp.concatenate(parts, axis=1)
    right = jnp.concatenate(
        [rows_ref[:, j * WIDTH : (j + 1) * WIDTH] for j in range(CHUNKS)], axis=0
    )
    out_ref[...] = jnp.dot(left, right, preferred_element_type=jnp.float32).astype(jnp.bfloat16)


def send_rows(select, rows):
    total, tokens = select.shape
    step = total // 8
    return pl.pallas_call(
        send_kernel,
        out_shape=jax.ShapeDtypeStruct((total, WIDTH), jnp.bfloat16),
        grid=(8,),
        in_specs=[
            pl.BlockSpec((step, tokens), lambda i: (i, 0)),
            pl.BlockSpec((tokens, D), lambda i: (0, 0)),
        ],
        out_specs=pl.BlockSpec((step, WIDTH), lambda i: (i, 0)),
        compiler_params=pltpu.CompilerParams(vmem_limit_bytes=24 * MIB),
        name="send_rows",
    )(select, rows)


def pack_matrix(transposed):
    side = PACK * GROUP
    a = lax.broadcasted_iota(jnp.int32, (side, side), 1 if transposed else 0)
    b = lax.broadcasted_iota(jnp.int32, (side, side), 0 if transposed else 1)
    return (b == (a % PACK) * GROUP + a // PACK).astype(jnp.float32).astype(jnp.bfloat16)


def expert_kernel(recv_ref, gate_ref, up_ref, down_ref, out_ref, x_ref, acc_ref, y_ref):
    expert, part = pl.program_id(0), pl.program_id(1)
    parts = pl.num_programs(1)
    side = PACK * GROUP
    blocks = recv_ref.shape[0] // side

    @pl.when((expert == 0) & (part == 0))
    def _():
        unpack = pack_matrix(False)
        for b in range(blocks):
            got = jnp.dot(
                unpack,
                recv_ref[b * side : (b + 1) * side, :],
                preferred_element_type=jnp.float32,
            ).astype(jnp.bfloat16)
            for k in range(LOCAL):
                for j in range(CHUNKS):
                    at = (k * CHUNKS + j) * PACK
                    x_ref[k, b * PACK : (b + 1) * PACK, j * WIDTH : (j + 1) * WIDTH] = got[
                        at : at + PACK, :
                    ]

    x = x_ref[expert]
    gate = jnp.dot(x, gate_ref[0], preferred_element_type=jnp.float32)
    up = jnp.dot(x, up_ref[0], preferred_element_type=jnp.float32)
    inner = (gate / (1.0 + jnp.exp(-gate)) * up).astype(jnp.bfloat16)
    out = lax.dot_general(
        inner, down_ref[0], (((1,), (1,)), ((), ())), preferred_element_type=jnp.float32
    )

    @pl.when(part == 0)
    def _():
        acc_ref[...] = out

    @pl.when((part > 0) & (part < parts - 1))
    def _():
        acc_ref[...] += out

    @pl.when(part == parts - 1)
    def _():
        y_ref[expert] = (acc_ref[...] + out).astype(jnp.bfloat16)

    @pl.when((expert == LOCAL - 1) & (part == parts - 1))
    def _():
        pack = pack_matrix(True)
        for b in range(blocks):
            pieces = [
                y_ref[k, b * PACK : (b + 1) * PACK, j * WIDTH : (j + 1) * WIDTH]
                for k in range(LOCAL)
                for j in range(CHUNKS)
            ]
            out_ref[b * side : (b + 1) * side, :] = jnp.dot(
                pack, jnp.concatenate(pieces, axis=0), preferred_element_type=jnp.float32
            ).astype(jnp.bfloat16)


def run_experts(received, weights):
    total = received.shape[0]
    items = total // GROUP
    hidden_units = weights.shape[2]
    return pl.pallas_call(
        expert_kernel,
        out_shape=jax.ShapeDtypeStruct(received.shape, jnp.bfloat16),
        grid=(LOCAL, hidden_units // FF_BLOCK),
        in_specs=[
            pl.BlockSpec((total, WIDTH), lambda k, f: (0, 0), pipeline_mode=pl.Buffered(1)),
            pl.BlockSpec((1, D, FF_BLOCK), lambda k, f: (k, 0, f)),
            pl.BlockSpec((1, D, FF_BLOCK), lambda k, f: (LOCAL + k, 0, f)),
            pl.BlockSpec((1, D, FF_BLOCK), lambda k, f: (2 * LOCAL + k, 0, f)),
        ],
        out_specs=pl.BlockSpec((total, WIDTH), lambda k, f: (0, 0), pipeline_mode=pl.Buffered(1)),
        scratch_shapes=[
            pltpu.VMEM((LOCAL, items, D), jnp.bfloat16),
            pltpu.VMEM((items, D), jnp.float32),
            pltpu.VMEM((LOCAL, items, D), jnp.bfloat16),
        ],
        compiler_params=pltpu.CompilerParams(vmem_limit_bytes=52 * MIB),
        name="run_experts",
    )(received, weights, weights, weights)


def combine_kernel(combine_ref, rows_ref, residual_ref, out_ref):
    combine = combine_ref[...]
    which = lax.broadcasted_iota(jnp.int32, combine.shape, 1) % CHUNKS
    left = jnp.concatenate(
        [jnp.where(which == j, combine, jnp.zeros_like(combine)) for j in range(CHUNKS)], axis=0
    )
    got = jnp.dot(left, rows_ref[...], preferred_element_type=jnp.float32)
    tokens = combine.shape[0]
    for j in range(CHUNKS):
        cols = slice(j * WIDTH, (j + 1) * WIDTH)
        out_ref[:, cols] = (
            residual_ref[:, cols].astype(jnp.float32) + got[j * tokens : (j + 1) * tokens, :]
        ).astype(jnp.bfloat16)


def combine_rows(combine, rows, residual):
    return pl.pallas_call(
        combine_kernel,
        out_shape=jax.ShapeDtypeStruct(residual.shape, jnp.bfloat16),
        in_specs=[whole_vmem(), whole_vmem(), whole_vmem()],
        out_specs=whole_vmem(),
        compiler_params=pltpu.CompilerParams(vmem_limit_bytes=32 * MIB),
        name="combine_rows",
    )(combine, rows, residual)


def body(
    hidden,
    queries,
    latent,
    group_order,
    w_uk,
    w_uv,
    w_out,
    norm_gain,
    expert_ids,
    gate_weights,
    w_gate,
    w_up,
    w_down,
):
    peers = lax.axis_size("exp")
    block_rows = hidden.shape[1]
    half_rows = block_rows // 2
    seq_rows = block_rows * lax.axis_size("ctx")
    whole = gather_directly(latent[0], "ctx")
    weights = lax.all_gather(
        jnp.concatenate([w_gate, w_up, w_down], axis=0), "ctx", axis=2, tiled=True
    )
    row_index = jnp.arange(seq_rows, dtype=jnp.int32)
    positions = group_order[row_index // half_rows] * half_rows + row_index % half_rows
    own_positions = lax.dynamic_slice_in_dim(
        positions, lax.axis_index("ctx") * block_rows, block_rows
    )
    send, combine = selectors(expert_ids[0], gate_weights[0], peers)

    content = whole[:, :KVR]
    key_rope = whole[:, KVR:]
    key_nope = jnp.dot(content, w_uk, preferred_element_type=jnp.float32).astype(jnp.bfloat16)
    values = jnp.dot(content, w_uv, preferred_element_type=jnp.float32).astype(jnp.bfloat16)
    query_full = queries[0].reshape(block_rows, HEADS, NOPE + ROPE)
    scores = jnp.einsum(
        "qhd,khd->hqk",
        query_full[:, :, :NOPE],
        key_nope.reshape(seq_rows, HEADS, NOPE),
        preferred_element_type=jnp.float32,
    )
    scores = scores + jnp.einsum(
        "qhr,kr->hqk", query_full[:, :, NOPE:], key_rope, preferred_element_type=jnp.float32
    )
    scores = scores * (NOPE + ROPE) ** (-0.5)
    visible = positions[None, :] <= own_positions[:, None]
    scores = jnp.where(visible[None], scores, -jnp.inf)
    peak = jnp.max(scores, axis=2, keepdims=True)
    expo = jnp.exp(scores - peak)
    totals = jnp.sum(expo, axis=2)
    heads_out = jnp.einsum(
        "hqk,khv->qhv",
        expo.astype(jnp.bfloat16),
        values.reshape(seq_rows, HEADS, VDIM),
        preferred_element_type=jnp.float32,
    )
    heads_out = heads_out / jnp.transpose(totals)[:, :, None]
    attended = heads_out.astype(jnp.bfloat16).reshape(block_rows, HEADS * VDIM)
    residual = (
        hidden[0].astype(jnp.float32) + jnp.dot(attended, w_out, preferred_element_type=jnp.float32)
    ).astype(jnp.bfloat16)
    stream = residual.astype(jnp.float32)
    factor = lax.rsqrt(jnp.mean(stream * stream, axis=1, keepdims=True) + EPSILON)
    normed = (stream * factor * norm_gain).astype(jnp.bfloat16)

    outgoing = send_rows(send, normed).reshape(peers, BLOCK, WIDTH)
    received = lax.all_to_all(outgoing, "exp", split_axis=0, concat_axis=0, tiled=True)
    done = run_experts(received.reshape(peers * BLOCK, WIDTH), weights)
    returned = lax.all_to_all(
        done.reshape(peers, BLOCK, WIDTH), "exp", split_axis=0, concat_axis=0, tiled=True
    )
    return combine_rows(combine, returned.reshape(peers * BLOCK, WIDTH), residual)[None]


def solution(mesh):
    return jax.shard_map(
        body,
        mesh=mesh,
        in_specs=(
            P("exp", "ctx", None),
            P("exp", "ctx", None),
            P("exp", "ctx", None),
            P(),
            P(),
            P(),
            P(),
            P(),
            P("exp", "ctx", None),
            P("exp", "ctx", None),
            P("exp", None, "ctx"),
            P("exp", None, "ctx"),
            P("exp", None, "ctx"),
        ),
        out_specs=P("exp", "ctx", None),
        check_vma=False,
    )
```

time: 297 us -> 273 us (0.919)
  local copies, waits for them, and re-layouts: 40.6 us -> 12.3 us
  Pallas kernels: 0 us -> 26.9 us
  matrix products: 29.6 us -> 13.7 us
  other arithmetic: 24.6 us -> 15.4 us
    pallas_call x0 -> x3, Pallas kernels: none -> 26.9 us  [the longest x1 20.9 us: run_experts(): pl.pallas_call(expert_kernel, out_shape=jax.ShapeDtypeStruct(received.sha...]
    dot_general x3 -> x4, matrix products: 23.4 us -> 7.51 us  [the longest x1 2.82 us: selectors(): lax.dot_general(onehot, rank_of, (((1,), (1,)), ((), ())), preferred_elem...]
    reshape x4 -> x1, local copies, waits for them, and re-layouts: 12.5 us -> 0.17 us  [gather_directly(): lax.all_to_all(jnp.broadcast_to(shard[None], (length, *shard.shape)), axi...]
    gather x2 -> x0, local copies, waits for them, and re-layouts: 10.5 us -> none  [body(): picked = jnp.take(returned, slot_index, axis=0).reshape(block_rows, TOPK, D)]
    reduce_sum x3 -> x1, other arithmetic: 7.33 us -> 0.03 us  [routing(): gate_of = jnp.sum(jnp.where(chosen, gates[:, :, None], 0.0), axis=1)]
    convert_element_type x1 -> x0, local copies, waits for them, and re-layouts: 7.19 us -> none  [body(): expert_block(received, pieces[0], pieces[1], pieces[2]).astype(jnp.bfloat16)]
    unnamed x30 -> x37, local copies, waits for them, and re-layouts: 3.44 us -> 10.1 us
    all_gather x1, waiting for transfers between devices: 0.01 us -> 3.85 us  [body(): lax.all_gather(jnp.concatenate([w_gate, w_up, w_down], axis=0), 'ctx', ax...]
  transfers between devices with their start and end apart: 3 -> 3, of which waited for: 2 -> 3; matrix products, arithmetic and copies ran while one was open for 12% -> 10% of each run, Pallas kernels for 0% -> 1%
where the time goes in v1:
time: 273 us; the launch traced here: 269 us
  blocking collectives  90.7 us (33%)
  waiting for transfers between devices  80.5 us (29%)
  Pallas kernels  26.9 us (10%)
  starting transfers between devices  15.8 us (6%)
  other arithmetic  15.4 us (6%)
  matrix products  13.7 us (5%)
  between operations  13.7 us (5%)
  local copies, waits for them, and re-layouts  12.3 us (5%)
    all_to_all x1, blocking collectives, body(): lax.all_to_all(outgoing, 'exp', split_axis=0, concat_axis=0, tiled=True)  90.7 us
    all_to_all x1, waiting for transfers between devices, body(): lax.all_to_all(done.reshape(peers, BLOCK, WIDTH), 'exp', split_axis=0, co...  72.3 us
    pallas_call x1, Pallas kernels, run_experts(): pl.pallas_call(expert_kernel, out_shape=jax.ShapeDtypeStruct(received.sha...  20.9 us
    all_to_all x1, starting transfers between devices, body(): lax.all_to_all(done.reshape(peers, BLOCK, WIDTH), 'exp', split_axis=0, co...  11.3 us
    unnamed x37, local copies, waits for them, and re-layouts  10.1 us
    add x1, other arithmetic, body(): group_order[row_index // half_rows] * half_rows + row_index % half_rows  5.71 us
  transfers between devices with their start and end apart: 3, of which 3 were waited for; matrix products, arithmetic and copies ran while one was open for 10% of the time, Pallas kernels for 1%

profile of v1, /device:TPU:32, one launch (start us, length us, event | category | flops | bytes accessed | tf_op | source)
XLA Modules:
  0.0 268.8 jit_solution(3324250912426601630)
XLA Ops:
  6.5 3.3 %pad_maximum_fusion = bf16[6,2048,128]{2,1,0:T(8,128)(2,1)} fusion(bf16[2,2048,128]{2,1,0:T(8,128)(2,1)} %param.25, bf16[2,2048,128]{2,1,0:T(8,128)(2,1)} %param.24, bf16[2,2048,128]{2,1,0:T(8,128)(2,1)} %param.23), kind=kLoop, calls=%fused_computation.11 | loop fusion | flops 3145728 | bytes 6291456 | tf_op jit(solution)/shard_map/concatenate | solution.py:239
  9.9 0.9 copy-done.11
  10.8 1.3 broadcast_in_dim.65
  12.1 4.5 %all-to-all-start = ((bf16[8,128,576]{1,2,0:T(8,128)(2,1)}), bf16[8,128,576]{1,2,0:T(8,128)(2,1)S(1)}, u32[]{:S(2)}, u32[]{:S(2)}) async-start(bf16[8,128,576]{1,2,0:T(8,128)(2,1)} %broadcast_in_dim.65), calls=%async_computation | async-start | bytes 2359296 | tf_op jit(solution)/shard_map/all_to_all | solution.py:35
  16.8 0.7 fusion.55
  17.6 4.3 %compare_select_fusion.1 = s32[1024,1]{0,1:T(1,128)S(1)} fusion(s32[]{:T(128)} %bitcast.12, s32[]{:T(128)} %bitcast.13, s32[]{:T(128)} %bitcast.14, s32[]{:T(128)} %bitcast.15, s32[]{:T(128)} %bitcast.16, s32[]{:T(128)} %bitcast.18, s32[]{:T(128)} %bitcast.17), kind=kLoop, calls=%fused_computation.87 | loop fusion | flops 23552 | bytes 4124 | tf_op jit(solution)/shard_map/gather | solution.py:242
  21.9 5.7 %fusion.51 = s32[1024]{0:T(1024)S(1)} fusion(pred[1024]{0:T(1024)(128)(4,1)S(1)} %compare_reduce_fusion, pred[1024]{0:T(1024)(128)(4,1)S(1)} %compare_reduce_fusion.1, pred[1024]{0:T(1024)(128)(4,1)S(1)} %compare_reduce_fusion.2, pred[1024]{0:T(1024)(128)(4,1)S(1)} %compare_reduce_fusion.3, pred[1024]{0:T(1024)(128)(4,1)S(1)} %compare_reduce_fusion.4, ...), kind=kLoop, calls=%fused_computation.98 | loop fusion | flops 17408 | bytes 17444 | tf_op jit(solution)/shard_map/add | solution.py:242
  28.2 0.9 broadcast_compare_fusion
  29.0 2.8 %fusion.1.select_ref = bf16[3328,128]{1,0:T(8,128)(2,1)S(1)} fusion(bf16[128,64]{0,1:T(8,128)(2,1)S(1)} %fusion.19, f32[3328]{0:T(1024)S(1)} %get-tuple-element.26, s32[3328]{0:T(1024)S(1)} %get-tuple-element.25), kind=kOutput, calls=%fused_computation.4 | convolution fusion | flops 55590912 | bytes 894976 | tf_op jit(solution)/shard_map/dot_general | solution.py:59
  31.9 4.3 %all-to-all-done = bf16[8,128,576]{1,2,0:T(8,128)(2,1)S(1)} async-done(((bf16[8,128,576]{1,2,0:T(8,128)(2,1)}), bf16[8,128,576]{1,2,0:T(8,128)(2,1)S(1)}, u32[]{:S(2)}, u32[]{:S(2)}) %all-to-all-start) | async-done | bytes 1179680 | tf_op jit(solution)/shard_map/all_to_all | solution.py:35
  36.3 1.3 convolution_convert_fusion
  37.7 0.8 fusion.28
  38.6 0.9 fusion.56
  40.1 0.7 copy-done.16
  40.7 1.3 convolution_convert_fusion.1
  42.1 0.9 fusion.16
  43.0 1.3 copy-done.7
  44.5 0.8 fusion.20
  45.5 0.8 copy-done.4
  46.3 3.2 %send_rows.1 = bf16[3328,512]{1,0:T(8,128)(2,1)S(1)} custom-call(bf16[3328,128]{1,0:T(8,128)(2,1)S(1)} %fusion.1.select_ref, bf16[128,2048]{1,0:T(8,128)(2,1)S(1)} %fusion.22.rows_ref), custom_call_target="tpu_custom_call" | custom-call | tf_op jit(solution)/shard_map/send_rows/pallas_call | solution.py:90
  49.5 90.7 %all_to_all.15 = bf16[32,104,512]{2,1,0:T(8,128)(2,1)} all-to-all(bf16[32,104,512]{2,1,0:T(8,128)(2,1)S(1)} %bitcast.71), channel_id=1, replica_groups=mesh['ctx'=8,'exp'=32] {'exp'}, dimensions={0} | all-to-all | bytes 6815744 | tf_op jit(solution)/shard_map/all_to_all | solution.py:284
  140.2 3.8 %all-gather.2.cloned.1.call-done.gate_ref.up_ref.down_ref = bf16[6,2048,1024]{2,1,0:T(8,128)(2,1)} async-done(((bf16[6,2048,128]{2,1,0:T(8,128)(2,1)}), bf16[6,2048,1024]{2,1,0:T(8,128)(2,1)}) %all-gather.2.cloned.1.call-update) | async-done | bytes 25165840 | tf_op jit(solution)/shard_map/all_gather | solution.py:238
  144.1 20.9 %run_experts.1 = bf16[3328,512]{1,0:T(8,128)(2,1)} custom-call(bf16[3328,512]{1,0:T(8,128)(2,1)} %bitcast.74, bf16[6,2048,1024]{2,1,0:T(8,128)(2,1)} %all-gather.2.cloned.1.call-done.gate_ref.up_ref.down_ref, bf16[6,2048,1024]{2,1,0:T(8,128)(2,1)} %all-gather.2.cloned.1.call-done.gate_ref.up_ref.down_ref, ...), custom_call_target="tpu_custom_call" | custom-call | tf_op jit(solution)/shard_map/run_experts/pallas_call | solution.py:171
  165.0 11.3 %all-to-all-start.2 = ((bf16[32,104,512]{2,1,0:T(8,128)(2,1)}), bf16[32,104,512]{2,1,0:T(8,128)(2,1)S(1)}, u32[]{:S(2)}, u32[]{:S(2)}) async-start(bf16[32,104,512]{2,1,0:T(8,128)(2,1)} %bitcast.73), calls=%async_computation.2 | async-start | bytes 6815744 | tf_op jit(solution)/shard_map/all_to_all | solution.py:286
  176.4 1.9 convolution_compare_fusion.1
  178.3 2.6 fusion.combine_ref
  181.0 72.3 %all-to-all-done.2 = bf16[32,104,512]{2,1,0:T(8,128)(2,1)S(1)} async-done(((bf16[32,104,512]{2,1,0:T(8,128)(2,1)}), bf16[32,104,512]{2,1,0:T(8,128)(2,1)S(1)}, u32[]{:S(2)}, u32[]{:S(2)}) %all-to-all-start.2) | async-done | bytes 3407904 | tf_op jit(solution)/shard_map/all_to_all | solution.py:286
  253.3 1.7 copy-done.2
  255.0 2.1 copy-done.3
  257.1 1.0 copy-done.5
  258.1 1.2 copy-done.6
  259.3 2.7 %combine_rows.1 = bf16[128,2048]{1,0:T(8,128)(2,1)} custom-call(bf16[128,3328]{1,0:T(8,128)(2,1)S(1)} %copy-done.6, bf16[3328,512]{1,0:T(8,128)(2,1)S(1)} %bitcast.72, bf16[128,2048]{1,0:T(8,128)(2,1)S(1)} %copy-done.5), custom_call_target="tpu_custom_call" | custom-call | tf_op jit(solution)/shard_map/combine_rows/pallas_call | solution.py:208
  (49 shorter events, 2.1 us)
Async XLA Ops:
  6.5 29.8 %copy-start = (bf16[512,1024]{1,0:T(8,128)(2,1)S(1)}, bf16[512,1024]{1,0:T(8,128)(2,1)}, u32[]{:S(2)}) copy-start(bf16[512,1024]{1,0:T(8,128)(2,1)} %param.17) | copy-start | bytes 3145732
  6.5 137.5 %all-gather.2.cloned.1.call-start = ((), (), s32[]{:S(2)}) async-start(), calls=%async_computation.3 | async-start | bytes 28311552 | tf_op jit(solution)/shard_map/all_gather | solution.py:238
  9.9 0.9 copy-start.11
  9.9 6.9 %copy-start.12 = (s32[16]{0:T(128)S(1)}, s32[16]{0:T(128)}, u32[]{:S(2)}) copy-start(s32[16]{0:T(128)} %param.16) | copy-start | bytes 196
  9.9 17.7 %copy-start.10 = (bf16[1,128,1536]{2,1,0:T(8,128)(2,1)S(1)}, bf16[1,128,1536]{2,1,0:T(8,128)(2,1)}, u32[]{:S(2)}) copy-start(bf16[1,128,1536]{2,1,0:T(8,128)(2,1)} %param.14) | copy-start | bytes 1179652
  10.8 17.1 %copy-start.14 = (s32[1,128,6]{1,0,2:T(1,128)S(1)}, s32[1,128,6]{1,0,2:T(1,128)}, u32[]{:S(2)}) copy-start(s32[1,128,6]{1,0,2:T(1,128)} %param.21) | copy-start | bytes 9220
  12.1 24.1 %all-to-all-start = ((bf16[8,128,576]{1,2,0:T(8,128)(2,1)}), bf16[8,128,576]{1,2,0:T(8,128)(2,1)S(1)}, u32[]{:S(2)}, u32[]{:S(2)}) async-start(bf16[8,128,576]{1,2,0:T(8,128)(2,1)} %broadcast_in_dim.65), calls=%async_computation | async-start | bytes 2359296 | tf_op jit(solution)/shard_map/all_to_all | solution.py:35
  37.6 0.9 copy-start.8
  39.5 1.2 copy-start.16
  42.1 2.3 copy-start.7
  42.1 2.4 copy-start.9
  44.5 0.9 copy-start.13
  45.5 0.8 copy-start.4
  165.0 11.3 %copy-start.15 = (f32[1,128,6]{1,0,2:T(1,128)S(1)}, f32[1,128,6]{1,0,2:T(1,128)}, u32[]{:S(2)}) copy-start(f32[1,128,6]{1,0,2:T(1,128)} %param.22) | copy-start | bytes 9220
  165.0 88.3 %all-to-all-start.2 = ((bf16[32,104,512]{2,1,0:T(8,128)(2,1)}), bf16[32,104,512]{2,1,0:T(8,128)(2,1)S(1)}, u32[]{:S(2)}, u32[]{:S(2)}) async-start(bf16[32,104,512]{2,1,0:T(8,128)(2,1)} %bitcast.73), calls=%async_computation.2 | async-start | bytes 6815744 | tf_op jit(solution)/shard_map/all_to_all | solution.py:286
  253.3 1.7 copy-start.2
  255.0 7.0 %copy-start.1 = (bf16[512,1024]{1,0:T(8,128)(2,1)S(1)}, bf16[512,1024]{1,0:T(8,128)(2,1)}, u32[]{:S(2)}) copy-start(bf16[512,1024]{1,0:T(8,128)(2,1)} %param.17) | copy-start | bytes 3145732
  255.0 2.1 copy-start.3
  257.1 1.0 copy-start.5
  258.1 1.2 copy-start.6
Sparse Core Ops, SparseCore 0:
  10.0 133.9 all-gather.1

commit v2 on v1

--- a/solution.py
+++ b/solution.py
@@ -16,13 +16,12 @@
 CAP = 13
 EPSILON = 1e-06
 
-CHUNKS = 4
+CHUNKS = 8
 WIDTH = D // CHUNKS
 LOCAL = 2
-GROUP = LOCAL * CHUNKS
-BLOCK = CAP * GROUP
+BLOCK = CAP * CHUNKS
 PACK = 16
-FF_BLOCK = 512
+FF_BLOCK = 256
 MIB = 1 << 20
 
 
@@ -35,6 +34,12 @@
     return lax.all_to_all(
         jnp.broadcast_to(shard[None], (length, *shard.shape)), axis, 0, 0, tiled=True
     ).reshape(length * shard.shape[0], *shard.shape[1:])
+
+
+def exchanged(rows, peers):
+    return lax.all_to_all(
+        rows.reshape(peers, BLOCK, WIDTH), "exp", split_axis=0, concat_axis=0, tiled=True
+    ).reshape(peers * BLOCK, WIDTH)
 
 
 def routing(ids, gates):
@@ -49,12 +54,11 @@
     return rank_of, gate_of
 
 
-def selectors(ids, gates, peers):
-    rank_of, gate_of = routing(ids, gates)
+def selectors(rank_of, gate_of, local, peers):
     total = peers * BLOCK
     row = jnp.arange(total, dtype=jnp.int32)
-    expert = (row // BLOCK) * LOCAL + (row // CHUNKS) % LOCAL
-    rank = ((row % BLOCK) // GROUP).astype(jnp.float32)
+    expert = (row // BLOCK) * LOCAL + local
+    rank = ((row % BLOCK) // CHUNKS).astype(jnp.float32)
     onehot = (expert[:, None] == jnp.arange(EXPERTS, dtype=jnp.int32)[None, :]).astype(jnp.bfloat16)
     at_rows = lax.dot_general(
         onehot, rank_of, (((1,), (1,)), ((), ())), preferred_element_type=jnp.float32
@@ -102,19 +106,19 @@
 
 
 def pack_matrix(transposed):
-    side = PACK * GROUP
+    side = PACK * CHUNKS
     a = lax.broadcasted_iota(jnp.int32, (side, side), 1 if transposed else 0)
     b = lax.broadcasted_iota(jnp.int32, (side, side), 0 if transposed else 1)
-    return (b == (a % PACK) * GROUP + a // PACK).astype(jnp.float32).astype(jnp.bfloat16)
-
-
-def expert_kernel(recv_ref, gate_ref, up_ref, down_ref, out_ref, x_ref, acc_ref, y_ref):
-    expert, part = pl.program_id(0), pl.program_id(1)
-    parts = pl.num_programs(1)
-    side = PACK * GROUP
+    return (b == (a % PACK) * CHUNKS + a // PACK).astype(jnp.float32).astype(jnp.bfloat16)
+
+
+def expert_kernel(recv_ref, gate_ref, up_ref, down_ref, out_ref, x_ref, acc_ref):
+    part = pl.program_id(0)
+    parts = pl.num_programs(0)
+    side = PACK * CHUNKS
     blocks = recv_ref.shape[0] // side
 
-    @pl.when((expert == 0) & (part == 0))
+    @pl.when(part == 0)
     def _():
         unpack = pack_matrix(False)
         for b in range(blocks):
@@ -123,14 +127,12 @@
                 recv_ref[b * side : (b + 1) * side, :],
                 preferred_element_type=jnp.float32,
             ).astype(jnp.bfloat16)
-            for k in range(LOCAL):
-                for j in range(CHUNKS):
-                    at = (k * CHUNKS + j) * PACK
-                    x_ref[k, b * PACK : (b + 1) * PACK, j * WIDTH : (j + 1) * WIDTH] = got[
-                        at : at + PACK, :
-                    ]
-
-    x = x_ref[expert]
+            for j in range(CHUNKS):
+                x_ref[b * PACK : (b + 1) * PACK, j * WIDTH : (j + 1) * WIDTH] = got[
+                    j * PACK : (j + 1) * PACK, :
+                ]
+
+    x = x_ref[...]
     gate = jnp.dot(x, gate_ref[0], preferred_element_type=jnp.float32)
     up = jnp.dot(x, up_ref[0], preferred_element_type=jnp.float32)
     inner = (gate / (1.0 + jnp.exp(-gate)) * up).astype(jnp.bfloat16)
@@ -148,15 +150,11 @@
 
     @pl.when(part == parts - 1)
     def _():
-        y_ref[expert] = (acc_ref[...] + out).astype(jnp.bfloat16)
-
-    @pl.when((expert == LOCAL - 1) & (part == parts - 1))
-    def _():
+        x_ref[...] = (acc_ref[...] + out).astype(jnp.bfloat16)
         pack = pack_matrix(True)
         for b in range(blocks):
             pieces = [
-                y_ref[k, b * PACK : (b + 1) * PACK, j * WIDTH : (j + 1) * WIDTH]
-                for k in range(LOCAL)
+                x_ref[b * PACK : (b + 1) * PACK, j * WIDTH : (j + 1) * WIDTH]
                 for j in range(CHUNKS)
             ]
             out_ref[b * side : (b + 1) * side, :] = jnp.dot(
@@ -164,28 +162,27 @@
             ).astype(jnp.bfloat16)
 
 
-def run_experts(received, weights):
+def run_expert(received, weights):
     total = received.shape[0]
-    items = total // GROUP
+    items = total // CHUNKS
     hidden_units = weights.shape[2]
     return pl.pallas_call(
         expert_kernel,
         out_shape=jax.ShapeDtypeStruct(received.shape, jnp.bfloat16),
-        grid=(LOCAL, hidden_units // FF_BLOCK),
+        grid=(hidden_units // FF_BLOCK,),
         in_specs=[
-            pl.BlockSpec((total, WIDTH), lambda k, f: (0, 0), pipeline_mode=pl.Buffered(1)),
-            pl.BlockSpec((1, D, FF_BLOCK), lambda k, f: (k, 0, f)),
-            pl.BlockSpec((1, D, FF_BLOCK), lambda k, f: (LOCAL + k, 0, f)),
-            pl.BlockSpec((1, D, FF_BLOCK), lambda k, f: (2 * LOCAL + k, 0, f)),
+            pl.BlockSpec((total, WIDTH), lambda f: (0, 0), pipeline_mode=pl.Buffered(1)),
+            pl.BlockSpec((1, D, FF_BLOCK), lambda f: (0, 0, f)),
+            pl.BlockSpec((1, D, FF_BLOCK), lambda f: (1, 0, f)),
+            pl.BlockSpec((1, D, FF_BLOCK), lambda f: (2, 0, f)),
         ],
-        out_specs=pl.BlockSpec((total, WIDTH), lambda k, f: (0, 0), pipeline_mode=pl.Buffered(1)),
+        out_specs=pl.BlockSpec((total, WIDTH), lambda f: (0, 0), pipeline_mode=pl.Buffered(1)),
         scratch_shapes=[
-            pltpu.VMEM((LOCAL, items, D), jnp.bfloat16),
+            pltpu.VMEM((items, D), jnp.bfloat16),
             pltpu.VMEM((items, D), jnp.float32),
-            pltpu.VMEM((LOCAL, items, D), jnp.bfloat16),
         ],
-        compiler_params=pltpu.CompilerParams(vmem_limit_bytes=52 * MIB),
-        name="run_experts",
+        compiler_params=pltpu.CompilerParams(vmem_limit_bytes=36 * MIB),
+        name="run_expert",
     )(received, weights, weights, weights)
 
 
@@ -201,13 +198,13 @@
         cols = slice(j * WIDTH, (j + 1) * WIDTH)
         out_ref[:, cols] = (
             residual_ref[:, cols].astype(jnp.float32) + got[j * tokens : (j + 1) * tokens, :]
-        ).astype(jnp.bfloat16)
-
-
-def combine_rows(combine, rows, residual):
+        ).astype(out_ref.dtype)
+
+
+def combine_rows(combine, rows, residual, dtype):
     return pl.pallas_call(
         combine_kernel,
-        out_shape=jax.ShapeDtypeStruct(residual.shape, jnp.bfloat16),
+        out_shape=jax.ShapeDtypeStruct(residual.shape, dtype),
         in_specs=[whole_vmem(), whole_vmem(), whole_vmem()],
         out_specs=whole_vmem(),
         compiler_params=pltpu.CompilerParams(vmem_limit_bytes=32 * MIB),
@@ -235,15 +232,19 @@
     half_rows = block_rows // 2
     seq_rows = block_rows * lax.axis_size("ctx")
     whole = gather_directly(latent[0], "ctx")
-    weights = lax.all_gather(
-        jnp.concatenate([w_gate, w_up, w_down], axis=0), "ctx", axis=2, tiled=True
-    )
+    weights = [
+        lax.all_gather(
+            jnp.stack([w_gate[k], w_up[k], w_down[k]]), "ctx", axis=2, tiled=True
+        )
+        for k in range(LOCAL)
+    ]
     row_index = jnp.arange(seq_rows, dtype=jnp.int32)
     positions = group_order[row_index // half_rows] * half_rows + row_index % half_rows
     own_positions = lax.dynamic_slice_in_dim(
         positions, lax.axis_index("ctx") * block_rows, block_rows
     )
-    send, combine = selectors(expert_ids[0], gate_weights[0], peers)
+    rank_of, gate_of = routing(expert_ids[0], gate_weights[0])
+    plans = [selectors(rank_of, gate_of, k, peers) for k in range(LOCAL)]
 
     content = whole[:, :KVR]
     key_rope = whole[:, KVR:]
@@ -280,13 +281,18 @@
     factor = lax.rsqrt(jnp.mean(stream * stream, axis=1, keepdims=True) + EPSILON)
     normed = (stream * factor * norm_gain).astype(jnp.bfloat16)
 
-    outgoing = send_rows(send, normed).reshape(peers, BLOCK, WIDTH)
-    received = lax.all_to_all(outgoing, "exp", split_axis=0, concat_axis=0, tiled=True)
-    done = run_experts(received.reshape(peers * BLOCK, WIDTH), weights)
-    returned = lax.all_to_all(
-        done.reshape(peers, BLOCK, WIDTH), "exp", split_axis=0, concat_axis=0, tiled=True
-    )
-    return combine_rows(combine, returned.reshape(peers * BLOCK, WIDTH), residual)[None]
+    received = []
+    for k in range(LOCAL):
+        outgoing = send_rows(plans[k][0], normed)
+        if received:
+            outgoing, _ = lax.optimization_barrier((outgoing, received[-1]))
+        received.append(exchanged(outgoing, peers))
+    mixed = residual
+    returned = [exchanged(run_expert(received[k], weights[k]), peers) for k in range(LOCAL)]
+    for k in range(LOCAL):
+        last = k == LOCAL - 1
+        mixed = combine_rows(plans[k][1], returned[k], mixed, jnp.bfloat16 if last else jnp.float32)
+    return mixed[None]
 
 
 def solution(mesh):

time: 273 us -> 262 us (0.960); the launches traced: 269 us -> 261 us
  blocking collectives: 90.7 us -> 0 us
  waiting for transfers between devices: 80.5 us -> 121 us
  starting transfers between devices: 15.8 us -> 34.2 us
  local copies, waits for them, and re-layouts: 12.3 us -> 22.6 us
  Pallas kernels: 26.9 us -> 34.2 us
  matrix products: 13.7 us -> 20.3 us
    all_to_all x1 -> x0, blocking collectives: 90.7 us -> none  [body(): lax.all_to_all(outgoing, 'exp', split_axis=0, concat_axis=0, tiled=True)]
    all_to_all x1 -> x4, waiting for transfers between devices: 72.3 us -> 104 us  [exchanged(): lax.all_to_all(rows.reshape(peers, BLOCK, WIDTH), 'exp', split_axis=0, co...]
    all_to_all x1 -> x4, starting transfers between devices: 11.3 us -> 29.5 us  [exchanged(): lax.all_to_all(rows.reshape(peers, BLOCK, WIDTH), 'exp', split_axis=0, co...]
    unnamed x37 -> x49, local copies, waits for them, and re-layouts: 10.1 us -> 18.8 us
    all_gather x1 -> x2, waiting for transfers between devices: 3.85 us -> 10.6 us  [body(): lax.all_gather(jnp.stack([w_gate[k], w_up[k], w_down[k]]), 'ctx', axis=2,...]
    pallas_call x1 -> x2, Pallas kernels: 3.21 us -> 9.54 us  [send_rows(): pl.pallas_call(send_kernel, out_shape=jax.ShapeDtypeStruct((total, WIDTH)...]
    concatenate x1 -> x0, other arithmetic: 3.35 us -> none  [body(): jnp.concatenate([w_gate, w_up, w_down], axis=0)]
    dot_general x1 -> x2, matrix products: 2.82 us -> 5.67 us  [selectors(): lax.dot_general(onehot, rank_of, (((1,), (1,)), ((), ())), preferred_elem...]
  transfers between devices with their start and end apart: 3 -> 7, of which waited for: 3 -> 6; matrix products, arithmetic and copies ran while one was open for 10% -> 14% of each run, Pallas kernels for 1% -> 12%
where the time goes in v2:
time: 262 us; the launch traced here: 261 us
  waiting for transfers between devices  121 us (46%)
  starting transfers between devices  34.2 us (13%)
  Pallas kernels  34.2 us (13%)
  local copies, waits for them, and re-layouts  22.6 us (9%)
  matrix products  20.3 us (8%)
  other arithmetic  14.8 us (6%)
  between operations  13.8 us (5%)
    all_to_all x4, waiting for transfers between devices, exchanged(): lax.all_to_all(rows.reshape(peers, BLOCK, WIDTH), 'exp', split_axis=0, co...  104 us
    all_to_all x4, starting transfers between devices, exchanged(): lax.all_to_all(rows.reshape(peers, BLOCK, WIDTH), 'exp', split_axis=0, co...  29.5 us
    pallas_call x2, Pallas kernels, run_expert(): pl.pallas_call(expert_kernel, out_shape=jax.ShapeDtypeStruct(received.sha...  20 us
    unnamed x49, local copies, waits for them, and re-layouts  18.8 us
    all_gather x2, waiting for transfers between devices, body(): lax.all_gather(jnp.stack([w_gate[k], w_up[k], w_down[k]]), 'ctx', axis=2,...  10.6 us
    pallas_call x2, Pallas kernels, send_rows(): pl.pallas_call(send_kernel, out_shape=jax.ShapeDtypeStruct((total, WIDTH)...  9.54 us
    all_to_all x1, waiting for transfers between devices, gather_directly(): lax.all_to_all(jnp.broadcast_to(shard[None], (length, *shard.shape)), axi...  6.79 us
    add x1, other arithmetic, body(): group_order[row_index // half_rows] * half_rows + row_index % half_rows  5.74 us
  transfers between devices with their start and end apart: 7, of which 6 were waited for; matrix products, arithmetic and copies ran while one was open for 14% of the time, Pallas kernels for 12%

profile of v2, /device:TPU:32, one launch (start us, length us, event | category | flops | bytes accessed | tf_op | source)
XLA Modules:
  0.0 261.3 jit_solution(14885418790390247716)
XLA Ops:
  6.5 1.4 fusion.59
  10.0 1.4 pad_maximum_fusion
  12.7 4.6 %all-to-all-start = ((bf16[8,128,576]{1,2,0:T(8,128)(2,1)}), bf16[8,128,576]{1,2,0:T(8,128)(2,1)S(1)}, u32[]{:S(2)}, u32[]{:S(2)}) async-start(bf16[8,128,576]{1,2,0:T(8,128)(2,1)} %broadcast_in_dim.70), calls=%async_computation | async-start | bytes 2359296 | tf_op jit(solution)/shard_map/all_to_all | solution.py:34
  18.4 4.3 %compare_select_fusion.1 = s32[1024,1]{0,1:T(1,128)S(1)} fusion(s32[]{:T(128)} %bitcast.12, s32[]{:T(128)} %bitcast.13, s32[]{:T(128)} %bitcast.14, s32[]{:T(128)} %bitcast.15, s32[]{:T(128)} %bitcast.16, s32[]{:T(128)} %bitcast.18, s32[]{:T(128)} %bitcast.17), kind=kLoop, calls=%fused_computation.86 | loop fusion | flops 23552 | bytes 4124 | tf_op jit(solution)/shard_map/gather | solution.py:242
  22.7 5.7 %fusion.53 = s32[1024]{0:T(1024)S(1)} fusion(pred[1024]{0:T(1024)(128)(4,1)S(1)} %compare_reduce_fusion, pred[1024]{0:T(1024)(128)(4,1)S(1)} %compare_reduce_fusion.1, pred[1024]{0:T(1024)(128)(4,1)S(1)} %compare_reduce_fusion.2, pred[1024]{0:T(1024)(128)(4,1)S(1)} %compare_reduce_fusion.3, pred[1024]{0:T(1024)(128)(4,1)S(1)} %compare_reduce_fusion.4, ...), kind=kLoop, calls=%fused_computation.100 | loop fusion | flops 17408 | bytes 17444 | tf_op jit(solution)/shard_map/add | solution.py:242
  29.9 2.8 %fusion.3.select_ref = bf16[3328,128]{1,0:T(8,128)(2,1)S(1)} fusion(bf16[128,64]{0,1:T(8,128)(2,1)S(1)} %fusion.21, s32[3328]{0:T(1024)S(1)} %get-tuple-element.33, f32[3328]{0:T(1024)S(1)} %get-tuple-element.34), kind=kOutput, calls=%fused_computation.9 | convolution fusion | flops 55590912 | bytes 894976 | tf_op jit(solution)/shard_map/dot_general | solution.py:63
  32.7 6.8 %all-to-all-done = bf16[8,128,576]{1,2,0:T(8,128)(2,1)S(1)} async-done(((bf16[8,128,576]{1,2,0:T(8,128)(2,1)}), bf16[8,128,576]{1,2,0:T(8,128)(2,1)S(1)}, u32[]{:S(2)}, u32[]{:S(2)}) %all-to-all-start) | async-done | bytes 1179680 | tf_op jit(solution)/shard_map/all_to_all | solution.py:34
  39.7 1.3 convolution_convert_fusion
  44.0 1.3 convolution_convert_fusion.1
  49.5 4.7 %send_rows.3 = bf16[3328,256]{1,0:T(8,128)(2,1)} custom-call(bf16[3328,128]{1,0:T(8,128)(2,1)S(1)} %fusion.3.select_ref, bf16[128,2048]{1,0:T(8,128)(2,1)S(1)} %fusion.24.rows_ref), custom_call_target="tpu_custom_call" | custom-call | tf_op jit(solution)/shard_map/send_rows/pallas_call | solution.py:94
  54.3 12.3 %all-to-all-start.1 = ((bf16[32,104,256]{2,1,0:T(8,128)(2,1)}), bf16[32,104,256]{2,1,0:T(8,128)(2,1)S(1)}, u32[]{:S(2)}, u32[]{:S(2)}) async-start(bf16[32,104,256]{2,1,0:T(8,128)(2,1)} %bitcast.28), calls=%async_computation.1 | async-start | bytes 3407872 | tf_op jit(solution)/shard_map/all_to_all | solution.py:40
  66.6 2.9 %fusion.2.select_ref = bf16[3328,128]{1,0:T(8,128)(2,1)S(1)} fusion(bf16[128,64]{0,1:T(8,128)(2,1)S(1)} %fusion.21, f32[3328]{0:T(1024)S(1)} %get-tuple-element.34, s32[3328]{0:T(1024)S(1)} %broadcast_add_fusion), kind=kOutput, calls=%fused_computation.8 | convolution fusion | flops 55590912 | bytes 894976 | tf_op jit(solution)/shard_map/dot_general | solution.py:63
  69.5 4.8 %send_rows.2 = bf16[3328,256]{1,0:T(8,128)(2,1)} custom-call(bf16[3328,128]{1,0:T(8,128)(2,1)S(1)} %fusion.2.select_ref, bf16[128,2048]{1,0:T(8,128)(2,1)S(1)} %fusion.24.rows_ref), custom_call_target="tpu_custom_call" | custom-call | tf_op jit(solution)/shard_map/send_rows/pallas_call | solution.py:94
  74.2 33.2 %all-to-all-done.1 = bf16[32,104,256]{2,1,0:T(8,128)(2,1)S(1)} async-done(((bf16[32,104,256]{2,1,0:T(8,128)(2,1)}), bf16[32,104,256]{2,1,0:T(8,128)(2,1)S(1)}, u32[]{:S(2)}, u32[]{:S(2)}) %all-to-all-start.1) | async-done | bytes 1703968 | tf_op jit(solution)/shard_map/all_to_all | solution.py:40
  107.4 5.8 %all-to-all-start.2 = ((bf16[32,104,256]{2,1,0:T(8,128)(2,1)}), bf16[32,104,256]{2,1,0:T(8,128)(2,1)S(1)}, u32[]{:S(2)}, u32[]{:S(2)}) async-start(bf16[32,104,256]{2,1,0:T(8,128)(2,1)} %bitcast.30), calls=%async_computation.2 | async-start | bytes 3407872 | tf_op jit(solution)/shard_map/all_to_all | solution.py:40
  113.2 4.8 %copy-done.3 = bf16[3,2048,1024]{2,1,0:T(8,128)(2,1)S(1)} copy-done((bf16[3,2048,1024]{2,1,0:T(8,128)(2,1)S(1)}, bf16[3,2048,1024]{2,1,0:T(8,128)(2,1)}, u32[]{:S(2)}) %copy-start.3) | copy-done | bytes 12582936
  118.0 10.0 %run_expert.3 = bf16[3328,256]{1,0:T(8,128)(2,1)S(1)} custom-call(bf16[3328,256]{1,0:T(8,128)(2,1)S(1)} %bitcast.82, bf16[3,2048,1024]{2,1,0:T(8,128)(2,1)S(1)} %copy-done.3, bf16[3,2048,1024]{2,1,0:T(8,128)(2,1)S(1)} %copy-done.3, bf16[3,2048,1024]{2,1,0:T(8,128)(2,1)S(1)} %copy-done.3), custom_call_target="tpu_custom_call" | custom-call | tf_op jit(solution)/shard_map/run_expert/pallas_call | solution.py:169
  129.2 25.5 %all-to-all-done.2 = bf16[32,104,256]{2,1,0:T(8,128)(2,1)S(1)} async-done(((bf16[32,104,256]{2,1,0:T(8,128)(2,1)}), bf16[32,104,256]{2,1,0:T(8,128)(2,1)S(1)}, u32[]{:S(2)}, u32[]{:S(2)}) %all-to-all-start.2) | async-done | bytes 1703968 | tf_op jit(solution)/shard_map/all_to_all | solution.py:40
  154.7 5.6 %all-to-all-start.4 = ((bf16[32,104,256]{2,1,0:T(8,128)(2,1)}), bf16[32,104,256]{2,1,0:T(8,128)(2,1)S(1)}, u32[]{:S(2)}, u32[]{:S(2)}) async-start(bf16[32,104,256]{2,1,0:T(8,128)(2,1)} %bitcast.83), calls=%async_computation.4 | async-start | bytes 3407872 | tf_op jit(solution)/shard_map/all_to_all | solution.py:40
  160.3 10.6 %all-gather.3.cloned.1.call-done.gate_ref.up_ref.down_ref = bf16[3,2048,1024]{2,1,0:T(8,128)(2,1)} async-done(((bf16[3,2048,128]{2,1,0:T(8,128)(2,1)}), bf16[3,2048,1024]{2,1,0:T(8,128)(2,1)}) %all-gather.3.cloned.1.call-update) | async-done | bytes 12582928 | tf_op jit(solution)/shard_map/all_gather | solution.py:236
  170.9 4.6 %copy-done.2 = bf16[3,2048,1024]{2,1,0:T(8,128)(2,1)S(1)} copy-done((bf16[3,2048,1024]{2,1,0:T(8,128)(2,1)S(1)}, bf16[3,2048,1024]{2,1,0:T(8,128)(2,1)}, u32[]{:S(2)}) %copy-start.2) | copy-done | bytes 12582936
  175.5 10.0 %run_expert.2 = bf16[3328,256]{1,0:T(8,128)(2,1)S(1)} custom-call(bf16[3328,256]{1,0:T(8,128)(2,1)S(1)} %bitcast.81, bf16[3,2048,1024]{2,1,0:T(8,128)(2,1)S(1)} %copy-done.2, bf16[3,2048,1024]{2,1,0:T(8,128)(2,1)S(1)} %copy-done.2, bf16[3,2048,1024]{2,1,0:T(8,128)(2,1)S(1)} %copy-done.2), custom_call_target="tpu_custom_call" | custom-call | tf_op jit(solution)/shard_map/run_expert/pallas_call | solution.py:169
  186.7 15.2 %all-to-all-done.4 = bf16[32,104,256]{2,1,0:T(8,128)(2,1)S(1)} async-done(((bf16[32,104,256]{2,1,0:T(8,128)(2,1)}), bf16[32,104,256]{2,1,0:T(8,128)(2,1)S(1)}, u32[]{:S(2)}, u32[]{:S(2)}) %all-to-all-start.4) | async-done | bytes 1703968 | tf_op jit(solution)/shard_map/all_to_all | solution.py:40
  201.9 5.8 %all-to-all-start.3 = ((bf16[32,104,256]{2,1,0:T(8,128)(2,1)}), bf16[32,104,256]{2,1,0:T(8,128)(2,1)S(1)}, u32[]{:S(2)}, u32[]{:S(2)}) async-start(bf16[32,104,256]{2,1,0:T(8,128)(2,1)} %bitcast.80), calls=%async_computation.3 | async-start | bytes 3407872 | tf_op jit(solution)/shard_map/all_to_all | solution.py:40
  207.8 1.9 convolution_compare_fusion
  209.7 1.9 convolution_compare_fusion.3
  211.6 1.8 fusion.1.combine_ref
  213.5 2.6 %fusion.combine_ref = bf16[128,3328]{1,0:T(8,128)(2,1)} fusion(pred[128,3328]{1,0:T(32,128)(4,1)S(1)} %convolution_compare_fusion.3, s32[3328]{0:T(1024)S(1)} %broadcast_add_fusion, bf16[128,64]{0,1:T(8,128)(2,1)S(1)} %select_reduce_fusion), kind=kOutput, calls=%fused_computation.2 | convolution fusion | flops 55590912 | bytes 1307648 | tf_op jit(solution)/shard_map/dot_general | solution.py:70
  216.1 1.9 combine_rows.2.residual_ref
  219.0 30.3 %all-to-all-done.3 = bf16[32,104,256]{2,1,0:T(8,128)(2,1)S(1)} async-done(((bf16[32,104,256]{2,1,0:T(8,128)(2,1)}), bf16[32,104,256]{2,1,0:T(8,128)(2,1)S(1)}, u32[]{:S(2)}, u32[]{:S(2)}) %all-to-all-start.3) | async-done | bytes 1703968 | tf_op jit(solution)/shard_map/all_to_all | solution.py:40
  249.3 1.3 copy-done.9
  251.7 2.7 %combine_rows.3 = bf16[128,2048]{1,0:T(8,128)(2,1)} custom-call(bf16[128,3328]{1,0:T(8,128)(2,1)S(1)} %copy-done.10, bf16[3328,256]{1,0:T(8,128)(2,1)S(1)} %bitcast.79, f32[128,2048]{1,0:T(8,128)S(1)} %copy-done.9), custom_call_target="tpu_custom_call" | custom-call | tf_op jit(solution)/shard_map/combine_rows/pallas_call | solution.py:205
  (79 shorter events, 17.6 us)
Async XLA Ops:
  6.5 33.1 %copy-start = (bf16[512,1024]{1,0:T(8,128)(2,1)S(1)}, bf16[512,1024]{1,0:T(8,128)(2,1)}, u32[]{:S(2)}) copy-start(bf16[512,1024]{1,0:T(8,128)(2,1)} %param.17) | copy-start | bytes 3145732
  6.5 106.7 %all-gather.5.cloned.1.call-start = ((), (), s32[]{:S(2)}) async-start(), calls=%async_computation.6 | async-start | bytes 14155776 | tf_op jit(solution)/shard_map/all_gather | solution.py:236
  6.5 1.6 copy-start.12
  6.5 1.9 copy-start.13
  9.9 160.9 %all-gather.3.cloned.1.call-start = ((), (), s32[]{:S(2)}) async-start(), calls=%async_computation.5 | async-start | bytes 14155776 | tf_op jit(solution)/shard_map/all_gather | solution.py:236
  10.0 1.5 copy-start.17
  11.5 6.2 %copy-start.18 = (s32[16]{0:T(128)S(1)}, s32[16]{0:T(128)}, u32[]{:S(2)}) copy-start(s32[16]{0:T(128)} %param.16) | copy-start | bytes 196
  11.5 17.0 %copy-start.16 = (bf16[1,128,1536]{2,1,0:T(8,128)(2,1)S(1)}, bf16[1,128,1536]{2,1,0:T(8,128)(2,1)}, u32[]{:S(2)}) copy-start(bf16[1,128,1536]{2,1,0:T(8,128)(2,1)} %param.14) | copy-start | bytes 1179652
  12.7 15.9 %copy-start.20 = (s32[1,128,6]{1,0,2:T(1,128)S(1)}, s32[1,128,6]{1,0,2:T(1,128)}, u32[]{:S(2)}) copy-start(s32[1,128,6]{1,0,2:T(1,128)} %param.21) | copy-start | bytes 9220
  12.7 26.7 %all-to-all-start = ((bf16[8,128,576]{1,2,0:T(8,128)(2,1)}), bf16[8,128,576]{1,2,0:T(8,128)(2,1)S(1)}, u32[]{:S(2)}, u32[]{:S(2)}) async-start(bf16[8,128,576]{1,2,0:T(8,128)(2,1)} %broadcast_in_dim.70), calls=%async_computation | async-start | bytes 2359296 | tf_op jit(solution)/shard_map/all_to_all | solution.py:34
  41.0 0.9 copy-start.14
  42.8 1.2 copy-start.22
  45.4 2.2 copy-start.11
  45.4 2.3 copy-start.15
  47.7 0.9 copy-start.19
  48.7 0.8 copy-start.6
  54.3 53.1 %all-to-all-start.1 = ((bf16[32,104,256]{2,1,0:T(8,128)(2,1)}), bf16[32,104,256]{2,1,0:T(8,128)(2,1)S(1)}, u32[]{:S(2)}, u32[]{:S(2)}) async-start(bf16[32,104,256]{2,1,0:T(8,128)(2,1)} %bitcast.28), calls=%async_computation.1 | async-start | bytes 3407872 | tf_op jit(solution)/shard_map/all_to_all | solution.py:40
  107.4 47.3 %all-to-all-start.2 = ((bf16[32,104,256]{2,1,0:T(8,128)(2,1)}), bf16[32,104,256]{2,1,0:T(8,128)(2,1)S(1)}, u32[]{:S(2)}, u32[]{:S(2)}) async-start(bf16[32,104,256]{2,1,0:T(8,128)(2,1)} %bitcast.30), calls=%async_computation.2 | async-start | bytes 3407872 | tf_op jit(solution)/shard_map/all_to_all | solution.py:40
  113.2 4.8 %copy-start.3 = (bf16[3,2048,1024]{2,1,0:T(8,128)(2,1)S(1)}, bf16[3,2048,1024]{2,1,0:T(8,128)(2,1)}, u32[]{:S(2)}) copy-start(bf16[3,2048,1024]{2,1,0:T(8,128)(2,1)} %all-gather.5.cloned.1.call-done.gate_ref.up_ref.down_ref) | copy-start | bytes 37748740
  128.0 1.2 copy-start.5
  154.7 47.2 %all-to-all-start.4 = ((bf16[32,104,256]{2,1,0:T(8,128)(2,1)}), bf16[32,104,256]{2,1,0:T(8,128)(2,1)S(1)}, u32[]{:S(2)}, u32[]{:S(2)}) async-start(bf16[32,104,256]{2,1,0:T(8,128)(2,1)} %bitcast.83), calls=%async_computation.4 | async-start | bytes 3407872 | tf_op jit(solution)/shard_map/all_to_all | solution.py:40
  170.9 4.6 %copy-start.2 = (bf16[3,2048,1024]{2,1,0:T(8,128)(2,1)S(1)}, bf16[3,2048,1024]{2,1,0:T(8,128)(2,1)}, u32[]{:S(2)}) copy-start(bf16[3,2048,1024]{2,1,0:T(8,128)(2,1)} %all-gather.3.cloned.1.call-done.gate_ref.up_ref.down_ref) | copy-start | bytes 37748740
  185.5 1.2 copy-start.4
  201.9 5.9 %copy-start.21 = (f32[1,128,6]{1,0,2:T(1,128)S(1)}, f32[1,128,6]{1,0,2:T(1,128)}, u32[]{:S(2)}) copy-start(f32[1,128,6]{1,0,2:T(1,128)} %param.22) | copy-start | bytes 9220
  201.9 47.4 %all-to-all-start.3 = ((bf16[32,104,256]{2,1,0:T(8,128)(2,1)}), bf16[32,104,256]{2,1,0:T(8,128)(2,1)S(1)}, u32[]{:S(2)}, u32[]{:S(2)}) async-start(bf16[32,104,256]{2,1,0:T(8,128)(2,1)} %bitcast.80), calls=%async_computation.3 | async-start | bytes 3407872 | tf_op jit(solution)/shard_map/all_to_all | solution.py:40
  211.6 4.5 %copy-start.7 = (bf16[128,2048]{1,0:T(8,128)(2,1)S(1)}, bf16[128,2048]{1,0:T(8,128)(2,1)}, u32[]{:S(2)}) copy-start(bf16[128,2048]{1,0:T(8,128)(2,1)} %copy-done.6) | copy-start | bytes 1572868
  218.0 1.0 copy-start.8
  249.3 5.2 %copy-start.1 = (bf16[512,1024]{1,0:T(8,128)(2,1)S(1)}, bf16[512,1024]{1,0:T(8,128)(2,1)}, u32[]{:S(2)}) copy-start(bf16[512,1024]{1,0:T(8,128)(2,1)} %param.17) | copy-start | bytes 3145732
  249.3 1.3 copy-start.9
  250.6 1.2 copy-start.10
Sparse Core Ops, SparseCore 0:
  10.1 81.9 all-gather.4
  93.9 76.9 all-gather.2

commit v3 on v2

--- a/solution.py
+++ b/solution.py
@@ -3,6 +3,7 @@
 from jax import lax
 from jax.experimental import pallas as pl
 from jax.experimental.pallas import tpu as pltpu
+from jax.sharding import Mesh
 from jax.sharding import PartitionSpec as P
 
 D = 2048
@@ -24,6 +25,10 @@
 FF_BLOCK = 256
 MIB = 1 << 20
 
+EXTRA = 128
+NEAR = 2
+PAIR = LOCAL * CAP
+
 
 def whole_vmem():
     return pl.BlockSpec(memory_space=pltpu.VMEM)
@@ -38,7 +43,7 @@
 
 def exchanged(rows, peers):
     return lax.all_to_all(
-        rows.reshape(peers, BLOCK, WIDTH), "exp", split_axis=0, concat_axis=0, tiled=True
+        rows.reshape(peers, BLOCK, WIDTH), ("x", "z"), split_axis=0, concat_axis=0, tiled=True
     ).reshape(peers * BLOCK, WIDTH)
 
 
@@ -54,16 +59,12 @@
     return rank_of, gate_of
 
 
-def selectors(rank_of, gate_of, local, peers):
+def combine_weights(rank_of, gate_of, local, peers):
     total = peers * BLOCK
     row = jnp.arange(total, dtype=jnp.int32)
     expert = (row // BLOCK) * LOCAL + local
     rank = ((row % BLOCK) // CHUNKS).astype(jnp.float32)
     onehot = (expert[:, None] == jnp.arange(EXPERTS, dtype=jnp.int32)[None, :]).astype(jnp.bfloat16)
-    at_rows = lax.dot_general(
-        onehot, rank_of, (((1,), (1,)), ((), ())), preferred_element_type=jnp.float32
-    )
-    send = (at_rows == rank[:, None]).astype(jnp.bfloat16)
     at_cols = lax.dot_general(
         rank_of, onehot, (((1,), (1,)), ((), ())), preferred_element_type=jnp.float32
     )
@@ -73,64 +74,102 @@
         (((1,), (1,)), ((), ())),
         preferred_element_type=jnp.float32,
     )
-    combine = jnp.where(at_cols == rank[None, :], gate_cols, 0.0).astype(jnp.bfloat16)
-    return send, combine
-
-
-def send_kernel(select_ref, rows_ref, out_ref):
-    select = select_ref[...]
-    which = lax.broadcasted_iota(jnp.int32, select.shape, 0) % CHUNKS
-    parts = [jnp.where(which == j, select, jnp.zeros_like(select)) for j in range(CHUNKS)]
-    left = jnp.concatenate(parts, axis=1)
-    right = jnp.concatenate(
-        [rows_ref[:, j * WIDTH : (j + 1) * WIDTH] for j in range(CHUNKS)], axis=0
-    )
-    out_ref[...] = jnp.dot(left, right, preferred_element_type=jnp.float32).astype(jnp.bfloat16)
-
-
-def send_rows(select, rows):
-    total, tokens = select.shape
-    step = total // 8
+    return jnp.where(at_cols == rank[None, :], gate_cols, 0.0).astype(jnp.bfloat16)
+
+
+def shifted(rows, axis, by):
+    length = lax.axis_size(axis)
+    return lax.ppermute(rows, axis, [(i, (i + by) % length) for i in range(length)])
+
+
+def group_rows(count):
+    return -(-count * PAIR // 8) * 8
+
+
+def pick_plan(count, ring, columns):
+    rows = group_rows(count)
+    row = jnp.arange(rows, dtype=jnp.int32)
+    block = row // PAIR
+    rank = row % CAP
+    local = (row % PAIR) // CAP
+    target = jnp.arange(columns, dtype=jnp.int32)
+    expert = (target[:, None] * ring + lax.axis_index("z")) * LOCAL + local[None, :]
+    onehot = expert[:, :, None] == jnp.arange(EXTRA, dtype=jnp.int32)[None, None, :]
+    onehot = onehot.astype(jnp.bfloat16).reshape(columns * rows, EXTRA)
+    wide = lambda v: jnp.broadcast_to(jnp.tile(v, columns)[:, None], (columns * rows, EXTRA))
+    return onehot, wide(rank.astype(jnp.float32)), wide(block)
+
+
+def pick_kernel(onehot_ref, rank_ref, block_ref, *refs):
+    blocks, out_ref = refs[:-1], refs[-1]
+    onehot, rank, block = onehot_ref[...], rank_ref[...], block_ref[...]
+    left = []
+    for p, ref in enumerate(blocks):
+        at = lax.dot_general(
+            onehot, ref[:, D:], (((1,), (1,)), ((), ())), preferred_element_type=jnp.float32
+        )
+        left.append(((at == rank) & (block == p)).astype(jnp.float32).astype(jnp.bfloat16))
+    left = jnp.concatenate(left, axis=1)
+    width = 512
+    for c in range(0, D, width):
+        right = jnp.concatenate([ref[:, c : c + width] for ref in blocks], axis=0)
+        out_ref[:, c : c + width] = jnp.dot(
+            left, right, preferred_element_type=jnp.float32
+        ).astype(jnp.bfloat16)
+
+
+def pick_rows(plan, blocks):
     return pl.pallas_call(
-        send_kernel,
-        out_shape=jax.ShapeDtypeStruct((total, WIDTH), jnp.bfloat16),
-        grid=(8,),
-        in_specs=[
-            pl.BlockSpec((step, tokens), lambda i: (i, 0)),
-            pl.BlockSpec((tokens, D), lambda i: (0, 0)),
-        ],
-        out_specs=pl.BlockSpec((step, WIDTH), lambda i: (i, 0)),
-        compiler_params=pltpu.CompilerParams(vmem_limit_bytes=24 * MIB),
-        name="send_rows",
-    )(select, rows)
-
-
-def pack_matrix(transposed):
+        pick_kernel,
+        out_shape=jax.ShapeDtypeStruct((plan[0].shape[0], D), jnp.bfloat16),
+        in_specs=[whole_vmem()] * (3 + len(blocks)),
+        out_specs=whole_vmem(),
+        compiler_params=pltpu.CompilerParams(vmem_limit_bytes=32 * MIB),
+        name="pick_rows",
+    )(*plan, *blocks)
+
+
+def unpick_matrix(first, count, local, ring):
+    rows = group_rows(count)
+    out = jnp.arange(2 * ring * CAP, dtype=jnp.int32)
+    source = (out // CAP) % ring
+    listed = (source - lax.axis_index("z") + NEAR) % ring - first
+    inside = (listed >= 0) & (listed < count)
+    at = (out // (ring * CAP)) * rows + listed * PAIR + local * CAP + out % CAP
+    col = jnp.arange(2 * rows, dtype=jnp.int32)
+    return (inside[:, None] & (at[:, None] == col[None, :])).astype(jnp.bfloat16)
+
+
+def pack_matrix():
     side = PACK * CHUNKS
-    a = lax.broadcasted_iota(jnp.int32, (side, side), 1 if transposed else 0)
-    b = lax.broadcasted_iota(jnp.int32, (side, side), 0 if transposed else 1)
+    a = lax.broadcasted_iota(jnp.int32, (side, side), 1)
+    b = lax.broadcasted_iota(jnp.int32, (side, side), 0)
     return (b == (a % PACK) * CHUNKS + a // PACK).astype(jnp.float32).astype(jnp.bfloat16)
 
 
-def expert_kernel(recv_ref, gate_ref, up_ref, down_ref, out_ref, x_ref, acc_ref):
+def expert_kernel(
+    near_ref, far_ref, near_order_ref, far_order_ref, gate_ref, up_ref, down_ref, out_ref, x_ref, acc_ref
+):
     part = pl.program_id(0)
     parts = pl.num_programs(0)
     side = PACK * CHUNKS
-    blocks = recv_ref.shape[0] // side
+    blocks = out_ref.shape[0] // side
 
     @pl.when(part == 0)
     def _():
-        unpack = pack_matrix(False)
-        for b in range(blocks):
+        rows, near = near_order_ref.shape
+        far = far_order_ref.shape[1]
+        for i in range(x_ref.shape[0] // rows):
             got = jnp.dot(
-                unpack,
-                recv_ref[b * side : (b + 1) * side, :],
+                near_order_ref[...],
+                near_ref[i * near : (i + 1) * near, :],
                 preferred_element_type=jnp.float32,
-            ).astype(jnp.bfloat16)
-            for j in range(CHUNKS):
-                x_ref[b * PACK : (b + 1) * PACK, j * WIDTH : (j + 1) * WIDTH] = got[
-                    j * PACK : (j + 1) * PACK, :
-                ]
+            ) + jnp.dot(
+                far_order_ref[...],
+                far_ref[i * far : (i + 1) * far, :],
+                preferred_element_type=jnp.float32,
+            )
+            x_ref[i * rows : (i + 1) * rows, :] = got.astype(jnp.bfloat16)
 
     x = x_ref[...]
     gate = jnp.dot(x, gate_ref[0], preferred_element_type=jnp.float32)
@@ -151,7 +190,7 @@
     @pl.when(part == parts - 1)
     def _():
         x_ref[...] = (acc_ref[...] + out).astype(jnp.bfloat16)
-        pack = pack_matrix(True)
+        pack = pack_matrix()
         for b in range(blocks):
             pieces = [
                 x_ref[b * PACK : (b + 1) * PACK, j * WIDTH : (j + 1) * WIDTH]
@@ -162,16 +201,16 @@
             ).astype(jnp.bfloat16)
 
 
-def run_expert(received, weights):
-    total = received.shape[0]
-    items = total // CHUNKS
+def run_expert(received, orders, weights, items):
+    total = items * CHUNKS
     hidden_units = weights.shape[2]
+    once = lambda a: pl.BlockSpec(a.shape, lambda f: (0, 0), pipeline_mode=pl.Buffered(1))
     return pl.pallas_call(
         expert_kernel,
-        out_shape=jax.ShapeDtypeStruct(received.shape, jnp.bfloat16),
+        out_shape=jax.ShapeDtypeStruct((total, WIDTH), jnp.bfloat16),
         grid=(hidden_units // FF_BLOCK,),
         in_specs=[
-            pl.BlockSpec((total, WIDTH), lambda f: (0, 0), pipeline_mode=pl.Buffered(1)),
+            *(once(a) for a in (*received, *orders)),
             pl.BlockSpec((1, D, FF_BLOCK), lambda f: (0, 0, f)),
             pl.BlockSpec((1, D, FF_BLOCK), lambda f: (1, 0, f)),
             pl.BlockSpec((1, D, FF_BLOCK), lambda f: (2, 0, f)),
@@ -183,7 +222,7 @@
         ],
         compiler_params=pltpu.CompilerParams(vmem_limit_bytes=36 * MIB),
         name="run_expert",
-    )(received, weights, weights, weights)
+    )(*received, *orders, weights, weights, weights)
 
 
 def combine_kernel(combine_ref, rows_ref, residual_ref, out_ref):
@@ -227,7 +266,8 @@
     w_up,
     w_down,
 ):
-    peers = lax.axis_size("exp")
+    ring, columns = lax.axis_size("z"), lax.axis_size("x")
+    peers = columns * ring
     block_rows = hidden.shape[1]
     half_rows = block_rows // 2
     seq_rows = block_rows * lax.axis_size("ctx")
@@ -244,7 +284,14 @@
         positions, lax.axis_index("ctx") * block_rows, block_rows
     )
     rank_of, gate_of = routing(expert_ids[0], gate_weights[0])
-    plans = [selectors(rank_of, gate_of, k, peers) for k in range(LOCAL)]
+    combines = [combine_weights(rank_of, gate_of, k, peers) for k in range(LOCAL)]
+    counts = (2 * NEAR + 1, ring - 2 * NEAR - 1)
+    plans = [pick_plan(count, ring, columns) for count in counts]
+    orders = [
+        [unpick_matrix(first, count, k, ring) for first, count in zip((0, counts[0]), counts)]
+        for k in range(LOCAL)
+    ]
+    table = jnp.pad(rank_of, ((0, 0), (0, EXTRA - EXPERTS)))
 
     content = whole[:, :KVR]
     key_rope = whole[:, KVR:]
@@ -281,39 +328,42 @@
     factor = lax.rsqrt(jnp.mean(stream * stream, axis=1, keepdims=True) + EPSILON)
     normed = (stream * factor * norm_gain).astype(jnp.bfloat16)
 
+    own = jnp.concatenate([normed, table], axis=1)
+    up, down = [own], [own]
+    for _ in range(NEAR + 1):
+        up.append(shifted(up[-1], "z", 1))
+        down.append(shifted(down[-1], "z", -1))
+    half = block_rows // 2
+    across = jnp.concatenate(
+        [shifted(up[3][:half], "z", 1), shifted(down[3][half:], "z", -1)], axis=0
+    )
+    groups = ([up[2], up[1], own, down[1], down[2]], [down[3], across, up[3]])
     received = []
-    for k in range(LOCAL):
-        outgoing = send_rows(plans[k][0], normed)
-        if received:
-            outgoing, _ = lax.optimization_barrier((outgoing, received[-1]))
-        received.append(exchanged(outgoing, peers))
+    for plan, blocks in zip(plans, groups):
+        picked = pick_rows(plan, blocks).reshape(columns, -1, D)
+        got = lax.all_to_all(picked, "x", split_axis=0, concat_axis=0, tiled=True)
+        received.append(got.reshape(-1, D))
+    items = peers * CAP
+    returned = [
+        exchanged(run_expert(received, orders[k], weights[k], items), peers) for k in range(LOCAL)
+    ]
     mixed = residual
-    returned = [exchanged(run_expert(received[k], weights[k]), peers) for k in range(LOCAL)]
     for k in range(LOCAL):
         last = k == LOCAL - 1
-        mixed = combine_rows(plans[k][1], returned[k], mixed, jnp.bfloat16 if last else jnp.float32)
+        mixed = combine_rows(combines[k], returned[k], mixed, jnp.bfloat16 if last else jnp.float32)
     return mixed[None]
 
 
 def solution(mesh):
+    ctx, exp = mesh.devices.shape
+    ring = 8
+    mesh = Mesh(mesh.devices.reshape(ctx, exp // ring, ring), ("ctx", "x", "z"))
+    part = P(("x", "z"), "ctx", None)
+    units = P(("x", "z"), None, "ctx")
     return jax.shard_map(
         body,
         mesh=mesh,
-        in_specs=(
-            P("exp", "ctx", None),
-            P("exp", "ctx", None),
-            P("exp", "ctx", None),
-            P(),
-            P(),
-            P(),
-            P(),
-            P(),
-            P("exp", "ctx", None),
-            P("exp", "ctx", None),
-            P("exp", None, "ctx"),
-            P("exp", None, "ctx"),
-            P("exp", None, "ctx"),
-        ),
-        out_specs=P("exp", "ctx", None),
+        in_specs=(part, part, part, P(), P(), P(), P(), P(), part, part, units, units, units),
+        out_specs=part,
         check_vma=False,
     )

time: 262 us -> 255 us (0.973)
  waiting for transfers between devices: 121 us -> 104 us
  local copies, waits for them, and re-layouts: 22.6 us -> 31.6 us
  starting transfers between devices: 34.2 us -> 40.8 us
  matrix products: 20.3 us -> 14.5 us
    all_to_all x4, waiting for transfers between devices: 104 us -> 44.9 us  [the longest x2 34.5 us: exchanged(): lax.all_to_all(rows.reshape(peers, BLOCK, WIDTH), ('x', 'z'), split_axis=...]
    ppermute x0 -> x8, waiting for transfers between devices: none -> 37.1 us  [shifted(): lax.ppermute(rows, axis, [(i, (i + by) % length) for i in range(length)])]
    ppermute x0 -> x8, starting transfers between devices: none -> 14.4 us  [shifted(): lax.ppermute(rows, axis, [(i, (i + by) % length) for i in range(length)])]
    all_to_all x4, starting transfers between devices: 29.5 us -> 21.8 us  [the longest x2 12.6 us: exchanged(): lax.all_to_all(rows.reshape(peers, BLOCK, WIDTH), ('x', 'z'), split_axis=...]
    unnamed x49 -> x65, local copies, waits for them, and re-layouts: 18.8 us -> 24.9 us
    dot_general x6 -> x4, matrix products: 14 us -> 8.19 us  [the longest x2 4.45 us: combine_weights(): lax.dot_general(gate_of.astype(jnp.bfloat16), onehot, (((1,), (1,)), ((),...]
    pallas_call x4, Pallas kernels: 29.6 us -> 25.9 us  [the longest x2 21.8 us: run_expert(): pl.pallas_call(expert_kernel, out_shape=jax.ShapeDtypeStruct((total, WIDT...]
    all_to_all x1, waiting for transfers between devices: 6.79 us -> 10.2 us  [gather_directly(): lax.all_to_all(jnp.broadcast_to(shard[None], (length, *shard.shape)), axi...]
  transfers between devices with their start and end apart: 7 -> 15, of which waited for: 6 -> 11; matrix products, arithmetic and copies ran while one was open for 14% -> 14% of each run, Pallas kernels for 12% -> 12%
where the time goes in v3:
time: 255 us; the launch traced here: 254 us
  waiting for transfers between devices  104 us (41%)
  starting transfers between devices  40.8 us (16%)
  Pallas kernels  32 us (13%)
  local copies, waits for them, and re-layouts  31.6 us (12%)
  other arithmetic  17.4 us (7%)
  matrix products  14.5 us (6%)
  between operations  13.9 us (5%)
    ppermute x8, waiting for transfers between devices, shifted(): lax.ppermute(rows, axis, [(i, (i + by) % length) for i in range(length)])  37.1 us
    all_to_all x2, waiting for transfers between devices, exchanged(): lax.all_to_all(rows.reshape(peers, BLOCK, WIDTH), ('x', 'z'), split_axis=...  34.5 us
    unnamed x65, local copies, waits for them, and re-layouts  24.9 us
    pallas_call x2, Pallas kernels, run_expert(): pl.pallas_call(expert_kernel, out_shape=jax.ShapeDtypeStruct((total, WIDT...  21.8 us
    ppermute x8, starting transfers between devices, shifted(): lax.ppermute(rows, axis, [(i, (i + by) % length) for i in range(length)])  14.4 us
    all_to_all x2, starting transfers between devices, exchanged(): lax.all_to_all(rows.reshape(peers, BLOCK, WIDTH), ('x', 'z'), split_axis=...  12.6 us
    all_gather x2, waiting for transfers between devices, body(): lax.all_gather(jnp.stack([w_gate[k], w_up[k], w_down[k]]), 'ctx', axis=2,...  11.6 us
    all_to_all x2, waiting for transfers between devices, body(): got = lax.all_to_all(picked, 'x', split_axis=0, concat_axis=0, tiled=True)  10.4 us
  transfers between devices with their start and end apart: 15, of which 11 were waited for; matrix products, arithmetic and copies ran while one was open for 14% of the time, Pallas kernels for 12%

profile of v3, /device:TPU:32, one launch (start us, length us, event | category | flops | bytes accessed | tf_op | source)
XLA Modules:
  0.0 254.1 jit_solution(7586677137296784156)
XLA Ops:
  12.7 4.6 %all-to-all-start = ((bf16[8,128,576]{1,2,0:T(8,128)(2,1)}), bf16[8,128,576]{1,2,0:T(8,128)(2,1)S(1)}, u32[]{:S(2)}, u32[]{:S(2)}) async-start(bf16[8,128,576]{1,2,0:T(8,128)(2,1)} %broadcast_in_dim.63), calls=%async_computation | async-start | bytes 2359296 | tf_op jit(solution)/shard_map/all_to_all | solution.py:39
  18.8 4.3 %compare_select_fusion.1 = s32[1024,1]{0,1:T(1,128)S(1)} fusion(s32[]{:T(128)} %bitcast.12, s32[]{:T(128)} %bitcast.13, s32[]{:T(128)} %bitcast.14, s32[]{:T(128)} %bitcast.15, s32[]{:T(128)} %bitcast.16, s32[]{:T(128)} %bitcast.18, s32[]{:T(128)} %bitcast.17), kind=kLoop, calls=%fused_computation.100 | loop fusion | flops 23552 | bytes 4124 | tf_op jit(solution)/shard_map/gather | solution.py:282
  23.1 5.6 %fusion.61 = s32[1024]{0:T(1024)S(1)} fusion(pred[1024]{0:T(1024)(128)(4,1)S(1)} %compare_reduce_fusion, pred[1024]{0:T(1024)(128)(4,1)S(1)} %compare_reduce_fusion.1, pred[1024]{0:T(1024)(128)(4,1)S(1)} %compare_reduce_fusion.2, pred[1024]{0:T(1024)(128)(4,1)S(1)} %compare_reduce_fusion.3, pred[1024]{0:T(1024)(128)(4,1)S(1)} %compare_reduce_fusion.4, ...), kind=kLoop, calls=%fused_computation.114 | loop fusion | flops 17408 | bytes 17444 | tf_op jit(solution)/shard_map/add | solution.py:282
  29.2 10.2 %all-to-all-done = bf16[8,128,576]{1,2,0:T(8,128)(2,1)S(1)} async-done(((bf16[8,128,576]{1,2,0:T(8,128)(2,1)}), bf16[8,128,576]{1,2,0:T(8,128)(2,1)S(1)}, u32[]{:S(2)}, u32[]{:S(2)}) %all-to-all-start) | async-done | bytes 1179680 | tf_op jit(solution)/shard_map/all_to_all | solution.py:39
  49.4 2.3 collective-permute-start
  51.9 10.8 %collective-permute-done.refs_1_ = bf16[128,2176]{1,0:T(8,128)(2,1)S(1)} collective-permute-done((bf16[128,2176]{1,0:T(8,128)(2,1)S(1)}, bf16[128,2176]{1,0:T(8,128)(2,1)S(1)}, u32[]{:S(2)}, u32[]{:S(2)}) %collective-permute-start) | collective-permute-done | bytes 557088 | tf_op jit(solution)/shard_map/ppermute | solution.py:82
  62.7 2.3 collective-permute-start.1
  65.2 3.8 %collective-permute-start.3 = (bf16[128,2176]{1,0:T(8,128)(2,1)S(1)}, bf16[128,2176]{1,0:T(8,128)(2,1)S(1)}, u32[]{:S(2)}, u32[]{:S(2)}) collective-permute-start(bf16[128,2176]{1,0:T(8,128)(2,1)S(1)} %collective-permute-done.2.refs_3_), channel_id=1, source_target_pairs={{0,7},{1,0},{2,1},{3,2},{4,3},{5,4},{6,5},{7,6},{8,15},{9,8},{10,9... | collective-permute-start | bytes 1671176 | tf_op jit(solution)/shard_map/ppermute | solution.py:82
  69.5 10.6 %collective-permute-done.1.refs_0_ = bf16[128,2176]{1,0:T(8,128)(2,1)} collective-permute-done((bf16[128,2176]{1,0:T(8,128)(2,1)S(1)}, bf16[128,2176]{1,0:T(8,128)(2,1)}, u32[]{:S(2)}, u32[]{:S(2)}) %collective-permute-start.1) | collective-permute-done | bytes 557088 | tf_op jit(solution)/shard_map/ppermute | solution.py:82
  80.4 3.1 %pick_rows.2 = bf16[544,2048]{1,0:T(8,128)(2,1)S(1)} custom-call(bf16[544,128]{1,0:T(8,128)(2,1)S(1)} %fusion.35.onehot_ref, f32[544,128]{1,0:T(8,128)S(1)} %broadcast_in_dim.59.rank_ref, s32[544,128]{1,0:T(8,128)S(1)} %broadcast_in_dim.61.block_ref, bf16[128,2176]{1,0:T(8,128)(2,1)} %collective-permute-done.1.refs_0_, ...), custom_call_target="tpu_custom_call" | custom-call | tf_op jit(solution)/shard_map/pick_rows/pallas_call | solution.py:122
  85.0 4.4 %all-to-all-start.1 = ((bf16[4,136,2048]{2,1,0:T(8,128)(2,1)}), bf16[4,136,2048]{2,1,0:T(8,128)(2,1)S(1)}, u32[]{:S(2)}, u32[]{:S(2)}) async-start(bf16[4,136,2048]{2,1,0:T(8,128)(2,1)} %bitcast.80), calls=%async_computation.1 | async-start | bytes 4456448 | tf_op jit(solution)/shard_map/all_to_all | solution.py:344
  89.4 2.2 collective-permute-start.5
  92.4 9.9 %collective-permute-done.5.refs_2_ = bf16[128,2176]{1,0:T(8,128)(2,1)S(1)} collective-permute-done((bf16[128,2176]{1,0:T(8,128)(2,1)}, bf16[128,2176]{1,0:T(8,128)(2,1)S(1)}, u32[]{:S(2)}, u32[]{:S(2)}) %collective-permute-start.5) | collective-permute-done | bytes 557088 | tf_op jit(solution)/shard_map/ppermute | solution.py:82
  103.0 1.9 collective-permute-start.6
  107.3 3.5 %collective-permute-done.6 = bf16[64,2176]{1,0:T(8,128)(2,1)} collective-permute-done((bf16[64,2176]{1,0:T(8,128)(2,1)}, bf16[64,2176]{1,0:T(8,128)(2,1)}, u32[]{:S(2)}, u32[]{:S(2)}) %collective-permute-start.6) | collective-permute-done | bytes 278560 | tf_op jit(solution)/shard_map/ppermute | solution.py:82
  110.8 2.1 collective-permute-done.7
  116.3 4.8 %all-to-all-start.2 = ((bf16[4,80,2048]{2,1,0:T(8,128)(2,1)}), bf16[4,80,2048]{2,1,0:T(8,128)(2,1)S(1)}, u32[]{:S(2)}, u32[]{:S(2)}) async-start(bf16[4,80,2048]{2,1,0:T(8,128)(2,1)} %bitcast.84), calls=%async_computation.2 | async-start | bytes 2621440 | tf_op jit(solution)/shard_map/all_to_all | solution.py:344
  122.9 10.4 %all-to-all-done.2 = bf16[4,80,2048]{2,1,0:T(8,128)(2,1)S(1)} async-done(((bf16[4,80,2048]{2,1,0:T(8,128)(2,1)}), bf16[4,80,2048]{2,1,0:T(8,128)(2,1)S(1)}, u32[]{:S(2)}, u32[]{:S(2)}) %all-to-all-start.2) | async-done | bytes 1310752 | tf_op jit(solution)/shard_map/all_to_all | solution.py:344
  133.4 4.8 %copy-done.2 = bf16[3,2048,1024]{2,1,0:T(8,128)(2,1)S(1)} copy-done((bf16[3,2048,1024]{2,1,0:T(8,128)(2,1)S(1)}, bf16[3,2048,1024]{2,1,0:T(8,128)(2,1)}, u32[]{:S(2)}) %copy-start.2) | copy-done | bytes 12582936
  140.0 10.9 %run_expert.3 = bf16[3328,256]{1,0:T(8,128)(2,1)S(1)} custom-call(bf16[544,2048]{1,0:T(8,128)(2,1)S(1)} %bitcast.76, bf16[320,2048]{1,0:T(8,128)(2,1)S(1)} %bitcast.78, bf16[208,272]{1,0:T(8,128)(2,1)S(1)} %copy-done.14, bf16[208,160]{1,0:T(8,128)(2,1)S(1)} %copy-done.17, bf16[3,2048,1024]{2,1,0:T(8,128)(2,1)S(1)} %copy-done.2, ...), custom_call_target="tpu_custom_call" | custom-call | tf_op jit(solution)/shard_map/run_expert/pallas_call | solution.py:208
  152.1 7.1 %all-to-all-start.4 = ((bf16[32,104,256]{2,1,0:T(8,128)(2,1)}), bf16[32,104,256]{2,1,0:T(8,128)(2,1)}, u32[]{:S(2)}, u32[]{:S(2)}) async-start(bf16[32,104,256]{2,1,0:T(8,128)(2,1)} %bitcast.83), calls=%async_computation.4 | async-start | bytes 3407872 | tf_op jit(solution)/shard_map/all_to_all | solution.py:45
  159.3 11.6 %all-gather.3.cloned.1.call-done.gate_ref.up_ref.down_ref = bf16[3,2048,1024]{2,1,0:T(8,128)(2,1)} async-done(((bf16[3,2048,128]{2,1,0:T(8,128)(2,1)}), bf16[3,2048,1024]{2,1,0:T(8,128)(2,1)}) %all-gather.3.cloned.1.call-update) | async-done | bytes 12582928 | tf_op jit(solution)/shard_map/all_gather | solution.py:276
  170.9 4.6 %copy-done.3 = bf16[3,2048,1024]{2,1,0:T(8,128)(2,1)S(1)} copy-done((bf16[3,2048,1024]{2,1,0:T(8,128)(2,1)S(1)}, bf16[3,2048,1024]{2,1,0:T(8,128)(2,1)}, u32[]{:S(2)}) %copy-start.3) | copy-done | bytes 12582936
  177.3 10.9 %run_expert.2 = bf16[3328,256]{1,0:T(8,128)(2,1)S(1)} custom-call(bf16[544,2048]{1,0:T(8,128)(2,1)S(1)} %bitcast.77, bf16[320,2048]{1,0:T(8,128)(2,1)S(1)} %bitcast.79, bf16[208,272]{1,0:T(8,128)(2,1)S(1)} %copy-done.13, bf16[208,160]{1,0:T(8,128)(2,1)S(1)} %copy-done.16, bf16[3,2048,1024]{2,1,0:T(8,128)(2,1)S(1)} %copy-done.3, ...), custom_call_target="tpu_custom_call" | custom-call | tf_op jit(solution)/shard_map/run_expert/pallas_call | solution.py:208
  189.4 6.0 %all-to-all-done.4 = bf16[32,104,256]{2,1,0:T(8,128)(2,1)} async-done(((bf16[32,104,256]{2,1,0:T(8,128)(2,1)}), bf16[32,104,256]{2,1,0:T(8,128)(2,1)}, u32[]{:S(2)}, u32[]{:S(2)}) %all-to-all-start.4) | async-done | bytes 1703968 | tf_op jit(solution)/shard_map/all_to_all | solution.py:45
  195.4 5.5 %all-to-all-start.3 = ((bf16[32,104,256]{2,1,0:T(8,128)(2,1)}), bf16[32,104,256]{2,1,0:T(8,128)(2,1)S(1)}, u32[]{:S(2)}, u32[]{:S(2)}) async-start(bf16[32,104,256]{2,1,0:T(8,128)(2,1)} %bitcast.82), calls=%async_computation.3 | async-start | bytes 3407872 | tf_op jit(solution)/shard_map/all_to_all | solution.py:45
  201.0 1.9 convolution_compare_fusion
  202.9 1.9 convolution_compare_fusion.1
  206.6 2.6 %fusion.combine_ref = bf16[128,3328]{1,0:T(8,128)(2,1)} fusion(pred[128,3328]{1,0:T(32,128)(4,1)S(1)} %convolution_compare_fusion.1, s32[3328]{0:T(1024)S(1)} %broadcast_add_fusion, bf16[128,64]{0,1:T(8,128)(2,1)S(1)} %select_reduce_fusion), kind=kOutput, calls=%fused_computation.2 | convolution fusion | flops 55590912 | bytes 1307648 | tf_op jit(solution)/shard_map/dot_general | solution.py:71
  209.3 3.4 %combine_rows.2.residual_ref = f32[128,2048]{1,0:T(8,128)S(1)} custom-call(bf16[128,3328]{1,0:T(8,128)(2,1)S(1)} %fusion.1.combine_ref, bf16[3328,256]{1,0:T(8,128)(2,1)} %bitcast.35.rows_ref, bf16[128,2048]{1,0:T(8,128)(2,1)S(1)} %copy-done.9), custom_call_target="tpu_custom_call" | custom-call | tf_op jit(solution)/shard_map/combine_rows/pallas_call | solution.py:244
  213.6 28.5 %all-to-all-done.3 = bf16[32,104,256]{2,1,0:T(8,128)(2,1)S(1)} async-done(((bf16[32,104,256]{2,1,0:T(8,128)(2,1)}), bf16[32,104,256]{2,1,0:T(8,128)(2,1)S(1)}, u32[]{:S(2)}, u32[]{:S(2)}) %all-to-all-start.3) | async-done | bytes 1703968 | tf_op jit(solution)/shard_map/all_to_all | solution.py:45
  244.5 2.7 %combine_rows.3 = bf16[128,2048]{1,0:T(8,128)(2,1)} custom-call(bf16[128,3328]{1,0:T(8,128)(2,1)S(1)} %copy-done.12, bf16[3328,256]{1,0:T(8,128)(2,1)S(1)} %bitcast.81, f32[128,2048]{1,0:T(8,128)S(1)} %copy-done.11), custom_call_target="tpu_custom_call" | custom-call | tf_op jit(solution)/shard_map/combine_rows/pallas_call | solution.py:244
  (151 shorter events, 40.9 us)
Async XLA Ops:
  6.5 33.0 %copy-start = (bf16[512,1024]{1,0:T(8,128)(2,1)S(1)}, bf16[512,1024]{1,0:T(8,128)(2,1)}, u32[]{:S(2)}) copy-start(bf16[512,1024]{1,0:T(8,128)(2,1)} %param.17) | copy-start | bytes 3145732
  6.5 126.8 %all-gather.5.cloned.1.call-start = ((), (), s32[]{:S(2)}) async-start(), calls=%async_computation.6 | async-start | bytes 14155776 | tf_op jit(solution)/shard_map/all_gather | solution.py:276
  6.5 1.6 copy-start.19
  6.5 1.9 copy-start.20
  10.0 160.8 %all-gather.3.cloned.1.call-start = ((), (), s32[]{:S(2)}) async-start(), calls=%async_computation.5 | async-start | bytes 14155776 | tf_op jit(solution)/shard_map/all_gather | solution.py:276
  11.4 5.9 %copy-start.22 = (bf16[1,128,1536]{2,1,0:T(8,128)(2,1)S(1)}, bf16[1,128,1536]{2,1,0:T(8,128)(2,1)}, u32[]{:S(2)}) copy-start(bf16[1,128,1536]{2,1,0:T(8,128)(2,1)} %param.14) | copy-start | bytes 1179652
  12.7 4.8 %copy-start.28 = (s32[1,128,6]{1,0,2:T(1,128)S(1)}, s32[1,128,6]{1,0,2:T(1,128)}, u32[]{:S(2)}) copy-start(s32[1,128,6]{1,0,2:T(1,128)} %param.21) | copy-start | bytes 9220
  12.7 5.3 %copy-start.24 = (s32[16]{0:T(128)S(1)}, s32[16]{0:T(128)}, u32[]{:S(2)}) copy-start(s32[16]{0:T(128)} %param.16) | copy-start | bytes 196
  12.7 26.6 %all-to-all-start = ((bf16[8,128,576]{1,2,0:T(8,128)(2,1)}), bf16[8,128,576]{1,2,0:T(8,128)(2,1)S(1)}, u32[]{:S(2)}, u32[]{:S(2)}) async-start(bf16[8,128,576]{1,2,0:T(8,128)(2,1)} %broadcast_in_dim.63), calls=%async_computation | async-start | bytes 2359296 | tf_op jit(solution)/shard_map/all_to_all | solution.py:39
  29.0 19.6 %copy-start.25 = (bf16[128,64]{1,0:T(8,128)(2,1)}, bf16[128,64]{1,0:T(8,128)(2,1)S(1)}, u32[]{:S(2)}) copy-start(bf16[128,64]{1,0:T(8,128)(2,1)S(1)} %fusion.19) | copy-start | bytes 49156
  45.2 2.2 copy-start.18
  45.2 2.3 copy-start.21
  49.4 13.3 %collective-permute-start = (bf16[128,2176]{1,0:T(8,128)(2,1)S(1)}, bf16[128,2176]{1,0:T(8,128)(2,1)S(1)}, u32[]{:S(2)}, u32[]{:S(2)}) collective-permute-start(bf16[128,2176]{1,0:T(8,128)(2,1)S(1)} %fusion.30.refs_2_), channel_id=1, source_target_pairs={{0,1},{1,2},{2,3},{3,4},{4,5},{5,6},{6,7},{7,0},{8,9},{9,10},{10,1... | collective-permute-start | bytes 1671176 | tf_op jit(solution)/shard_map/ppermute | solution.py:82
  51.7 13.5 %collective-permute-start.2 = (bf16[128,2176]{1,0:T(8,128)(2,1)S(1)}, bf16[128,2176]{1,0:T(8,128)(2,1)S(1)}, u32[]{:S(2)}, u32[]{:S(2)}) collective-permute-start(bf16[128,2176]{1,0:T(8,128)(2,1)S(1)} %fusion.30.refs_2_), channel_id=1, source_target_pairs={{0,7},{1,0},{2,1},{3,2},{4,3},{5,4},{6,5},{7,6},{8,15},{9,8},{10,9... | collective-permute-start | bytes 1671176 | tf_op jit(solution)/shard_map/ppermute | solution.py:82
  62.7 17.4 %collective-permute-start.1 = (bf16[128,2176]{1,0:T(8,128)(2,1)S(1)}, bf16[128,2176]{1,0:T(8,128)(2,1)}, u32[]{:S(2)}, u32[]{:S(2)}) collective-permute-start(bf16[128,2176]{1,0:T(8,128)(2,1)S(1)} %collective-permute-done.refs_1_), channel_id=1, source_target_pairs={{0,1},{1,2},{2,3},{3,4},{4,5},{5,6},{6,7},{7,0},{8,9},{9,10},{10,1... | collective-permute-start | bytes 1671176 | tf_op jit(solution)/shard_map/ppermute | solution.py:82
  65.2 14.9 %collective-permute-start.3 = (bf16[128,2176]{1,0:T(8,128)(2,1)S(1)}, bf16[128,2176]{1,0:T(8,128)(2,1)S(1)}, u32[]{:S(2)}, u32[]{:S(2)}) collective-permute-start(bf16[128,2176]{1,0:T(8,128)(2,1)S(1)} %collective-permute-done.2.refs_3_), channel_id=1, source_target_pairs={{0,7},{1,0},{2,1},{3,2},{4,3},{5,4},{6,5},{7,6},{8,15},{9,8},{10,9... | collective-permute-start | bytes 1671176 | tf_op jit(solution)/shard_map/ppermute | solution.py:82
  80.1 3.4 %copy-start.15 = (bf16[128,2176]{1,0:T(8,128)(2,1)}, bf16[128,2176]{1,0:T(8,128)(2,1)S(1)}, u32[]{:S(2)}) copy-start(bf16[128,2176]{1,0:T(8,128)(2,1)S(1)} %collective-permute-done.3.refs_4_) | copy-start | bytes 1671172
  83.5 1.4 copy-start.4
  85.0 31.3 %all-to-all-start.1 = ((bf16[4,136,2048]{2,1,0:T(8,128)(2,1)}), bf16[4,136,2048]{2,1,0:T(8,128)(2,1)S(1)}, u32[]{:S(2)}, u32[]{:S(2)}) async-start(bf16[4,136,2048]{2,1,0:T(8,128)(2,1)} %bitcast.80), calls=%async_computation.1 | async-start | bytes 4456448 | tf_op jit(solution)/shard_map/all_to_all | solution.py:344
  89.4 12.9 %collective-permute-start.5 = (bf16[128,2176]{1,0:T(8,128)(2,1)}, bf16[128,2176]{1,0:T(8,128)(2,1)S(1)}, u32[]{:S(2)}, u32[]{:S(2)}) collective-permute-start(bf16[128,2176]{1,0:T(8,128)(2,1)} %collective-permute-done.1.refs_0_), channel_id=1, source_target_pairs={{0,1},{1,2},{2,3},{3,4},{4,5},{5,6},{6,7},{7,0},{8,9},{9,10},{10,1... | collective-permute-start | bytes 1671176 | tf_op jit(solution)/shard_map/ppermute | solution.py:82
  91.6 13.4 %collective-permute-start.4 = (bf16[128,2176]{1,0:T(8,128)(2,1)}, bf16[128,2176]{1,0:T(8,128)(2,1)S(1)}, u32[]{:S(2)}, u32[]{:S(2)}) collective-permute-start(bf16[128,2176]{1,0:T(8,128)(2,1)} %copy-done.15), channel_id=1, source_target_pairs={{0,7},{1,0},{2,1},{3,2},{4,3},{5,4},{6,5},{7,6},{8,15},{9,8},{10,9... | collective-permute-start | bytes 1671176 | tf_op jit(solution)/shard_map/ppermute | solution.py:82
  103.0 7.8 %collective-permute-start.6 = (bf16[64,2176]{1,0:T(8,128)(2,1)}, bf16[64,2176]{1,0:T(8,128)(2,1)}, u32[]{:S(2)}, u32[]{:S(2)}) collective-permute-start(bf16[64,2176]{1,0:T(8,128)(2,1)} %slice.69), channel_id=1, source_target_pairs={{0,1},{1,2},{2,3},{3,4},{4,5},{5,6},{6,7},{7,0},{8,9},{9,10},{10,1... | collective-permute-start | bytes 835592 | tf_op jit(solution)/shard_map/ppermute | solution.py:82
  105.7 7.2 %collective-permute-start.7 = (bf16[64,2176]{1,0:T(8,128)(2,1)}, bf16[64,2176]{1,0:T(8,128)(2,1)}, u32[]{:S(2)}, u32[]{:S(2)}) collective-permute-start(bf16[64,2176]{1,0:T(8,128)(2,1)} %slice.70), channel_id=1, source_target_pairs={{0,7},{1,0},{2,1},{3,2},{4,3},{5,4},{6,5},{7,6},{8,15},{9,8},{10,9... | collective-permute-start | bytes 835592 | tf_op jit(solution)/shard_map/ppermute | solution.py:82
  116.3 17.1 %all-to-all-start.2 = ((bf16[4,80,2048]{2,1,0:T(8,128)(2,1)}), bf16[4,80,2048]{2,1,0:T(8,128)(2,1)S(1)}, u32[]{:S(2)}, u32[]{:S(2)}) async-start(bf16[4,80,2048]{2,1,0:T(8,128)(2,1)} %bitcast.84), calls=%async_computation.2 | async-start | bytes 2621440 | tf_op jit(solution)/shard_map/all_to_all | solution.py:344
  133.4 4.8 %copy-start.2 = (bf16[3,2048,1024]{2,1,0:T(8,128)(2,1)S(1)}, bf16[3,2048,1024]{2,1,0:T(8,128)(2,1)}, u32[]{:S(2)}) copy-start(bf16[3,2048,1024]{2,1,0:T(8,128)(2,1)} %all-gather.5.cloned.1.call-done.gate_ref.up_ref.down_ref) | copy-start | bytes 37748740
  152.1 43.3 %all-to-all-start.4 = ((bf16[32,104,256]{2,1,0:T(8,128)(2,1)}), bf16[32,104,256]{2,1,0:T(8,128)(2,1)}, u32[]{:S(2)}, u32[]{:S(2)}) async-start(bf16[32,104,256]{2,1,0:T(8,128)(2,1)} %bitcast.83), calls=%async_computation.4 | async-start | bytes 3407872 | tf_op jit(solution)/shard_map/all_to_all | solution.py:45
  170.9 4.6 %copy-start.3 = (bf16[3,2048,1024]{2,1,0:T(8,128)(2,1)S(1)}, bf16[3,2048,1024]{2,1,0:T(8,128)(2,1)}, u32[]{:S(2)}) copy-start(bf16[3,2048,1024]{2,1,0:T(8,128)(2,1)} %all-gather.3.cloned.1.call-done.gate_ref.up_ref.down_ref) | copy-start | bytes 37748740
  195.4 5.5 %copy-start.29 = (f32[1,128,6]{1,0,2:T(1,128)S(1)}, f32[1,128,6]{1,0,2:T(1,128)}, u32[]{:S(2)}) copy-start(f32[1,128,6]{1,0,2:T(1,128)} %param.22) | copy-start | bytes 9220
  195.4 5.6 %copy-start.26 = (bf16[128,64]{1,0:T(8,128)(2,1)S(1)}, bf16[128,64]{1,0:T(8,128)(2,1)}, u32[]{:S(2)}) copy-start(bf16[128,64]{1,0:T(8,128)(2,1)} %copy-done.25) | copy-start | bytes 49156
  195.4 46.7 %all-to-all-start.3 = ((bf16[32,104,256]{2,1,0:T(8,128)(2,1)}), bf16[32,104,256]{2,1,0:T(8,128)(2,1)S(1)}, u32[]{:S(2)}, u32[]{:S(2)}) async-start(bf16[32,104,256]{2,1,0:T(8,128)(2,1)} %bitcast.82), calls=%async_computation.3 | async-start | bytes 3407872 | tf_op jit(solution)/shard_map/all_to_all | solution.py:45
  204.8 4.5 %copy-start.9 = (bf16[128,2048]{1,0:T(8,128)(2,1)S(1)}, bf16[128,2048]{1,0:T(8,128)(2,1)}, u32[]{:S(2)}) copy-start(bf16[128,2048]{1,0:T(8,128)(2,1)} %copy-done.8) | copy-start | bytes 1572868
  242.1 5.2 %copy-start.1 = (bf16[512,1024]{1,0:T(8,128)(2,1)S(1)}, bf16[512,1024]{1,0:T(8,128)(2,1)}, u32[]{:S(2)}) copy-start(bf16[512,1024]{1,0:T(8,128)(2,1)} %param.17) | copy-start | bytes 3145732
  (14 other events, 14.8 us)
Sparse Core Ops, SparseCore 0:
  10.2 81.8 all-gather.4
  93.9 76.9 all-gather.2

commit v4 on v3

--- a/solution.py
+++ b/solution.py
@@ -27,18 +27,17 @@
 
 EXTRA = 128
 NEAR = 2
-PAIR = LOCAL * CAP
-
-
-def whole_vmem():
-    return pl.BlockSpec(memory_space=pltpu.VMEM)
-
-
-def gather_directly(shard, axis):
-    length = lax.axis_size(axis)
-    return lax.all_to_all(
-        jnp.broadcast_to(shard[None], (length, *shard.shape)), axis, 0, 0, tiled=True
-    ).reshape(length * shard.shape[0], *shard.shape[1:])
+
+
+def gather_latent(own):
+    near = [own, shifted(own, "y", 1), shifted(own, "y", -1), shifted(own, "y", 2)]
+    mine = jnp.concatenate(near, axis=0)
+    whole = jnp.concatenate([mine, shifted(mine, "core", 1)], axis=0)
+    length, cores = lax.axis_size("y"), lax.axis_size("core")
+    along = (lax.axis_index("y") + jnp.array([0, -1, 1, -2], jnp.int32)) % length
+    core = lax.axis_index("core")
+    places = [along * cores + (core + i) % cores for i in range(cores)]
+    return whole, jnp.concatenate(places)
 
 
 def exchanged(rows, peers):
@@ -83,59 +82,68 @@
 
 
 def group_rows(count):
-    return -(-count * PAIR // 8) * 8
-
-
-def pick_plan(count, ring, columns):
-    rows = group_rows(count)
+    return -(-count * CAP // 8) * 8
+
+
+def pick_plan(count, locals_, ring, columns):
+    rows = group_rows(count * len(locals_))
     row = jnp.arange(rows, dtype=jnp.int32)
-    block = row // PAIR
+    local = row // (count * CAP)
+    block = (row // CAP) % count
     rank = row % CAP
-    local = (row % PAIR) // CAP
     target = jnp.arange(columns, dtype=jnp.int32)
-    expert = (target[:, None] * ring + lax.axis_index("z")) * LOCAL + local[None, :]
-    onehot = expert[:, :, None] == jnp.arange(EXTRA, dtype=jnp.int32)[None, None, :]
-    onehot = onehot.astype(jnp.bfloat16).reshape(columns * rows, EXTRA)
-    wide = lambda v: jnp.broadcast_to(jnp.tile(v, columns)[:, None], (columns * rows, EXTRA))
-    return onehot, wide(rank.astype(jnp.float32)), wide(block)
-
-
-def pick_kernel(onehot_ref, rank_ref, block_ref, *refs):
-    blocks, out_ref = refs[:-1], refs[-1]
-    onehot, rank, block = onehot_ref[...], rank_ref[...], block_ref[...]
+    first = (target * ring + lax.axis_index("z")) * LOCAL + locals_[0]
+    expert = (first[:, None] + local[None, :]).reshape(-1)
+    onehot = expert[:, None] == jnp.arange(EXTRA, dtype=jnp.int32)[None, :]
+    code = jnp.where(local < len(locals_), block * PACK + rank, -PACK).astype(jnp.float32)
+    code = jnp.broadcast_to(jnp.tile(code, columns)[:, None], (columns * rows, EXTRA))
+    return onehot.astype(jnp.bfloat16), code
+
+
+def pick_kernel(onehot_ref, code_ref, *refs):
+    blocks, (out_ref, made_ref, sems) = refs[:-3], refs[-3:]
+    onehot, code = onehot_ref[...], code_ref[...]
     left = []
     for p, ref in enumerate(blocks):
         at = lax.dot_general(
             onehot, ref[:, D:], (((1,), (1,)), ((), ())), preferred_element_type=jnp.float32
         )
-        left.append(((at == rank) & (block == p)).astype(jnp.float32).astype(jnp.bfloat16))
+        left.append((at + float(p * PACK) == code).astype(jnp.float32).astype(jnp.bfloat16))
     left = jnp.concatenate(left, axis=1)
-    width = 512
-    for c in range(0, D, width):
-        right = jnp.concatenate([ref[:, c : c + width] for ref in blocks], axis=0)
-        out_ref[:, c : c + width] = jnp.dot(
-            left, right, preferred_element_type=jnp.float32
-        ).astype(jnp.bfloat16)
+    copies = []
+    for c in range(made_ref.shape[0]):
+        width = made_ref.shape[2]
+        cols = slice(c * width, (c + 1) * width)
+        right = jnp.concatenate([ref[:, cols] for ref in blocks], axis=0)
+        made_ref[c] = jnp.dot(left, right, preferred_element_type=jnp.float32).astype(jnp.bfloat16)
+        copy = pltpu.make_async_copy(made_ref.at[c], out_ref.at[:, cols], sems.at[c])
+        copy.start()
+        copies.append(copy)
+    for copy in copies:
+        copy.wait()
 
 
 def pick_rows(plan, blocks):
+    total, width = plan[0].shape[0], 512
     return pl.pallas_call(
         pick_kernel,
-        out_shape=jax.ShapeDtypeStruct((plan[0].shape[0], D), jnp.bfloat16),
-        in_specs=[whole_vmem()] * (3 + len(blocks)),
-        out_specs=whole_vmem(),
-        compiler_params=pltpu.CompilerParams(vmem_limit_bytes=32 * MIB),
+        out_shape=jax.ShapeDtypeStruct((total, D), jnp.bfloat16),
+        out_specs=pl.BlockSpec(memory_space=pltpu.HBM),
+        scratch_shapes=[
+            pltpu.VMEM((D // width, total, width), jnp.bfloat16),
+            pltpu.SemaphoreType.DMA((D // width,)),
+        ],
+        compiler_params=pltpu.CompilerParams(vmem_limit_bytes=24 * MIB),
         name="pick_rows",
     )(*plan, *blocks)
 
 
-def unpick_matrix(first, count, local, ring):
-    rows = group_rows(count)
+def unpick_matrix(first, count, rows, offset, ring):
     out = jnp.arange(2 * ring * CAP, dtype=jnp.int32)
     source = (out // CAP) % ring
     listed = (source - lax.axis_index("z") + NEAR) % ring - first
     inside = (listed >= 0) & (listed < count)
-    at = (out // (ring * CAP)) * rows + listed * PAIR + local * CAP + out % CAP
+    at = (out // (ring * CAP)) * rows + offset + listed * CAP + out % CAP
     col = jnp.arange(2 * rows, dtype=jnp.int32)
     return (inside[:, None] & (at[:, None] == col[None, :])).astype(jnp.bfloat16)
 
@@ -220,35 +228,48 @@
             pltpu.VMEM((items, D), jnp.bfloat16),
             pltpu.VMEM((items, D), jnp.float32),
         ],
-        compiler_params=pltpu.CompilerParams(vmem_limit_bytes=36 * MIB),
+        compiler_params=pltpu.CompilerParams(vmem_limit_bytes=54 * MIB),
         name="run_expert",
     )(*received, *orders, weights, weights, weights)
 
 
-def combine_kernel(combine_ref, rows_ref, residual_ref, out_ref):
+def combine_kernel(combine_hbm, rows_ref, base_hbm, out_ref, combine_ref, base_ref, sems):
+    copies = [
+        pltpu.make_async_copy(combine_hbm, combine_ref, sems.at[0]),
+        pltpu.make_async_copy(base_hbm, base_ref, sems.at[1]),
+    ]
+    for copy in copies:
+        copy.start()
+    copies[0].wait()
     combine = combine_ref[...]
     which = lax.broadcasted_iota(jnp.int32, combine.shape, 1) % CHUNKS
     left = jnp.concatenate(
         [jnp.where(which == j, combine, jnp.zeros_like(combine)) for j in range(CHUNKS)], axis=0
     )
     got = jnp.dot(left, rows_ref[...], preferred_element_type=jnp.float32)
+    copies[1].wait()
     tokens = combine.shape[0]
     for j in range(CHUNKS):
         cols = slice(j * WIDTH, (j + 1) * WIDTH)
         out_ref[:, cols] = (
-            residual_ref[:, cols].astype(jnp.float32) + got[j * tokens : (j + 1) * tokens, :]
+            base_ref[:, cols].astype(jnp.float32) + got[j * tokens : (j + 1) * tokens, :]
         ).astype(out_ref.dtype)
 
 
-def combine_rows(combine, rows, residual, dtype):
+def combine_rows(combine, rows, base, dtype):
+    hbm, vmem = pl.BlockSpec(memory_space=pltpu.HBM), pl.BlockSpec(memory_space=pltpu.VMEM)
     return pl.pallas_call(
         combine_kernel,
-        out_shape=jax.ShapeDtypeStruct(residual.shape, dtype),
-        in_specs=[whole_vmem(), whole_vmem(), whole_vmem()],
-        out_specs=whole_vmem(),
+        out_shape=jax.ShapeDtypeStruct(base.shape, dtype),
+        in_specs=[hbm, vmem, hbm],
+        scratch_shapes=[
+            pltpu.VMEM(combine.shape, combine.dtype),
+            pltpu.VMEM(base.shape, base.dtype),
+            pltpu.SemaphoreType.DMA((2,)),
+        ],
         compiler_params=pltpu.CompilerParams(vmem_limit_bytes=32 * MIB),
         name="combine_rows",
-    )(combine, rows, residual)
+    )(combine, rows, base)
 
 
 def body(
@@ -270,29 +291,27 @@
     peers = columns * ring
     block_rows = hidden.shape[1]
     half_rows = block_rows // 2
-    seq_rows = block_rows * lax.axis_size("ctx")
-    whole = gather_directly(latent[0], "ctx")
-    weights = [
-        lax.all_gather(
-            jnp.stack([w_gate[k], w_up[k], w_down[k]]), "ctx", axis=2, tiled=True
-        )
-        for k in range(LOCAL)
-    ]
-    row_index = jnp.arange(seq_rows, dtype=jnp.int32)
-    positions = group_order[row_index // half_rows] * half_rows + row_index % half_rows
-    own_positions = lax.dynamic_slice_in_dim(
-        positions, lax.axis_index("ctx") * block_rows, block_rows
-    )
+    whole, places = gather_latent(latent[0])
+    seq_rows = whole.shape[0]
+    inside = jnp.arange(half_rows, dtype=jnp.int32)
+
+    def positions_of(blocks):
+        halves = (blocks[:, None] * 2 + jnp.arange(2, dtype=jnp.int32)[None, :]).reshape(-1)
+        return (group_order[halves][:, None] * half_rows + inside[None, :]).reshape(-1)
+
+    positions = positions_of(places)
+    own_positions = positions_of(places[:1])
     rank_of, gate_of = routing(expert_ids[0], gate_weights[0])
     combines = [combine_weights(rank_of, gate_of, k, peers) for k in range(LOCAL)]
-    counts = (2 * NEAR + 1, ring - 2 * NEAR - 1)
-    plans = [pick_plan(count, ring, columns) for count in counts]
-    orders = [
-        [unpick_matrix(first, count, k, ring) for first, count in zip((0, counts[0]), counts)]
-        for k in range(LOCAL)
+    near_count, far_count = 2 * NEAR + 1, ring - 2 * NEAR - 1
+    near_plan = pick_plan(near_count, range(LOCAL), ring, columns)
+    far_plans = [pick_plan(far_count, [k], ring, columns) for k in range(LOCAL)]
+    near_rows, far_rows = group_rows(near_count * LOCAL), group_rows(far_count)
+    near_orders = [
+        unpick_matrix(0, near_count, near_rows, k * near_count * CAP, ring) for k in range(LOCAL)
     ]
+    far_order = unpick_matrix(near_count, far_count, far_rows, 0, ring)
     table = jnp.pad(rank_of, ((0, 0), (0, EXTRA - EXPERTS)))
-
     content = whole[:, :KVR]
     key_rope = whole[:, KVR:]
     key_nope = jnp.dot(content, w_uk, preferred_element_type=jnp.float32).astype(jnp.bfloat16)
@@ -328,24 +347,48 @@
     factor = lax.rsqrt(jnp.mean(stream * stream, axis=1, keepdims=True) + EPSILON)
     normed = (stream * factor * norm_gain).astype(jnp.bfloat16)
 
+    shares = (w_gate, w_up, w_down)
+    weights = []
+    for k in range(LOCAL):
+        if k:
+            shares, _ = lax.optimization_barrier((shares, normed))
+        stack = jnp.concatenate([w[k : k + 1] for w in shares])
+        weights.append(lax.all_gather(stack, ("y", "core"), axis=2, tiled=True))
+
     own = jnp.concatenate([normed, table], axis=1)
     up, down = [own], [own]
-    for _ in range(NEAR + 1):
+    for _ in range(NEAR):
         up.append(shifted(up[-1], "z", 1))
         down.append(shifted(down[-1], "z", -1))
+    near = [up[2], up[1], own, down[1], down[2]]
+
+    def along_x(picked):
+        picked = picked.reshape(columns, -1, D)
+        return lax.all_to_all(picked, "x", split_axis=0, concat_axis=0, tiled=True).reshape(-1, D)
+
+    first = pick_rows(near_plan, near)
+    first, upper, lower = lax.optimization_barrier((first, up[NEAR], down[NEAR]))
+    upper, lower = shifted(upper, "z", 1), shifted(lower, "z", -1)
     half = block_rows // 2
     across = jnp.concatenate(
-        [shifted(up[3][:half], "z", 1), shifted(down[3][half:], "z", -1)], axis=0
-    )
-    groups = ([up[2], up[1], own, down[1], down[2]], [down[3], across, up[3]])
-    received = []
-    for plan, blocks in zip(plans, groups):
-        picked = pick_rows(plan, blocks).reshape(columns, -1, D)
-        got = lax.all_to_all(picked, "x", split_axis=0, concat_axis=0, tiled=True)
-        received.append(got.reshape(-1, D))
+        [shifted(upper[:half], "z", 1), shifted(lower[half:], "z", -1)], axis=0
+    )
+    from_near = along_x(first)
+    before, from_far = from_near, []
+    for k in range(LOCAL):
+        picked = pick_rows(far_plans[k], [lower, across, upper])
+        picked, _ = lax.optimization_barrier((picked, before))
+        before = along_x(picked)
+        from_far.append(before)
     items = peers * CAP
     returned = [
-        exchanged(run_expert(received, orders[k], weights[k], items), peers) for k in range(LOCAL)
+        exchanged(
+            run_expert(
+                (from_near, from_far[k]), (near_orders[k], far_order), weights[k], items
+            ),
+            peers,
+        )
+        for k in range(LOCAL)
     ]
     mixed = residual
     for k in range(LOCAL):
@@ -356,10 +399,12 @@
 
 def solution(mesh):
     ctx, exp = mesh.devices.shape
-    ring = 8
-    mesh = Mesh(mesh.devices.reshape(ctx, exp // ring, ring), ("ctx", "x", "z"))
-    part = P(("x", "z"), "ctx", None)
-    units = P(("x", "z"), None, "ctx")
+    cores, ring = 2, 8
+    mesh = Mesh(
+        mesh.devices.reshape(ctx // cores, cores, exp // ring, ring), ("y", "core", "x", "z")
+    )
+    ctx, exp = ("y", "core"), ("x", "z")
+    part, units = P(exp, ctx, None), P(exp, None, ctx)
     return jax.shard_map(
         body,
         mesh=mesh,

time: 255 us -> 244 us (0.957)
  local copies, waits for them, and re-layouts: 31.6 us -> 14.1 us
  other arithmetic: 17.4 us -> 6.47 us
  Pallas kernels: 32 us -> 38.3 us
  waiting for transfers between devices: 104 us -> 110 us
  starting transfers between devices: 40.8 us -> 45.7 us
    unnamed x65 -> x44, local copies, waits for them, and re-layouts: 24.9 us -> 8.73 us
    all_to_all x3, waiting for transfers between devices: 20.6 us -> 9.29 us  [along_x(): lax.all_to_all(picked, 'x', split_axis=0, concat_axis=0, tiled=True)]
    ppermute x8 -> x12, waiting for transfers between devices: 37.1 us -> 47.1 us  [shifted(): lax.ppermute(rows, axis, [(i, (i + by) % length) for i in range(length)])]
    all_gather x2, waiting for transfers between devices: 11.6 us -> 18.2 us  [body(): weights.append(lax.all_gather(stack, ('y', 'core'), axis=2, tiled=True))]
    pallas_call x2, Pallas kernels: 21.8 us -> 27.3 us  [run_expert(): pl.pallas_call(expert_kernel, out_shape=jax.ShapeDtypeStruct((total, WIDT...]
    add x5 -> x9, other arithmetic: 5.71 us -> 0.44 us  [the longest x2 0.15 us: positions_of(): group_order[halves][:, None] * half_rows + inside[None, :]]
    gather x10 -> x1, other arithmetic: 4.63 us -> 0.01 us  [positions_of(): group_order[halves][:, None] * half_rows + inside[None, :]]
    all_to_all x2, starting transfers between devices: 12.6 us -> 16.5 us  [exchanged(): lax.all_to_all(rows.reshape(peers, BLOCK, WIDTH), ('x', 'z'), split_axis=...]
  transfers between devices with their start and end apart: 15 -> 19, of which waited for: 11 -> 15; matrix products, arithmetic and copies ran while one was open for 14% -> 10% of each run, Pallas kernels for 12% -> 15%
where the time goes in v4:
time: 244 us; the launch traced here: 243 us
  waiting for transfers between devices  110 us (45%)
  starting transfers between devices  45.7 us (19%)
  Pallas kernels  38.3 us (16%)
  matrix products  14.5 us (6%)
  local copies, waits for them, and re-layouts  14.1 us (6%)
  between operations  14 us (6%)
  other arithmetic  6.47 us (3%)
    ppermute x12, waiting for transfers between devices, shifted(): lax.ppermute(rows, axis, [(i, (i + by) % length) for i in range(length)])  47.1 us
    all_to_all x2, waiting for transfers between devices, exchanged(): lax.all_to_all(rows.reshape(peers, BLOCK, WIDTH), ('x', 'z'), split_axis=...  35.2 us
    pallas_call x2, Pallas kernels, run_expert(): pl.pallas_call(expert_kernel, out_shape=jax.ShapeDtypeStruct((total, WIDT...  27.3 us
    all_gather x2, waiting for transfers between devices, body(): weights.append(lax.all_gather(stack, ('y', 'core'), axis=2, tiled=True))  18.2 us
    ppermute x12, starting transfers between devices, shifted(): lax.ppermute(rows, axis, [(i, (i + by) % length) for i in range(length)])  17.6 us
    all_to_all x2, starting transfers between devices, exchanged(): lax.all_to_all(rows.reshape(peers, BLOCK, WIDTH), ('x', 'z'), split_axis=...  16.5 us
    all_to_all x3, starting transfers between devices, along_x(): lax.all_to_all(picked, 'x', split_axis=0, concat_axis=0, tiled=True)  11.5 us
    all_to_all x3, waiting for transfers between devices, along_x(): lax.all_to_all(picked, 'x', split_axis=0, concat_axis=0, tiled=True)  9.29 us
  transfers between devices with their start and end apart: 19, of which 15 were waited for; matrix products, arithmetic and copies ran while one was open for 10% of the time, Pallas kernels for 15%

profile of v4, /device:TPU:32, one launch (start us, length us, event | category | flops | bytes accessed | tf_op | source)
XLA Modules:
  0.0 243.0 jit_solution(18008741549643096580)
XLA Ops:
  11.3 1.7 collective-permute-start.1
  13.0 2.0 collective-permute-start.2
  16.9 2.2 collective-permute-done.1
  19.1 1.8 collective-permute-done.2
  36.3 2.0 collective-permute-start.4
  38.4 12.7 %collective-permute-done.4.refs_1_ = bf16[128,2176]{1,0:T(8,128)(2,1)S(1)} collective-permute-done((bf16[128,2176]{1,0:T(8,128)(2,1)S(1)}, bf16[128,2176]{1,0:T(8,128)(2,1)S(1)}, u32[]{:S(2)}, u32[]{:S(2)}) %collective-permute-start.4) | collective-permute-done | bytes 557088 | tf_op jit(solution)/shard_map/ppermute | solution.py:81
  51.1 1.9 collective-permute-start.5
  53.0 2.1 collective-permute-start.7
  55.6 12.2 %collective-permute-done.5.refs_0_ = bf16[128,2176]{1,0:T(8,128)(2,1)S(1)} collective-permute-done((bf16[128,2176]{1,0:T(8,128)(2,1)S(1)}, bf16[128,2176]{1,0:T(8,128)(2,1)S(1)}, u32[]{:S(2)}, u32[]{:S(2)}) %collective-permute-start.5) | collective-permute-done | bytes 557088 | tf_op jit(solution)/shard_map/ppermute | solution.py:81
  68.4 3.0 %pick_rows.3 = bf16[544,2048]{1,0:T(8,128)(2,1)} custom-call(bf16[544,128]{1,0:T(8,128)(2,1)S(1)} %fusion.35.onehot_ref, f32[544,128]{1,0:T(8,128)S(1)} %broadcast_in_dim.61.code_ref, bf16[128,2176]{1,0:T(8,128)(2,1)S(1)} %collective-permute-done.5.refs_0_, bf16[128,2176]{1,0:T(8,128)(2,1)S(1)} %collective-permute-done.4.refs_1_, ...), custom_call_target="tpu_custom_call" | custom-call | tf_op jit(solution)/shard_map/pick_rows/pallas_call | solution.py:128
  71.4 4.5 %all-to-all-start = ((bf16[4,136,2048]{2,1,0:T(8,128)(2,1)}), bf16[4,136,2048]{2,1,0:T(8,128)(2,1)}, u32[]{:S(2)}, u32[]{:S(2)}) async-start(bf16[4,136,2048]{2,1,0:T(8,128)(2,1)} %bitcast.14), calls=%async_computation | async-start | bytes 4456448 | tf_op jit(solution)/shard_map/all_to_all | solution.py:367
  75.9 3.0 %collective-permute-start.9 = (bf16[128,2176]{1,0:T(8,128)(2,1)S(1)}, bf16[128,2176]{1,0:T(8,128)(2,1)S(1)}, u32[]{:S(2)}, u32[]{:S(2)}) collective-permute-start(bf16[128,2176]{1,0:T(8,128)(2,1)S(1)} %collective-permute-done.5.refs_0_), channel_id=1, source_target_pairs={{0,1},{1,2},{2,3},{3,4},{4,5},{5,6},{6,7},{7,0},{8,9},{9,10},{10,1... | collective-permute-start | bytes 1671176 | tf_op jit(solution)/shard_map/ppermute | solution.py:81
  79.1 11.1 %collective-permute-done.9.refs_2_ = bf16[128,2176]{1,0:T(8,128)(2,1)S(1)} collective-permute-done((bf16[128,2176]{1,0:T(8,128)(2,1)S(1)}, bf16[128,2176]{1,0:T(8,128)(2,1)S(1)}, u32[]{:S(2)}, u32[]{:S(2)}) %collective-permute-start.9) | collective-permute-done | bytes 557088 | tf_op jit(solution)/shard_map/ppermute | solution.py:81
  90.2 2.2 collective-permute-start.10
  93.7 4.6 %collective-permute-done.10 = bf16[64,2176]{1,0:T(8,128)(2,1)S(1)} collective-permute-done((bf16[64,2176]{1,0:T(8,128)(2,1)S(1)}, bf16[64,2176]{1,0:T(8,128)(2,1)S(1)}, u32[]{:S(2)}, u32[]{:S(2)}) %collective-permute-start.10) | collective-permute-done | bytes 278560 | tf_op jit(solution)/shard_map/ppermute | solution.py:81
  101.3 1.7 all-to-all-done
  103.0 3.5 %all-to-all-start.1 = ((bf16[4,40,2048]{2,1,0:T(8,128)(2,1)}), bf16[4,40,2048]{2,1,0:T(8,128)(2,1)S(1)}, u32[]{:S(2)}, u32[]{:S(2)}) async-start(bf16[4,40,2048]{2,1,0:T(8,128)(2,1)} %bitcast.16), calls=%async_computation.1 | async-start | bytes 1310720 | tf_op jit(solution)/shard_map/all_to_all | solution.py:367
  108.2 7.6 %all-to-all-done.1 = bf16[4,40,2048]{2,1,0:T(8,128)(2,1)S(1)} async-done(((bf16[4,40,2048]{2,1,0:T(8,128)(2,1)}), bf16[4,40,2048]{2,1,0:T(8,128)(2,1)S(1)}, u32[]{:S(2)}, u32[]{:S(2)}) %all-to-all-start.1) | async-done | bytes 655392 | tf_op jit(solution)/shard_map/all_to_all | solution.py:367
  115.8 3.5 %all-to-all-start.2 = ((bf16[4,40,2048]{2,1,0:T(8,128)(2,1)}), bf16[4,40,2048]{2,1,0:T(8,128)(2,1)S(1)}, u32[]{:S(2)}, u32[]{:S(2)}) async-start(bf16[4,40,2048]{2,1,0:T(8,128)(2,1)} %bitcast.18), calls=%async_computation.2 | async-start | bytes 1310720 | tf_op jit(solution)/shard_map/all_to_all | solution.py:367
  120.9 13.7 %run_expert.3 = bf16[3328,256]{1,0:T(8,128)(2,1)} custom-call(bf16[544,2048]{1,0:T(8,128)(2,1)} %bitcast.15.near_ref, bf16[160,2048]{1,0:T(8,128)(2,1)} %bitcast.67, bf16[208,272]{1,0:T(8,128)(2,1)} %get-tuple-element.23.near_order_ref, bf16[208,80]{1,0:T(8,128)(2,1)} %fusion.41.far_order_ref, ...), custom_call_target="tpu_custom_call" | custom-call | tf_op jit(solution)/shard_map/run_expert/pallas_call | solution.py:216
  135.5 10.8 %all-to-all-start.4 = ((bf16[32,104,256]{2,1,0:T(8,128)(2,1)}), bf16[32,104,256]{2,1,0:T(8,128)(2,1)S(1)}, u32[]{:S(2)}, u32[]{:S(2)}) async-start(bf16[32,104,256]{2,1,0:T(8,128)(2,1)} %bitcast.66), calls=%async_computation.4 | async-start | bytes 3407872 | tf_op jit(solution)/shard_map/all_to_all | solution.py:44
  146.3 18.2 %all-gather.3.cloned.1.call-done.gate_ref.up_ref.down_ref = bf16[3,2048,1024]{2,1,0:T(8,128)(2,1)} async-done(((bf16[3,2048,128]{2,1,0:T(8,128)(2,1)}), bf16[3,2048,1024]{2,1,0:T(8,128)(2,1)}) %all-gather.3.cloned.1.call-update) | async-done | bytes 12582928 | tf_op jit(solution)/shard_map/all_gather | solution.py:356
  164.5 13.6 %run_expert.2 = bf16[3328,256]{1,0:T(8,128)(2,1)} custom-call(bf16[544,2048]{1,0:T(8,128)(2,1)} %bitcast.15.near_ref, bf16[160,2048]{1,0:T(8,128)(2,1)} %bitcast.68, bf16[208,272]{1,0:T(8,128)(2,1)} %get-tuple-element.24.near_order_ref, bf16[208,80]{1,0:T(8,128)(2,1)} %fusion.41.far_order_ref, ...), custom_call_target="tpu_custom_call" | custom-call | tf_op jit(solution)/shard_map/run_expert/pallas_call | solution.py:216
  178.2 6.4 %all-to-all-done.4 = bf16[32,104,256]{2,1,0:T(8,128)(2,1)S(1)} async-done(((bf16[32,104,256]{2,1,0:T(8,128)(2,1)}), bf16[32,104,256]{2,1,0:T(8,128)(2,1)S(1)}, u32[]{:S(2)}, u32[]{:S(2)}) %all-to-all-start.4) | async-done | bytes 1703968 | tf_op jit(solution)/shard_map/all_to_all | solution.py:44
  184.5 5.7 %all-to-all-start.3 = ((bf16[32,104,256]{2,1,0:T(8,128)(2,1)}), bf16[32,104,256]{2,1,0:T(8,128)(2,1)S(1)}, u32[]{:S(2)}, u32[]{:S(2)}) async-start(bf16[32,104,256]{2,1,0:T(8,128)(2,1)} %bitcast.65), calls=%async_computation.3 | async-start | bytes 3407872 | tf_op jit(solution)/shard_map/all_to_all | solution.py:44
  190.3 1.9 convolution_compare_fusion
  192.2 1.9 convolution_compare_fusion.1
  194.1 1.8 fusion.1.combine_hbm
  195.9 2.6 %fusion.combine_hbm = bf16[128,3328]{1,0:T(8,128)(2,1)} fusion(pred[128,3328]{1,0:T(32,128)(4,1)S(1)} %convolution_compare_fusion.1, s32[3328]{0:T(1024)S(1)} %broadcast_add_fusion, bf16[128,64]{0,1:T(8,128)(2,1)S(1)} %select_reduce_fusion), kind=kOutput, calls=%fused_computation.4 | convolution fusion | flops 55590912 | bytes 1307648 | tf_op jit(solution)/shard_map/dot_general | solution.py:70
  198.6 2.2 combine_rows.2.base_hbm
  201.7 28.8 %all-to-all-done.3 = bf16[32,104,256]{2,1,0:T(8,128)(2,1)S(1)} async-done(((bf16[32,104,256]{2,1,0:T(8,128)(2,1)}), bf16[32,104,256]{2,1,0:T(8,128)(2,1)S(1)}, u32[]{:S(2)}, u32[]{:S(2)}) %all-to-all-start.3) | async-done | bytes 1703968 | tf_op jit(solution)/shard_map/all_to_all | solution.py:44
  233.1 3.0 %combine_rows.3 = bf16[128,2048]{1,0:T(8,128)(2,1)} custom-call(bf16[128,3328]{1,0:T(8,128)(2,1)S(1)} %copy-done.6, bf16[3328,256]{1,0:T(8,128)(2,1)S(1)} %bitcast.64, f32[128,2048]{1,0:T(8,128)S(1)} %copy-done.5), custom_call_target="tpu_custom_call" | custom-call | tf_op jit(solution)/shard_map/combine_rows/pallas_call | solution.py:261
  (141 shorter events, 35.2 us)
Async XLA Ops:
  6.5 16.6 %copy-start = (bf16[512,1024]{1,0:T(8,128)(2,1)S(1)}, bf16[512,1024]{1,0:T(8,128)(2,1)}, u32[]{:S(2)}) copy-start(bf16[512,1024]{1,0:T(8,128)(2,1)} %param.18) | copy-start | bytes 3145732
  6.5 1.5 slice-start.2
  6.5 1.7 slice-start.4
  6.5 114.4 %all-gather.5.cloned.1.call-start = ((), (), s32[]{:S(2)}) async-start(), calls=%async_computation.6 | async-start | bytes 14155776 | tf_op jit(solution)/shard_map/all_gather | solution.py:356
  8.2 1.4 copy-start.11
  8.2 6.7 %copy-start.16 = (s32[4]{0:T(128)S(1)}, s32[4]{0:T(128)}, u32[]{:S(2)}) copy-start(s32[4]{0:T(128)} %constant.257.clone) | copy-start | bytes 52
  8.2 7.1 %copy-start.7 = (s32[16]{0:T(128)S(1)}, s32[16]{0:T(128)}, u32[]{:S(2)}) copy-start(s32[16]{0:T(128)} %param.17) | copy-start | bytes 196
  9.6 154.9 %all-gather.3.cloned.1.call-start = ((), (), s32[]{:S(2)}) async-start(), calls=%async_computation.5 | async-start | bytes 14155776 | tf_op jit(solution)/shard_map/all_gather | solution.py:356
  9.6 7.3 %collective-permute-start = (bf16[128,576]{0,1:T(8,128)(2,1)S(1)}, bf16[128,576]{0,1:T(8,128)(2,1)S(1)}, u32[]{:S(2)}, u32[]{:S(2)}) collective-permute-start(bf16[128,576]{0,1:T(8,128)(2,1)S(1)} %bitcast.72), channel_id=1, source_target_pairs={{0,64},{64,128},{128,192},{192,0},{1,65},{65,129},{129,193},{193,1... | collective-permute-start | bytes 442376 | tf_op jit(solution)/shard_map/ppermute | solution.py:81
  11.3 7.8 %collective-permute-start.1 = (bf16[128,576]{0,1:T(8,128)(2,1)S(1)}, bf16[128,576]{0,1:T(8,128)(2,1)S(1)}, u32[]{:S(2)}, u32[]{:S(2)}) collective-permute-start(bf16[128,576]{0,1:T(8,128)(2,1)S(1)} %bitcast.73), channel_id=1, source_target_pairs={{0,192},{64,0},{128,64},{192,128},{1,193},{65,1},{129,65},{193,129... | collective-permute-start | bytes 442376 | tf_op jit(solution)/shard_map/ppermute | solution.py:81
  13.0 8.0 %collective-permute-start.2 = (bf16[128,576]{0,1:T(8,128)(2,1)S(1)}, bf16[128,576]{0,1:T(8,128)(2,1)S(1)}, u32[]{:S(2)}, u32[]{:S(2)}) collective-permute-start(bf16[128,576]{0,1:T(8,128)(2,1)S(1)} %bitcast.74), channel_id=1, source_target_pairs={{0,128},{64,192},{128,0},{192,64},{1,129},{65,193},{129,1},{193,65... | collective-permute-start | bytes 442376 | tf_op jit(solution)/shard_map/ppermute | solution.py:81
  21.0 2.1 collective-permute-start.3
  26.2 1.4 copy-start.17
  29.0 2.3 copy-start.8
  29.0 2.4 copy-start.12
  36.3 14.8 %collective-permute-start.4 = (bf16[128,2176]{1,0:T(8,128)(2,1)S(1)}, bf16[128,2176]{1,0:T(8,128)(2,1)S(1)}, u32[]{:S(2)}, u32[]{:S(2)}) collective-permute-start(bf16[128,2176]{1,0:T(8,128)(2,1)S(1)} %fusion.30.refs_2_), channel_id=1, source_target_pairs={{0,1},{1,2},{2,3},{3,4},{4,5},{5,6},{6,7},{7,0},{8,9},{9,10},{10,1... | collective-permute-start | bytes 1671176 | tf_op jit(solution)/shard_map/ppermute | solution.py:81
  38.3 14.7 %collective-permute-start.6 = (bf16[128,2176]{1,0:T(8,128)(2,1)S(1)}, bf16[128,2176]{1,0:T(8,128)(2,1)S(1)}, u32[]{:S(2)}, u32[]{:S(2)}) collective-permute-start(bf16[128,2176]{1,0:T(8,128)(2,1)S(1)} %fusion.30.refs_2_), channel_id=1, source_target_pairs={{0,7},{1,0},{2,1},{3,2},{4,3},{5,4},{6,5},{7,6},{8,15},{9,8},{10,9... | collective-permute-start | bytes 1671176 | tf_op jit(solution)/shard_map/ppermute | solution.py:81
  51.1 16.6 %collective-permute-start.5 = (bf16[128,2176]{1,0:T(8,128)(2,1)S(1)}, bf16[128,2176]{1,0:T(8,128)(2,1)S(1)}, u32[]{:S(2)}, u32[]{:S(2)}) collective-permute-start(bf16[128,2176]{1,0:T(8,128)(2,1)S(1)} %collective-permute-done.4.refs_1_), channel_id=1, source_target_pairs={{0,1},{1,2},{2,3},{3,4},{4,5},{5,6},{6,7},{7,0},{8,9},{9,10},{10,1... | collective-permute-start | bytes 1671176 | tf_op jit(solution)/shard_map/ppermute | solution.py:81
  53.0 15.3 %collective-permute-start.7 = (bf16[128,2176]{1,0:T(8,128)(2,1)S(1)}, bf16[128,2176]{1,0:T(8,128)(2,1)S(1)}, u32[]{:S(2)}, u32[]{:S(2)}) collective-permute-start(bf16[128,2176]{1,0:T(8,128)(2,1)S(1)} %collective-permute-done.6.refs_3_), channel_id=1, source_target_pairs={{0,7},{1,0},{2,1},{3,2},{4,3},{5,4},{6,5},{7,6},{8,15},{9,8},{10,9... | collective-permute-start | bytes 1671176 | tf_op jit(solution)/shard_map/ppermute | solution.py:81
  71.4 31.6 %all-to-all-start = ((bf16[4,136,2048]{2,1,0:T(8,128)(2,1)}), bf16[4,136,2048]{2,1,0:T(8,128)(2,1)}, u32[]{:S(2)}, u32[]{:S(2)}) async-start(bf16[4,136,2048]{2,1,0:T(8,128)(2,1)} %bitcast.14), calls=%async_computation | async-start | bytes 4456448 | tf_op jit(solution)/shard_map/all_to_all | solution.py:367
  75.9 14.3 %collective-permute-start.9 = (bf16[128,2176]{1,0:T(8,128)(2,1)S(1)}, bf16[128,2176]{1,0:T(8,128)(2,1)S(1)}, u32[]{:S(2)}, u32[]{:S(2)}) collective-permute-start(bf16[128,2176]{1,0:T(8,128)(2,1)S(1)} %collective-permute-done.5.refs_0_), channel_id=1, source_target_pairs={{0,1},{1,2},{2,3},{3,4},{4,5},{5,6},{6,7},{7,0},{8,9},{9,10},{10,1... | collective-permute-start | bytes 1671176 | tf_op jit(solution)/shard_map/ppermute | solution.py:81
  78.9 13.9 %collective-permute-start.8 = (bf16[128,2176]{1,0:T(8,128)(2,1)S(1)}, bf16[128,2176]{1,0:T(8,128)(2,1)S(1)}, u32[]{:S(2)}, u32[]{:S(2)}) collective-permute-start(bf16[128,2176]{1,0:T(8,128)(2,1)S(1)} %collective-permute-done.7.refs_4_), channel_id=1, source_target_pairs={{0,7},{1,0},{2,1},{3,2},{4,3},{5,4},{6,5},{7,6},{8,15},{9,8},{10,9... | collective-permute-start | bytes 1671176 | tf_op jit(solution)/shard_map/ppermute | solution.py:81
  90.2 8.0 %collective-permute-start.10 = (bf16[64,2176]{1,0:T(8,128)(2,1)S(1)}, bf16[64,2176]{1,0:T(8,128)(2,1)S(1)}, u32[]{:S(2)}, u32[]{:S(2)}) collective-permute-start(bf16[64,2176]{1,0:T(8,128)(2,1)S(1)} %slice.60), channel_id=1, source_target_pairs={{0,1},{1,2},{2,3},{3,4},{4,5},{5,6},{6,7},{7,0},{8,9},{9,10},{10,1... | collective-permute-start | bytes 835592 | tf_op jit(solution)/shard_map/ppermute | solution.py:81
  92.9 6.9 %collective-permute-start.11 = (bf16[64,2176]{1,0:T(8,128)(2,1)S(1)}, bf16[64,2176]{1,0:T(8,128)(2,1)S(1)}, u32[]{:S(2)}, u32[]{:S(2)}) collective-permute-start(bf16[64,2176]{1,0:T(8,128)(2,1)S(1)} %slice.61), channel_id=1, source_target_pairs={{0,7},{1,0},{2,1},{3,2},{4,3},{5,4},{6,5},{7,6},{8,15},{9,8},{10,9... | collective-permute-start | bytes 835592 | tf_op jit(solution)/shard_map/ppermute | solution.py:81
  103.0 12.8 %all-to-all-start.1 = ((bf16[4,40,2048]{2,1,0:T(8,128)(2,1)}), bf16[4,40,2048]{2,1,0:T(8,128)(2,1)S(1)}, u32[]{:S(2)}, u32[]{:S(2)}) async-start(bf16[4,40,2048]{2,1,0:T(8,128)(2,1)} %bitcast.16), calls=%async_computation.1 | async-start | bytes 1310720 | tf_op jit(solution)/shard_map/all_to_all | solution.py:367
  115.8 5.2 %copy-start.9 = (bf16[4,40,2048]{2,1,0:T(8,128)(2,1)}, bf16[4,40,2048]{2,1,0:T(8,128)(2,1)S(1)}, u32[]{:S(2)}) copy-start(bf16[4,40,2048]{2,1,0:T(8,128)(2,1)S(1)} %all-to-all-done.1) | copy-start | bytes 1966084
  115.8 18.9 %all-to-all-start.2 = ((bf16[4,40,2048]{2,1,0:T(8,128)(2,1)}), bf16[4,40,2048]{2,1,0:T(8,128)(2,1)S(1)}, u32[]{:S(2)}, u32[]{:S(2)}) async-start(bf16[4,40,2048]{2,1,0:T(8,128)(2,1)} %bitcast.18), calls=%async_computation.2 | async-start | bytes 1310720 | tf_op jit(solution)/shard_map/all_to_all | solution.py:367
  135.5 49.0 %all-to-all-start.4 = ((bf16[32,104,256]{2,1,0:T(8,128)(2,1)}), bf16[32,104,256]{2,1,0:T(8,128)(2,1)S(1)}, u32[]{:S(2)}, u32[]{:S(2)}) async-start(bf16[32,104,256]{2,1,0:T(8,128)(2,1)} %bitcast.66), calls=%async_computation.4 | async-start | bytes 3407872 | tf_op jit(solution)/shard_map/all_to_all | solution.py:44
  184.5 5.7 %copy-start.15 = (f32[1,128,6]{1,0,2:T(1,128)S(1)}, f32[1,128,6]{1,0,2:T(1,128)}, u32[]{:S(2)}) copy-start(f32[1,128,6]{1,0,2:T(1,128)} %param.23) | copy-start | bytes 9220
  184.5 46.1 %all-to-all-start.3 = ((bf16[32,104,256]{2,1,0:T(8,128)(2,1)}), bf16[32,104,256]{2,1,0:T(8,128)(2,1)S(1)}, u32[]{:S(2)}, u32[]{:S(2)}) async-start(bf16[32,104,256]{2,1,0:T(8,128)(2,1)} %bitcast.65), calls=%async_computation.3 | async-start | bytes 3407872 | tf_op jit(solution)/shard_map/all_to_all | solution.py:44
  194.1 4.5 %copy-start.3 = (bf16[128,2048]{1,0:T(8,128)(2,1)S(1)}, bf16[128,2048]{1,0:T(8,128)(2,1)}, u32[]{:S(2)}) copy-start(bf16[128,2048]{1,0:T(8,128)(2,1)} %copy-done.2) | copy-start | bytes 1572868
  230.6 5.5 %copy-start.1 = (bf16[512,1024]{1,0:T(8,128)(2,1)S(1)}, bf16[512,1024]{1,0:T(8,128)(2,1)}, u32[]{:S(2)}) copy-start(bf16[512,1024]{1,0:T(8,128)(2,1)} %param.18) | copy-start | bytes 3145732
  (11 other events, 12.3 us)
Sparse Core Ops, SparseCore 0:
  9.7 77.2 all-gather.4
  88.8 75.6 all-gather.2

commit v5 on v4

--- a/solution.py
+++ b/solution.py
@@ -180,11 +180,12 @@
             x_ref[i * rows : (i + 1) * rows, :] = got.astype(jnp.bfloat16)
 
     x = x_ref[...]
-    gate = jnp.dot(x, gate_ref[0], preferred_element_type=jnp.float32)
-    up = jnp.dot(x, up_ref[0], preferred_element_type=jnp.float32)
+    joined = lambda ref: jnp.concatenate([ref[i, 0] for i in range(ref.shape[0])], axis=1)
+    gate = jnp.dot(x, joined(gate_ref), preferred_element_type=jnp.float32)
+    up = jnp.dot(x, joined(up_ref), preferred_element_type=jnp.float32)
     inner = (gate / (1.0 + jnp.exp(-gate)) * up).astype(jnp.bfloat16)
     out = lax.dot_general(
-        inner, down_ref[0], (((1,), (1,)), ((), ())), preferred_element_type=jnp.float32
+        inner, joined(down_ref), (((1,), (1,)), ((), ())), preferred_element_type=jnp.float32
     )
 
     @pl.when(part == 0)
@@ -211,17 +212,18 @@
 
 def run_expert(received, orders, weights, items):
     total = items * CHUNKS
-    hidden_units = weights.shape[2]
+    shares, _, _, width = weights.shape
+    step = FF_BLOCK // width
     once = lambda a: pl.BlockSpec(a.shape, lambda f: (0, 0), pipeline_mode=pl.Buffered(1))
     return pl.pallas_call(
         expert_kernel,
         out_shape=jax.ShapeDtypeStruct((total, WIDTH), jnp.bfloat16),
-        grid=(hidden_units // FF_BLOCK,),
+        grid=(shares // step,),
         in_specs=[
             *(once(a) for a in (*received, *orders)),
-            pl.BlockSpec((1, D, FF_BLOCK), lambda f: (0, 0, f)),
-            pl.BlockSpec((1, D, FF_BLOCK), lambda f: (1, 0, f)),
-            pl.BlockSpec((1, D, FF_BLOCK), lambda f: (2, 0, f)),
+            pl.BlockSpec((step, 1, D, width), lambda f: (f, 0, 0, 0)),
+            pl.BlockSpec((step, 1, D, width), lambda f: (f, 1, 0, 0)),
+            pl.BlockSpec((step, 1, D, width), lambda f: (f, 2, 0, 0)),
         ],
         out_specs=pl.BlockSpec((total, WIDTH), lambda f: (0, 0), pipeline_mode=pl.Buffered(1)),
         scratch_shapes=[
@@ -233,21 +235,13 @@
     )(*received, *orders, weights, weights, weights)
 
 
-def combine_kernel(combine_hbm, rows_ref, base_hbm, out_ref, combine_ref, base_ref, sems):
-    copies = [
-        pltpu.make_async_copy(combine_hbm, combine_ref, sems.at[0]),
-        pltpu.make_async_copy(base_hbm, base_ref, sems.at[1]),
-    ]
-    for copy in copies:
-        copy.start()
-    copies[0].wait()
+def combine_kernel(combine_ref, rows_ref, base_ref, out_ref):
     combine = combine_ref[...]
     which = lax.broadcasted_iota(jnp.int32, combine.shape, 1) % CHUNKS
     left = jnp.concatenate(
         [jnp.where(which == j, combine, jnp.zeros_like(combine)) for j in range(CHUNKS)], axis=0
     )
     got = jnp.dot(left, rows_ref[...], preferred_element_type=jnp.float32)
-    copies[1].wait()
     tokens = combine.shape[0]
     for j in range(CHUNKS):
         cols = slice(j * WIDTH, (j + 1) * WIDTH)
@@ -257,17 +251,14 @@
 
 
 def combine_rows(combine, rows, base, dtype):
-    hbm, vmem = pl.BlockSpec(memory_space=pltpu.HBM), pl.BlockSpec(memory_space=pltpu.VMEM)
+    whole = lambda a: pl.BlockSpec(a.shape, lambda i: (0, 0), pipeline_mode=pl.Buffered(1))
     return pl.pallas_call(
         combine_kernel,
         out_shape=jax.ShapeDtypeStruct(base.shape, dtype),
-        in_specs=[hbm, vmem, hbm],
-        scratch_shapes=[
-            pltpu.VMEM(combine.shape, combine.dtype),
-            pltpu.VMEM(base.shape, base.dtype),
-            pltpu.SemaphoreType.DMA((2,)),
-        ],
-        compiler_params=pltpu.CompilerParams(vmem_limit_bytes=32 * MIB),
+        grid=(1,),
+        in_specs=[whole(combine), whole(rows), whole(base)],
+        out_specs=whole(base),
+        compiler_params=pltpu.CompilerParams(vmem_limit_bytes=58 * MIB),
         name="combine_rows",
     )(combine, rows, base)
 
@@ -292,6 +283,10 @@
     block_rows = hidden.shape[1]
     half_rows = block_rows // 2
     whole, places = gather_latent(latent[0])
+    weights = []
+    for k in range(LOCAL):
+        stack = jnp.concatenate([w[k : k + 1] for w in (w_gate, w_up, w_down)])
+        weights.append(lax.all_gather(stack, ("y", "core"), axis=0))
     seq_rows = whole.shape[0]
     inside = jnp.arange(half_rows, dtype=jnp.int32)
 
@@ -347,14 +342,6 @@
     factor = lax.rsqrt(jnp.mean(stream * stream, axis=1, keepdims=True) + EPSILON)
     normed = (stream * factor * norm_gain).astype(jnp.bfloat16)
 
-    shares = (w_gate, w_up, w_down)
-    weights = []
-    for k in range(LOCAL):
-        if k:
-            shares, _ = lax.optimization_barrier((shares, normed))
-        stack = jnp.concatenate([w[k : k + 1] for w in shares])
-        weights.append(lax.all_gather(stack, ("y", "core"), axis=2, tiled=True))
-
     own = jnp.concatenate([normed, table], axis=1)
     up, down = [own], [own]
     for _ in range(NEAR):

time: 244 us -> 240 us (0.984)
  waiting for transfers between devices: 110 us -> 105 us
  Pallas kernels: 38.3 us -> 42.1 us
    all_gather x2, waiting for transfers between devices: 18.2 us -> 10.8 us  [body(): weights.append(lax.all_gather(stack, ('y', 'core'), axis=0))]
    pallas_call x2, Pallas kernels: 5.24 us -> 9.4 us  [combine_rows(): pl.pallas_call(combine_kernel, out_shape=jax.ShapeDtypeStruct(base.shape,...]
    all_to_all x2, waiting for transfers between devices: 35.2 us -> 38.3 us  [exchanged(): lax.all_to_all(rows.reshape(peers, BLOCK, WIDTH), ('x', 'z'), split_axis=...]
  transfers between devices with their start and end apart: 19 -> 19, of which waited for: 15 -> 15; matrix products, arithmetic and copies ran while one was open for 10% -> 10% of each run, Pallas kernels for 15% -> 16%
where the time goes in v5:
time: 240 us
  waiting for transfers between devices  105 us (44%)
  starting transfers between devices  45.3 us (19%)
  Pallas kernels  42.1 us (18%)
  matrix products  15.2 us (6%)
  between operations  14 us (6%)
  local copies, waits for them, and re-layouts  11.8 us (5%)
  other arithmetic  6.51 us (3%)
    ppermute x12, waiting for transfers between devices, shifted(): lax.ppermute(rows, axis, [(i, (i + by) % length) for i in range(length)])  46.4 us
    all_to_all x2, waiting for transfers between devices, exchanged(): lax.all_to_all(rows.reshape(peers, BLOCK, WIDTH), ('x', 'z'), split_axis=...  38.3 us
    pallas_call x2, Pallas kernels, run_expert(): pl.pallas_call(expert_kernel, out_shape=jax.ShapeDtypeStruct((total, WIDT...  26.9 us
    ppermute x12, starting transfers between devices, shifted(): lax.ppermute(rows, axis, [(i, (i + by) % length) for i in range(length)])  17.8 us
    all_to_all x2, starting transfers between devices, exchanged(): lax.all_to_all(rows.reshape(peers, BLOCK, WIDTH), ('x', 'z'), split_axis=...  16 us
    all_to_all x3, starting transfers between devices, along_x(): lax.all_to_all(picked, 'x', split_axis=0, concat_axis=0, tiled=True)  11.5 us
    all_gather x2, waiting for transfers between devices, body(): weights.append(lax.all_gather(stack, ('y', 'core'), axis=0))  10.8 us
    pallas_call x2, Pallas kernels, combine_rows(): pl.pallas_call(combine_kernel, out_shape=jax.ShapeDtypeStruct(base.shape,...  9.4 us
  transfers between devices with their start and end apart: 19, of which 15 were waited for; matrix products, arithmetic and copies ran while one was open for 10% of the time, Pallas kernels for 16%

profile of v5, /device:TPU:32, one launch (start us, length us, event | category | flops | bytes accessed | tf_op | source)
XLA Modules:
  0.0 239.7 jit_solution(15235572108193937732)
XLA Ops:
  13.1 1.7 collective-permute-start.1
  14.8 2.0 collective-permute-start.2
  19.1 1.8 collective-permute-done.1
  20.9 1.8 collective-permute-done.2
  34.7 1.9 collective-permute-start.4
  36.7 12.6 %collective-permute-done.4.refs_1_ = bf16[128,2176]{1,0:T(8,128)(2,1)S(1)} collective-permute-done((bf16[128,2176]{1,0:T(8,128)(2,1)S(1)}, bf16[128,2176]{1,0:T(8,128)(2,1)S(1)}, u32[]{:S(2)}, u32[]{:S(2)}) %collective-permute-start.4) | collective-permute-done | bytes 557088 | tf_op jit(solution)/shard_map/ppermute | solution.py:81
  49.3 1.9 collective-permute-start.5
  51.2 2.2 collective-permute-start.7
  53.9 12.1 %collective-permute-done.5.refs_0_ = bf16[128,2176]{1,0:T(8,128)(2,1)S(1)} collective-permute-done((bf16[128,2176]{1,0:T(8,128)(2,1)S(1)}, bf16[128,2176]{1,0:T(8,128)(2,1)S(1)}, u32[]{:S(2)}, u32[]{:S(2)}) %collective-permute-start.5) | collective-permute-done | bytes 557088 | tf_op jit(solution)/shard_map/ppermute | solution.py:81
  66.6 3.0 %pick_rows.3 = bf16[544,2048]{1,0:T(8,128)(2,1)} custom-call(bf16[544,128]{1,0:T(8,128)(2,1)S(1)} %fusion.35.onehot_ref, f32[544,128]{1,0:T(8,128)S(1)} %broadcast_in_dim.61.code_ref, bf16[128,2176]{1,0:T(8,128)(2,1)S(1)} %collective-permute-done.5.refs_0_, bf16[128,2176]{1,0:T(8,128)(2,1)S(1)} %collective-permute-done.4.refs_1_, ...), custom_call_target="tpu_custom_call" | custom-call | tf_op jit(solution)/shard_map/pick_rows/pallas_call | solution.py:128
  69.5 4.5 %all-to-all-start = ((bf16[4,136,2048]{2,1,0:T(8,128)(2,1)}), bf16[4,136,2048]{2,1,0:T(8,128)(2,1)}, u32[]{:S(2)}, u32[]{:S(2)}) async-start(bf16[4,136,2048]{2,1,0:T(8,128)(2,1)} %bitcast.14), calls=%async_computation | async-start | bytes 4456448 | tf_op jit(solution)/shard_map/all_to_all | solution.py:354
  74.1 3.2 %collective-permute-start.9 = (bf16[128,2176]{1,0:T(8,128)(2,1)S(1)}, bf16[128,2176]{1,0:T(8,128)(2,1)S(1)}, u32[]{:S(2)}, u32[]{:S(2)}) collective-permute-start(bf16[128,2176]{1,0:T(8,128)(2,1)S(1)} %collective-permute-done.5.refs_0_), channel_id=1, source_target_pairs={{0,1},{1,2},{2,3},{3,4},{4,5},{5,6},{6,7},{7,0},{8,9},{9,10},{10,1... | collective-permute-start | bytes 1671176 | tf_op jit(solution)/shard_map/ppermute | solution.py:81
  77.4 11.1 %collective-permute-done.9.refs_2_ = bf16[128,2176]{1,0:T(8,128)(2,1)S(1)} collective-permute-done((bf16[128,2176]{1,0:T(8,128)(2,1)S(1)}, bf16[128,2176]{1,0:T(8,128)(2,1)S(1)}, u32[]{:S(2)}, u32[]{:S(2)}) %collective-permute-start.9) | collective-permute-done | bytes 557088 | tf_op jit(solution)/shard_map/ppermute | solution.py:81
  88.6 2.0 collective-permute-start.10
  92.0 4.7 %collective-permute-done.10 = bf16[64,2176]{1,0:T(8,128)(2,1)S(1)} collective-permute-done((bf16[64,2176]{1,0:T(8,128)(2,1)S(1)}, bf16[64,2176]{1,0:T(8,128)(2,1)S(1)}, u32[]{:S(2)}, u32[]{:S(2)}) %collective-permute-start.10) | collective-permute-done | bytes 278560 | tf_op jit(solution)/shard_map/ppermute | solution.py:81
  99.5 1.8 all-to-all-done
  101.2 3.5 %all-to-all-start.1 = ((bf16[4,40,2048]{2,1,0:T(8,128)(2,1)}), bf16[4,40,2048]{2,1,0:T(8,128)(2,1)S(1)}, u32[]{:S(2)}, u32[]{:S(2)}) async-start(bf16[4,40,2048]{2,1,0:T(8,128)(2,1)} %bitcast.16), calls=%async_computation.1 | async-start | bytes 1310720 | tf_op jit(solution)/shard_map/all_to_all | solution.py:354
  106.4 7.6 %all-to-all-done.1 = bf16[4,40,2048]{2,1,0:T(8,128)(2,1)S(1)} async-done(((bf16[4,40,2048]{2,1,0:T(8,128)(2,1)}), bf16[4,40,2048]{2,1,0:T(8,128)(2,1)S(1)}, u32[]{:S(2)}, u32[]{:S(2)}) %all-to-all-start.1) | async-done | bytes 655392 | tf_op jit(solution)/shard_map/all_to_all | solution.py:354
  114.0 3.5 %all-to-all-start.2 = ((bf16[4,40,2048]{2,1,0:T(8,128)(2,1)}), bf16[4,40,2048]{2,1,0:T(8,128)(2,1)S(1)}, u32[]{:S(2)}, u32[]{:S(2)}) async-start(bf16[4,40,2048]{2,1,0:T(8,128)(2,1)} %bitcast.18), calls=%async_computation.2 | async-start | bytes 1310720 | tf_op jit(solution)/shard_map/all_to_all | solution.py:354
  119.2 13.6 %run_expert.3 = bf16[3328,256]{1,0:T(8,128)(2,1)} custom-call(bf16[544,2048]{1,0:T(8,128)(2,1)} %bitcast.15.near_ref, bf16[160,2048]{1,0:T(8,128)(2,1)} %bitcast.75, bf16[208,272]{1,0:T(8,128)(2,1)} %get-tuple-element.23.near_order_ref, bf16[208,80]{1,0:T(8,128)(2,1)} %fusion.41.far_order_ref, bf16[8,3,2048,128]{3,2,1,0:T(8,128)(2,1)} %bitcast.68, ...), custom_call_target="tpu_custom_call" | custom-call | tf_op jit(solution)/shard_map/run_expert/pallas_call | solution.py:218
  133.7 10.4 %all-to-all-start.4 = ((bf16[32,104,256]{2,1,0:T(8,128)(2,1)}), bf16[32,104,256]{2,1,0:T(8,128)(2,1)S(1)}, u32[]{:S(2)}, u32[]{:S(2)}) async-start(bf16[32,104,256]{2,1,0:T(8,128)(2,1)} %bitcast.74), calls=%async_computation.4 | async-start | bytes 3407872 | tf_op jit(solution)/shard_map/all_to_all | solution.py:44
  144.1 10.8 %all-gather.5.cloned.1.call-done = bf16[24,2048,128]{2,1,0:T(8,128)(2,1)} async-done(((bf16[3,2048,128]{2,1,0:T(8,128)(2,1)}), bf16[24,2048,128]{2,1,0:T(8,128)(2,1)}) %all-gather.5.cloned.1.call-update) | async-done | bytes 12582928 | tf_op jit(solution)/shard_map/all_gather | solution.py:289
  154.9 13.3 %run_expert.2 = bf16[3328,256]{1,0:T(8,128)(2,1)} custom-call(bf16[544,2048]{1,0:T(8,128)(2,1)} %bitcast.15.near_ref, bf16[160,2048]{1,0:T(8,128)(2,1)} %bitcast.76, bf16[208,272]{1,0:T(8,128)(2,1)} %get-tuple-element.24.near_order_ref, bf16[208,80]{1,0:T(8,128)(2,1)} %fusion.41.far_order_ref, bf16[8,3,2048,128]{3,2,1,0:T(8,128)(2,1)} %bitcast.65, ...), custom_call_target="tpu_custom_call" | custom-call | tf_op jit(solution)/shard_map/run_expert/pallas_call | solution.py:218
  168.2 14.2 %all-to-all-done.4 = bf16[32,104,256]{2,1,0:T(8,128)(2,1)S(1)} async-done(((bf16[32,104,256]{2,1,0:T(8,128)(2,1)}), bf16[32,104,256]{2,1,0:T(8,128)(2,1)S(1)}, u32[]{:S(2)}, u32[]{:S(2)}) %all-to-all-start.4) | async-done | bytes 1703968 | tf_op jit(solution)/shard_map/all_to_all | solution.py:44
  183.5 5.6 %all-to-all-start.3 = ((bf16[32,104,256]{2,1,0:T(8,128)(2,1)}), bf16[32,104,256]{2,1,0:T(8,128)(2,1)S(1)}, u32[]{:S(2)}, u32[]{:S(2)}) async-start(bf16[32,104,256]{2,1,0:T(8,128)(2,1)} %bitcast.73), calls=%async_computation.3 | async-start | bytes 3407872 | tf_op jit(solution)/shard_map/all_to_all | solution.py:44
  189.3 1.9 convolution_compare_fusion.1
  191.1 1.9 convolution_compare_fusion
  193.0 2.6 %fusion.combine_ref = bf16[128,3328]{1,0:T(8,128)(2,1)} fusion(pred[128,3328]{1,0:T(32,128)(4,1)S(1)} %convolution_compare_fusion.1, s32[3328]{0:T(1024)S(1)} %broadcast_add_fusion, bf16[128,64]{0,1:T(8,128)(2,1)S(1)} %select_reduce_fusion), kind=kOutput, calls=%fused_computation.4 | convolution fusion | flops 55590912 | bytes 1307648 | tf_op jit(solution)/shard_map/dot_general | solution.py:70
  195.6 2.6 %fusion.1.combine_ref = bf16[128,3328]{1,0:T(8,128)(2,1)} fusion(pred[128,3328]{1,0:T(32,128)(4,1)S(1)} %convolution_compare_fusion, s32[3328]{0:T(1024)S(1)} %fusion.50, bf16[128,64]{0,1:T(8,128)(2,1)S(1)} %select_reduce_fusion), kind=kOutput, calls=%fused_computation.5 | convolution fusion | flops 55590912 | bytes 1307648 | tf_op jit(solution)/shard_map/dot_general | solution.py:70
  198.2 4.7 %combine_rows.2.base_ref = f32[128,2048]{1,0:T(8,128)} custom-call(bf16[128,3328]{1,0:T(8,128)(2,1)} %fusion.1.combine_ref, bf16[3328,256]{1,0:T(8,128)(2,1)} %bitcast.71, bf16[128,2048]{1,0:T(8,128)(2,1)} %copy-done.5), custom_call_target="tpu_custom_call" | custom-call | tf_op jit(solution)/shard_map/combine_rows/pallas_call | solution.py:255
  202.9 24.1 %all-to-all-done.3 = bf16[32,104,256]{2,1,0:T(8,128)(2,1)S(1)} async-done(((bf16[32,104,256]{2,1,0:T(8,128)(2,1)}), bf16[32,104,256]{2,1,0:T(8,128)(2,1)S(1)}, u32[]{:S(2)}, u32[]{:S(2)}) %all-to-all-start.3) | async-done | bytes 1703968 | tf_op jit(solution)/shard_map/all_to_all | solution.py:44
  228.2 4.7 %combine_rows.3 = bf16[128,2048]{1,0:T(8,128)(2,1)} custom-call(bf16[128,3328]{1,0:T(8,128)(2,1)} %fusion.combine_ref, bf16[3328,256]{1,0:T(8,128)(2,1)} %bitcast.72, f32[128,2048]{1,0:T(8,128)} %combine_rows.2.base_ref), custom_call_target="tpu_custom_call" | custom-call | tf_op jit(solution)/shard_map/combine_rows/pallas_call | solution.py:255
  (131 shorter events, 32.7 us)
Async XLA Ops:
  6.5 18.4 %copy-start = (bf16[512,1024]{1,0:T(8,128)(2,1)S(1)}, bf16[512,1024]{1,0:T(8,128)(2,1)}, u32[]{:S(2)}) copy-start(bf16[512,1024]{1,0:T(8,128)(2,1)} %param.18) | copy-start | bytes 3145732
  6.5 112.7 %all-gather.7.cloned.1.call-start = ((), (), s32[]{:S(2)}) async-start(), calls=%async_computation.6 | async-start | bytes 14155776 | tf_op jit(solution)/shard_map/all_gather | solution.py:289
  6.5 1.6 copy-start.9
  6.5 1.9 copy-start.10
  10.0 144.9 %all-gather.5.cloned.1.call-start = ((), (), s32[]{:S(2)}) async-start(), calls=%async_computation.5 | async-start | bytes 14155776 | tf_op jit(solution)/shard_map/all_gather | solution.py:289
  10.1 1.4 copy-start.11
  10.1 6.7 %copy-start.14 = (s32[1,128,6]{1,0,2:T(1,128)S(1)}, s32[1,128,6]{1,0,2:T(1,128)}, u32[]{:S(2)}) copy-start(s32[1,128,6]{1,0,2:T(1,128)} %param.22) | copy-start | bytes 9220
  10.1 6.8 %copy-start.16 = (s32[4]{0:T(128)S(1)}, s32[4]{0:T(128)}, u32[]{:S(2)}) copy-start(s32[4]{0:T(128)} %constant.257.clone) | copy-start | bytes 52
  10.1 7.2 %copy-start.2 = (s32[16]{0:T(128)S(1)}, s32[16]{0:T(128)}, u32[]{:S(2)}) copy-start(s32[16]{0:T(128)} %param.17) | copy-start | bytes 196
  11.5 7.7 %collective-permute-start = (bf16[128,576]{0,1:T(8,128)(2,1)S(1)}, bf16[128,576]{0,1:T(8,128)(2,1)S(1)}, u32[]{:S(2)}, u32[]{:S(2)}) collective-permute-start(bf16[128,576]{0,1:T(8,128)(2,1)S(1)} %bitcast.80), channel_id=1, source_target_pairs={{0,64},{64,128},{128,192},{192,0},{1,65},{65,129},{129,193},{193,1... | collective-permute-start | bytes 442376 | tf_op jit(solution)/shard_map/ppermute | solution.py:81
  13.1 7.8 %collective-permute-start.1 = (bf16[128,576]{0,1:T(8,128)(2,1)S(1)}, bf16[128,576]{0,1:T(8,128)(2,1)S(1)}, u32[]{:S(2)}, u32[]{:S(2)}) collective-permute-start(bf16[128,576]{0,1:T(8,128)(2,1)S(1)} %bitcast.81), channel_id=1, source_target_pairs={{0,192},{64,0},{128,64},{192,128},{1,193},{65,1},{129,65},{193,129... | collective-permute-start | bytes 442376 | tf_op jit(solution)/shard_map/ppermute | solution.py:81
  14.8 8.0 %collective-permute-start.2 = (bf16[128,576]{0,1:T(8,128)(2,1)S(1)}, bf16[128,576]{0,1:T(8,128)(2,1)S(1)}, u32[]{:S(2)}, u32[]{:S(2)}) collective-permute-start(bf16[128,576]{0,1:T(8,128)(2,1)S(1)} %bitcast.82), channel_id=1, source_target_pairs={{0,128},{64,192},{128,0},{192,64},{1,129},{65,193},{129,1},{193,65... | collective-permute-start | bytes 442376 | tf_op jit(solution)/shard_map/ppermute | solution.py:81
  22.8 2.1 collective-permute-start.3
  28.1 1.3 copy-start.17
  30.7 2.2 copy-start.6
  30.7 2.3 copy-start.12
  34.7 14.7 %collective-permute-start.4 = (bf16[128,2176]{1,0:T(8,128)(2,1)S(1)}, bf16[128,2176]{1,0:T(8,128)(2,1)S(1)}, u32[]{:S(2)}, u32[]{:S(2)}) collective-permute-start(bf16[128,2176]{1,0:T(8,128)(2,1)S(1)} %fusion.30.refs_2_), channel_id=1, source_target_pairs={{0,1},{1,2},{2,3},{3,4},{4,5},{5,6},{6,7},{7,0},{8,9},{9,10},{10,1... | collective-permute-start | bytes 1671176 | tf_op jit(solution)/shard_map/ppermute | solution.py:81
  36.5 14.7 %collective-permute-start.6 = (bf16[128,2176]{1,0:T(8,128)(2,1)S(1)}, bf16[128,2176]{1,0:T(8,128)(2,1)S(1)}, u32[]{:S(2)}, u32[]{:S(2)}) collective-permute-start(bf16[128,2176]{1,0:T(8,128)(2,1)S(1)} %fusion.30.refs_2_), channel_id=1, source_target_pairs={{0,7},{1,0},{2,1},{3,2},{4,3},{5,4},{6,5},{7,6},{8,15},{9,8},{10,9... | collective-permute-start | bytes 1671176 | tf_op jit(solution)/shard_map/ppermute | solution.py:81
  49.3 16.7 %collective-permute-start.5 = (bf16[128,2176]{1,0:T(8,128)(2,1)S(1)}, bf16[128,2176]{1,0:T(8,128)(2,1)S(1)}, u32[]{:S(2)}, u32[]{:S(2)}) collective-permute-start(bf16[128,2176]{1,0:T(8,128)(2,1)S(1)} %collective-permute-done.4.refs_1_), channel_id=1, source_target_pairs={{0,1},{1,2},{2,3},{3,4},{4,5},{5,6},{6,7},{7,0},{8,9},{9,10},{10,1... | collective-permute-start | bytes 1671176 | tf_op jit(solution)/shard_map/ppermute | solution.py:81
  51.2 15.2 %collective-permute-start.7 = (bf16[128,2176]{1,0:T(8,128)(2,1)S(1)}, bf16[128,2176]{1,0:T(8,128)(2,1)S(1)}, u32[]{:S(2)}, u32[]{:S(2)}) collective-permute-start(bf16[128,2176]{1,0:T(8,128)(2,1)S(1)} %collective-permute-done.6.refs_3_), channel_id=1, source_target_pairs={{0,7},{1,0},{2,1},{3,2},{4,3},{5,4},{6,5},{7,6},{8,15},{9,8},{10,9... | collective-permute-start | bytes 1671176 | tf_op jit(solution)/shard_map/ppermute | solution.py:81
  69.5 31.7 %all-to-all-start = ((bf16[4,136,2048]{2,1,0:T(8,128)(2,1)}), bf16[4,136,2048]{2,1,0:T(8,128)(2,1)}, u32[]{:S(2)}, u32[]{:S(2)}) async-start(bf16[4,136,2048]{2,1,0:T(8,128)(2,1)} %bitcast.14), calls=%async_computation | async-start | bytes 4456448 | tf_op jit(solution)/shard_map/all_to_all | solution.py:354
  74.1 14.5 %collective-permute-start.9 = (bf16[128,2176]{1,0:T(8,128)(2,1)S(1)}, bf16[128,2176]{1,0:T(8,128)(2,1)S(1)}, u32[]{:S(2)}, u32[]{:S(2)}) collective-permute-start(bf16[128,2176]{1,0:T(8,128)(2,1)S(1)} %collective-permute-done.5.refs_0_), channel_id=1, source_target_pairs={{0,1},{1,2},{2,3},{3,4},{4,5},{5,6},{6,7},{7,0},{8,9},{9,10},{10,1... | collective-permute-start | bytes 1671176 | tf_op jit(solution)/shard_map/ppermute | solution.py:81
  77.2 13.8 %collective-permute-start.8 = (bf16[128,2176]{1,0:T(8,128)(2,1)S(1)}, bf16[128,2176]{1,0:T(8,128)(2,1)S(1)}, u32[]{:S(2)}, u32[]{:S(2)}) collective-permute-start(bf16[128,2176]{1,0:T(8,128)(2,1)S(1)} %collective-permute-done.7.refs_4_), channel_id=1, source_target_pairs={{0,7},{1,0},{2,1},{3,2},{4,3},{5,4},{6,5},{7,6},{8,15},{9,8},{10,9... | collective-permute-start | bytes 1671176 | tf_op jit(solution)/shard_map/ppermute | solution.py:81
  88.6 8.1 %collective-permute-start.10 = (bf16[64,2176]{1,0:T(8,128)(2,1)S(1)}, bf16[64,2176]{1,0:T(8,128)(2,1)S(1)}, u32[]{:S(2)}, u32[]{:S(2)}) collective-permute-start(bf16[64,2176]{1,0:T(8,128)(2,1)S(1)} %slice.60), channel_id=1, source_target_pairs={{0,1},{1,2},{2,3},{3,4},{4,5},{5,6},{6,7},{7,0},{8,9},{9,10},{10,1... | collective-permute-start | bytes 835592 | tf_op jit(solution)/shard_map/ppermute | solution.py:81
  91.0 7.0 %collective-permute-start.11 = (bf16[64,2176]{1,0:T(8,128)(2,1)S(1)}, bf16[64,2176]{1,0:T(8,128)(2,1)S(1)}, u32[]{:S(2)}, u32[]{:S(2)}) collective-permute-start(bf16[64,2176]{1,0:T(8,128)(2,1)S(1)} %slice.61), channel_id=1, source_target_pairs={{0,7},{1,0},{2,1},{3,2},{4,3},{5,4},{6,5},{7,6},{8,15},{9,8},{10,9... | collective-permute-start | bytes 835592 | tf_op jit(solution)/shard_map/ppermute | solution.py:81
  101.2 12.8 %all-to-all-start.1 = ((bf16[4,40,2048]{2,1,0:T(8,128)(2,1)}), bf16[4,40,2048]{2,1,0:T(8,128)(2,1)S(1)}, u32[]{:S(2)}, u32[]{:S(2)}) async-start(bf16[4,40,2048]{2,1,0:T(8,128)(2,1)} %bitcast.16), calls=%async_computation.1 | async-start | bytes 1310720 | tf_op jit(solution)/shard_map/all_to_all | solution.py:354
  114.0 5.2 %copy-start.7 = (bf16[4,40,2048]{2,1,0:T(8,128)(2,1)}, bf16[4,40,2048]{2,1,0:T(8,128)(2,1)S(1)}, u32[]{:S(2)}) copy-start(bf16[4,40,2048]{2,1,0:T(8,128)(2,1)S(1)} %all-to-all-done.1) | copy-start | bytes 1966084
  114.0 18.8 %all-to-all-start.2 = ((bf16[4,40,2048]{2,1,0:T(8,128)(2,1)}), bf16[4,40,2048]{2,1,0:T(8,128)(2,1)S(1)}, u32[]{:S(2)}, u32[]{:S(2)}) async-start(bf16[4,40,2048]{2,1,0:T(8,128)(2,1)} %bitcast.18), calls=%async_computation.2 | async-start | bytes 1310720 | tf_op jit(solution)/shard_map/all_to_all | solution.py:354
  133.7 48.7 %all-to-all-start.4 = ((bf16[32,104,256]{2,1,0:T(8,128)(2,1)}), bf16[32,104,256]{2,1,0:T(8,128)(2,1)S(1)}, u32[]{:S(2)}, u32[]{:S(2)}) async-start(bf16[32,104,256]{2,1,0:T(8,128)(2,1)} %bitcast.74), calls=%async_computation.4 | async-start | bytes 3407872 | tf_op jit(solution)/shard_map/all_to_all | solution.py:44
  182.4 6.8 %copy-start.15 = (f32[1,128,6]{1,0,2:T(1,128)S(1)}, f32[1,128,6]{1,0,2:T(1,128)}, u32[]{:S(2)}) copy-start(f32[1,128,6]{1,0,2:T(1,128)} %param.23) | copy-start | bytes 9220
  183.5 43.4 %all-to-all-start.3 = ((bf16[32,104,256]{2,1,0:T(8,128)(2,1)}), bf16[32,104,256]{2,1,0:T(8,128)(2,1)S(1)}, u32[]{:S(2)}, u32[]{:S(2)}) async-start(bf16[32,104,256]{2,1,0:T(8,128)(2,1)} %bitcast.73), calls=%async_computation.3 | async-start | bytes 3407872 | tf_op jit(solution)/shard_map/all_to_all | solution.py:44
  227.0 5.9 %copy-start.1 = (bf16[512,1024]{1,0:T(8,128)(2,1)S(1)}, bf16[512,1024]{1,0:T(8,128)(2,1)}, u32[]{:S(2)}) copy-start(bf16[512,1024]{1,0:T(8,128)(2,1)} %param.18) | copy-start | bytes 3145732
  (5 other events, 4.9 us)
Sparse Core Ops, SparseCore 0:
  10.1 72.5 all-gather.6
  84.5 70.2 all-gather.4

commit v6 on v5

--- a/solution.py
+++ b/solution.py
@@ -26,7 +26,7 @@
 MIB = 1 << 20
 
 EXTRA = 128
-NEAR = 2
+DISTANCES = ((-1, 0, 1), (-2, 2), (3, 4, -3))
 
 
 def gather_latent(own):
@@ -79,6 +79,10 @@
 def shifted(rows, axis, by):
     length = lax.axis_size(axis)
     return lax.ppermute(rows, axis, [(i, (i + by) % length) for i in range(length)])
+
+
+def held(*arrays):
+    return lax.optimization_barrier(arrays)
 
 
 def group_rows(count):
@@ -138,11 +142,13 @@
     )(*plan, *blocks)
 
 
-def unpick_matrix(first, count, rows, offset, ring):
+def unpick_matrix(distances, rows, offset, ring):
     out = jnp.arange(2 * ring * CAP, dtype=jnp.int32)
-    source = (out // CAP) % ring
-    listed = (source - lax.axis_index("z") + NEAR) % ring - first
-    inside = (listed >= 0) & (listed < count)
+    distance = ((out // CAP) % ring - lax.axis_index("z")) % ring
+    inside, listed = jnp.zeros(out.shape, bool), jnp.zeros_like(out)
+    for i, d in enumerate(distances):
+        here = distance == d % ring
+        inside, listed = inside | here, jnp.where(here, i, listed)
     at = (out // (ring * CAP)) * rows + offset + listed * CAP + out % CAP
     col = jnp.arange(2 * rows, dtype=jnp.int32)
     return (inside[:, None] & (at[:, None] == col[None, :])).astype(jnp.bfloat16)
@@ -155,9 +161,10 @@
     return (b == (a % PACK) * CHUNKS + a // PACK).astype(jnp.float32).astype(jnp.bfloat16)
 
 
-def expert_kernel(
-    near_ref, far_ref, near_order_ref, far_order_ref, gate_ref, up_ref, down_ref, out_ref, x_ref, acc_ref
-):
+def expert_kernel(*refs):
+    groups = len(DISTANCES)
+    received, orders = refs[:groups], refs[groups : 2 * groups]
+    gate_ref, up_ref, down_ref, out_ref, x_ref, acc_ref = refs[2 * groups :]
     part = pl.program_id(0)
     parts = pl.num_programs(0)
     side = PACK * CHUNKS
@@ -165,18 +172,16 @@
 
     @pl.when(part == 0)
     def _():
-        rows, near = near_order_ref.shape
-        far = far_order_ref.shape[1]
+        rows = orders[0].shape[0]
         for i in range(x_ref.shape[0] // rows):
-            got = jnp.dot(
-                near_order_ref[...],
-                near_ref[i * near : (i + 1) * near, :],
-                preferred_element_type=jnp.float32,
-            ) + jnp.dot(
-                far_order_ref[...],
-                far_ref[i * far : (i + 1) * far, :],
-                preferred_element_type=jnp.float32,
-            )
+            got = 0.0
+            for ref, order in zip(received, orders):
+                cols = order.shape[1]
+                got = got + jnp.dot(
+                    order[...],
+                    ref[i * cols : (i + 1) * cols, :],
+                    preferred_element_type=jnp.float32,
+                )
             x_ref[i * rows : (i + 1) * rows, :] = got.astype(jnp.bfloat16)
 
     x = x_ref[...]
@@ -251,14 +256,13 @@
 
 
 def combine_rows(combine, rows, base, dtype):
-    whole = lambda a: pl.BlockSpec(a.shape, lambda i: (0, 0), pipeline_mode=pl.Buffered(1))
+    vmem = pl.BlockSpec(memory_space=pltpu.VMEM)
     return pl.pallas_call(
         combine_kernel,
         out_shape=jax.ShapeDtypeStruct(base.shape, dtype),
-        grid=(1,),
-        in_specs=[whole(combine), whole(rows), whole(base)],
-        out_specs=whole(base),
-        compiler_params=pltpu.CompilerParams(vmem_limit_bytes=58 * MIB),
+        in_specs=[vmem] * 3,
+        out_specs=vmem,
+        compiler_params=pltpu.CompilerParams(vmem_limit_bytes=32 * MIB),
         name="combine_rows",
     )(combine, rows, base)
 
@@ -298,14 +302,16 @@
     own_positions = positions_of(places[:1])
     rank_of, gate_of = routing(expert_ids[0], gate_weights[0])
     combines = [combine_weights(rank_of, gate_of, k, peers) for k in range(LOCAL)]
-    near_count, far_count = 2 * NEAR + 1, ring - 2 * NEAR - 1
-    near_plan = pick_plan(near_count, range(LOCAL), ring, columns)
-    far_plans = [pick_plan(far_count, [k], ring, columns) for k in range(LOCAL)]
-    near_rows, far_rows = group_rows(near_count * LOCAL), group_rows(far_count)
-    near_orders = [
-        unpick_matrix(0, near_count, near_rows, k * near_count * CAP, ring) for k in range(LOCAL)
-    ]
-    far_order = unpick_matrix(near_count, far_count, far_rows, 0, ring)
+    both, alone = range(LOCAL), [[k] for k in range(LOCAL)]
+    plans, orders = [], [[] for _ in both]
+    for distances in DISTANCES:
+        count = len(distances)
+        together = distances is not DISTANCES[-1]
+        plans.append([pick_plan(count, g, ring, columns) for g in ([both] if together else alone)])
+        rows = group_rows(count * (LOCAL if together else 1))
+        for k in both:
+            offset = k * count * CAP if together else 0
+            orders[k].append(unpick_matrix(distances, rows, offset, ring))
     table = jnp.pad(rank_of, ((0, 0), (0, EXTRA - EXPERTS)))
     content = whole[:, :KVR]
     key_rope = whole[:, KVR:]
@@ -343,36 +349,33 @@
     normed = (stream * factor * norm_gain).astype(jnp.bfloat16)
 
     own = jnp.concatenate([normed, table], axis=1)
-    up, down = [own], [own]
-    for _ in range(NEAR):
-        up.append(shifted(up[-1], "z", 1))
-        down.append(shifted(down[-1], "z", -1))
-    near = [up[2], up[1], own, down[1], down[2]]
-
     def along_x(picked):
         picked = picked.reshape(columns, -1, D)
         return lax.all_to_all(picked, "x", split_axis=0, concat_axis=0, tiled=True).reshape(-1, D)
 
-    first = pick_rows(near_plan, near)
-    first, upper, lower = lax.optimization_barrier((first, up[NEAR], down[NEAR]))
-    upper, lower = shifted(upper, "z", 1), shifted(lower, "z", -1)
+    up1, down1 = shifted(own, "z", 1), shifted(own, "z", -1)
+    up2, down2 = shifted(up1, "z", 1), shifted(down1, "z", -1)
+    first = pick_rows(plans[0][0], [up1, own, down1])
+    from_first = along_x(first)
+    second = pick_rows(plans[1][0], [up2, down2])
+    _, up2, down2 = held(first, up2, down2)
+    up3, down3 = shifted(up2, "z", 1), shifted(down2, "z", -1)
+    second, _ = held(second, from_first)
+    from_second = along_x(second)
     half = block_rows // 2
     across = jnp.concatenate(
-        [shifted(upper[:half], "z", 1), shifted(lower[half:], "z", -1)], axis=0
-    )
-    from_near = along_x(first)
-    before, from_far = from_near, []
+        [shifted(up3[:half], "z", 1), shifted(down3[half:], "z", -1)], axis=0
+    )
+    before, from_last = from_second, []
     for k in range(LOCAL):
-        picked = pick_rows(far_plans[k], [lower, across, upper])
-        picked, _ = lax.optimization_barrier((picked, before))
+        picked = pick_rows(plans[2][k], [down3, across, up3])
+        picked, _ = held(picked, before)
         before = along_x(picked)
-        from_far.append(before)
+        from_last.append(before)
     items = peers * CAP
     returned = [
         exchanged(
-            run_expert(
-                (from_near, from_far[k]), (near_orders[k], far_order), weights[k], items
-            ),
+            run_expert((from_first, from_second, from_last[k]), orders[k], weights[k], items),
             peers,
         )
         for k in range(LOCAL)

time: 240 us -> 235 us (0.979)
  waiting for transfers between devices: 105 us -> 98.6 us
  Pallas kernels: 42.1 us -> 37.4 us
  starting transfers between devices: 45.3 us -> 48.8 us
    ppermute x12, waiting for transfers between devices: 46.4 us -> 39.7 us  [shifted(): lax.ppermute(rows, axis, [(i, (i + by) % length) for i in range(length)])]
    pallas_call x2, Pallas kernels: 9.4 us -> 4.65 us  [combine_rows(): pl.pallas_call(combine_kernel, out_shape=jax.ShapeDtypeStruct(base.shape,...]
    all_to_all x3 -> x4, starting transfers between devices: 11.5 us -> 15.6 us  [along_x(): lax.all_to_all(picked, 'x', split_axis=0, concat_axis=0, tiled=True)]
    unnamed x44 -> x48, local copies, waits for them, and re-layouts: 7.82 us -> 9.22 us
    pallas_call x3 -> x4, Pallas kernels: 5.76 us -> 5.99 us  [pick_rows(): pl.pallas_call(pick_kernel, out_shape=jax.ShapeDtypeStruct((total, D), jn...]
    all_to_all x3 -> x4, waiting for transfers between devices: 9.37 us -> 9.16 us  [along_x(): lax.all_to_all(picked, 'x', split_axis=0, concat_axis=0, tiled=True)]
  transfers between devices with their start and end apart: 19 -> 20, of which waited for: 15 -> 13; matrix products, arithmetic and copies ran while one was open for 10% -> 11% of each run, Pallas kernels for 16% -> 15%
where the time goes in v6:
time: 235 us; the launch traced here: 234 us
  waiting for transfers between devices  98.6 us (42%)
  starting transfers between devices  48.8 us (21%)
  Pallas kernels  37.4 us (16%)
  matrix products  14.4 us (6%)
  between operations  14.1 us (6%)
  local copies, waits for them, and re-layouts  13.4 us (6%)
  other arithmetic  7.42 us (3%)
    ppermute x12, waiting for transfers between devices, shifted(): lax.ppermute(rows, axis, [(i, (i + by) % length) for i in range(length)])  39.7 us
    all_to_all x2, waiting for transfers between devices, exchanged(): lax.all_to_all(rows.reshape(peers, BLOCK, WIDTH), ('x', 'z'), split_axis=...  37.1 us
    pallas_call x2, Pallas kernels, run_expert(): pl.pallas_call(expert_kernel, out_shape=jax.ShapeDtypeStruct((total, WIDT...  26.7 us
    ppermute x12, starting transfers between devices, shifted(): lax.ppermute(rows, axis, [(i, (i + by) % length) for i in range(length)])  17.8 us
    all_to_all x4, starting transfers between devices, along_x(): lax.all_to_all(picked, 'x', split_axis=0, concat_axis=0, tiled=True)  15.6 us
    all_to_all x2, starting transfers between devices, exchanged(): lax.all_to_all(rows.reshape(peers, BLOCK, WIDTH), ('x', 'z'), split_axis=...  15.4 us
    all_gather x2, waiting for transfers between devices, body(): weights.append(lax.all_gather(stack, ('y', 'core'), axis=0))  12.5 us
    unnamed x48, local copies, waits for them, and re-layouts  9.22 us
  transfers between devices with their start and end apart: 20, of which 13 were waited for; matrix products, arithmetic and copies ran while one was open for 11% of the time, Pallas kernels for 15%

profile of v6, /device:TPU:32, one launch (start us, length us, event | category | flops | bytes accessed | tf_op | source)
XLA Modules:
  0.0 234.1 jit_solution(10574030527709322984)
XLA Ops:
  13.1 1.7 collective-permute-start.1
  14.7 2.0 collective-permute-start.2
  20.9 1.8 collective-permute-done.2
  34.9 2.0 collective-permute-start.4
  37.3 12.3 %collective-permute-done.4.refs_0_ = bf16[128,2176]{1,0:T(8,128)(2,1)S(1)} collective-permute-done((bf16[128,2176]{1,0:T(8,128)(2,1)S(1)}, bf16[128,2176]{1,0:T(8,128)(2,1)S(1)}, u32[]{:S(2)}, u32[]{:S(2)}) %collective-permute-start.4) | collective-permute-done | bytes 557088 | tf_op jit(solution)/shard_map/ppermute | solution.py:81
  49.6 1.9 collective-permute-start.6
  51.5 2.2 collective-permute-start.7
  54.1 1.8 pick_rows.4
  55.9 4.3 %all-to-all-start = ((bf16[4,80,2048]{2,1,0:T(8,128)(2,1)}), bf16[4,80,2048]{2,1,0:T(8,128)(2,1)}, u32[]{:S(2)}, u32[]{:S(2)}) async-start(bf16[4,80,2048]{2,1,0:T(8,128)(2,1)} %bitcast.14), calls=%async_computation | async-start | bytes 2621440 | tf_op jit(solution)/shard_map/all_to_all | solution.py:354
  60.2 6.1 %collective-permute-done.6.refs_0_ = bf16[128,2176]{1,0:T(8,128)(2,1)S(1)} collective-permute-done((bf16[128,2176]{1,0:T(8,128)(2,1)S(1)}, bf16[128,2176]{1,0:T(8,128)(2,1)S(1)}, u32[]{:S(2)}, u32[]{:S(2)}) %collective-permute-start.6) | collective-permute-done | bytes 557088 | tf_op jit(solution)/shard_map/ppermute | solution.py:81
  66.8 3.0 %collective-permute-start.9 = (bf16[128,2176]{1,0:T(8,128)(2,1)S(1)}, bf16[128,2176]{1,0:T(8,128)(2,1)S(1)}, u32[]{:S(2)}, u32[]{:S(2)}) collective-permute-start(bf16[128,2176]{1,0:T(8,128)(2,1)S(1)} %collective-permute-done.6.refs_0_), channel_id=1, source_target_pairs={{0,1},{1,2},{2,3},{3,4},{4,5},{5,6},{6,7},{7,0},{8,9},{9,10},{10,1... | collective-permute-start | bytes 1671176 | tf_op jit(solution)/shard_map/ppermute | solution.py:81
  70.0 11.1 %collective-permute-done.9.refs_2_ = bf16[128,2176]{1,0:T(8,128)(2,1)S(1)} collective-permute-done((bf16[128,2176]{1,0:T(8,128)(2,1)S(1)}, bf16[128,2176]{1,0:T(8,128)(2,1)S(1)}, u32[]{:S(2)}, u32[]{:S(2)}) %collective-permute-start.9) | collective-permute-done | bytes 557088 | tf_op jit(solution)/shard_map/ppermute | solution.py:81
  81.1 2.1 collective-permute-start.10
  85.0 4.4 %all-to-all-start.1 = ((bf16[4,56,2048]{2,1,0:T(8,128)(2,1)}), bf16[4,56,2048]{2,1,0:T(8,128)(2,1)}, u32[]{:S(2)}, u32[]{:S(2)}) async-start(bf16[4,56,2048]{2,1,0:T(8,128)(2,1)} %bitcast.16), calls=%async_computation.1 | async-start | bytes 1835008 | tf_op jit(solution)/shard_map/all_to_all | solution.py:354
  90.5 6.0 %collective-permute-done.11 = bf16[64,2176]{1,0:T(8,128)(2,1)S(1)} collective-permute-done((bf16[64,2176]{1,0:T(8,128)(2,1)S(1)}, bf16[64,2176]{1,0:T(8,128)(2,1)S(1)}, u32[]{:S(2)}, u32[]{:S(2)}) %collective-permute-start.11) | collective-permute-done | bytes 278560 | tf_op jit(solution)/shard_map/ppermute | solution.py:81
  98.0 2.8 %all-to-all-done.1 = bf16[4,56,2048]{2,1,0:T(8,128)(2,1)} async-done(((bf16[4,56,2048]{2,1,0:T(8,128)(2,1)}), bf16[4,56,2048]{2,1,0:T(8,128)(2,1)}, u32[]{:S(2)}, u32[]{:S(2)}) %all-to-all-start.1) | async-done | bytes 917536 | tf_op jit(solution)/shard_map/all_to_all | solution.py:354
  100.8 3.5 %all-to-all-start.2 = ((bf16[4,40,2048]{2,1,0:T(8,128)(2,1)}), bf16[4,40,2048]{2,1,0:T(8,128)(2,1)S(1)}, u32[]{:S(2)}, u32[]{:S(2)}) async-start(bf16[4,40,2048]{2,1,0:T(8,128)(2,1)} %bitcast.18), calls=%async_computation.2 | async-start | bytes 1310720 | tf_op jit(solution)/shard_map/all_to_all | solution.py:354
  106.6 6.4 %all-to-all-done.2 = bf16[4,40,2048]{2,1,0:T(8,128)(2,1)S(1)} async-done(((bf16[4,40,2048]{2,1,0:T(8,128)(2,1)}), bf16[4,40,2048]{2,1,0:T(8,128)(2,1)S(1)}, u32[]{:S(2)}, u32[]{:S(2)}) %all-to-all-start.2) | async-done | bytes 655392 | tf_op jit(solution)/shard_map/all_to_all | solution.py:354
  113.0 3.5 %all-to-all-start.3 = ((bf16[4,40,2048]{2,1,0:T(8,128)(2,1)}), bf16[4,40,2048]{2,1,0:T(8,128)(2,1)S(1)}, u32[]{:S(2)}, u32[]{:S(2)}) async-start(bf16[4,40,2048]{2,1,0:T(8,128)(2,1)} %bitcast.20), calls=%async_computation.3 | async-start | bytes 1310720 | tf_op jit(solution)/shard_map/all_to_all | solution.py:354
  118.2 13.5 %run_expert.3 = bf16[3328,256]{1,0:T(8,128)(2,1)} custom-call(bf16[320,2048]{1,0:T(8,128)(2,1)} %bitcast.15.refs_0_, bf16[224,2048]{1,0:T(8,128)(2,1)} %bitcast.17.refs_1_, bf16[160,2048]{1,0:T(8,128)(2,1)} %bitcast.77, bf16[208,160]{1,0:T(8,128)(2,1)} %get-tuple-element.25.refs_3_, bf16[208,112]{1,0:T(8,128)(2,1)} %get-tuple-element.23.refs_4_, ...), custom_call_target="tpu_custom_call" | custom-call | tf_op jit(solution)/shard_map/run_expert/pallas_call | solution.py:223
  132.5 9.8 %all-to-all-start.5 = ((bf16[32,104,256]{2,1,0:T(8,128)(2,1)}), bf16[32,104,256]{2,1,0:T(8,128)(2,1)S(1)}, u32[]{:S(2)}, u32[]{:S(2)}) async-start(bf16[32,104,256]{2,1,0:T(8,128)(2,1)} %bitcast.76), calls=%async_computation.5 | async-start | bytes 3407872 | tf_op jit(solution)/shard_map/all_to_all | solution.py:44
  142.3 12.5 %all-gather.5.cloned.1.call-done = bf16[24,2048,128]{2,1,0:T(8,128)(2,1)} async-done(((bf16[3,2048,128]{2,1,0:T(8,128)(2,1)}), bf16[24,2048,128]{2,1,0:T(8,128)(2,1)}) %all-gather.5.cloned.1.call-update) | async-done | bytes 12582928 | tf_op jit(solution)/shard_map/all_gather | solution.py:293
  154.8 13.3 %run_expert.2 = bf16[3328,256]{1,0:T(8,128)(2,1)} custom-call(bf16[320,2048]{1,0:T(8,128)(2,1)} %bitcast.15.refs_0_, bf16[224,2048]{1,0:T(8,128)(2,1)} %bitcast.17.refs_1_, bf16[160,2048]{1,0:T(8,128)(2,1)} %bitcast.78, bf16[208,160]{1,0:T(8,128)(2,1)} %get-tuple-element.26.refs_3_, bf16[208,112]{1,0:T(8,128)(2,1)} %get-tuple-element.24.refs_4_, ...), custom_call_target="tpu_custom_call" | custom-call | tf_op jit(solution)/shard_map/run_expert/pallas_call | solution.py:223
  168.1 11.6 %all-to-all-done.5 = bf16[32,104,256]{2,1,0:T(8,128)(2,1)S(1)} async-done(((bf16[32,104,256]{2,1,0:T(8,128)(2,1)}), bf16[32,104,256]{2,1,0:T(8,128)(2,1)S(1)}, u32[]{:S(2)}, u32[]{:S(2)}) %all-to-all-start.5) | async-done | bytes 1703968 | tf_op jit(solution)/shard_map/all_to_all | solution.py:44
  179.7 5.6 %all-to-all-start.4 = ((bf16[32,104,256]{2,1,0:T(8,128)(2,1)}), bf16[32,104,256]{2,1,0:T(8,128)(2,1)S(1)}, u32[]{:S(2)}, u32[]{:S(2)}) async-start(bf16[32,104,256]{2,1,0:T(8,128)(2,1)} %bitcast.75), calls=%async_computation.4 | async-start | bytes 3407872 | tf_op jit(solution)/shard_map/all_to_all | solution.py:44
  185.4 1.9 convolution_compare_fusion.1
  187.3 1.9 convolution_compare_fusion
  189.1 2.6 %fusion.combine_ref = bf16[128,3328]{1,0:T(8,128)(2,1)} fusion(pred[128,3328]{1,0:T(32,128)(4,1)S(1)} %convolution_compare_fusion.1, s32[3328]{0:T(1024)S(1)} %broadcast_add_fusion, bf16[128,64]{0,1:T(8,128)(2,1)S(1)} %select_reduce_fusion), kind=kOutput, calls=%fused_computation.4 | convolution fusion | flops 55590912 | bytes 1307648 | tf_op jit(solution)/shard_map/dot_general | solution.py:70
  191.8 1.8 fusion.1.combine_ref
  193.6 1.9 combine_rows.2.base_ref
  196.5 25.6 %all-to-all-done.4 = bf16[32,104,256]{2,1,0:T(8,128)(2,1)S(1)} async-done(((bf16[32,104,256]{2,1,0:T(8,128)(2,1)}), bf16[32,104,256]{2,1,0:T(8,128)(2,1)S(1)}, u32[]{:S(2)}, u32[]{:S(2)}) %all-to-all-start.4) | async-done | bytes 1703968 | tf_op jit(solution)/shard_map/all_to_all | solution.py:44
  224.6 2.7 %combine_rows.3 = bf16[128,2048]{1,0:T(8,128)(2,1)} custom-call(bf16[128,3328]{1,0:T(8,128)(2,1)S(1)} %copy-done.6, bf16[3328,256]{1,0:T(8,128)(2,1)S(1)} %bitcast.68, f32[128,2048]{1,0:T(8,128)S(1)} %copy-done.5), custom_call_target="tpu_custom_call" | custom-call | tf_op jit(solution)/shard_map/combine_rows/pallas_call | solution.py:260
  (148 shorter events, 36.8 us)
Async XLA Ops:
  6.5 18.4 %copy-start = (bf16[512,1024]{1,0:T(8,128)(2,1)S(1)}, bf16[512,1024]{1,0:T(8,128)(2,1)}, u32[]{:S(2)}) copy-start(bf16[512,1024]{1,0:T(8,128)(2,1)} %param.18) | copy-start | bytes 3145732
  6.5 111.6 %all-gather.7.cloned.1.call-start = ((), (), s32[]{:S(2)}) async-start(), calls=%async_computation.7 | async-start | bytes 14155776 | tf_op jit(solution)/shard_map/all_gather | solution.py:293
  6.5 1.6 copy-start.11
  6.5 1.9 copy-start.12
  10.0 144.9 %all-gather.5.cloned.1.call-start = ((), (), s32[]{:S(2)}) async-start(), calls=%async_computation.6 | async-start | bytes 14155776 | tf_op jit(solution)/shard_map/all_gather | solution.py:293
  10.0 6.7 %copy-start.16 = (s32[1,128,6]{1,0,2:T(1,128)S(1)}, s32[1,128,6]{1,0,2:T(1,128)}, u32[]{:S(2)}) copy-start(s32[1,128,6]{1,0,2:T(1,128)} %param.22) | copy-start | bytes 9220
  10.1 6.8 %copy-start.18 = (s32[4]{0:T(128)S(1)}, s32[4]{0:T(128)}, u32[]{:S(2)}) copy-start(s32[4]{0:T(128)} %constant.319.clone) | copy-start | bytes 52
  10.1 7.2 %copy-start.7 = (s32[16]{0:T(128)S(1)}, s32[16]{0:T(128)}, u32[]{:S(2)}) copy-start(s32[16]{0:T(128)} %param.17) | copy-start | bytes 196
  11.4 7.8 %collective-permute-start = (bf16[128,576]{0,1:T(8,128)(2,1)S(1)}, bf16[128,576]{0,1:T(8,128)(2,1)S(1)}, u32[]{:S(2)}, u32[]{:S(2)}) collective-permute-start(bf16[128,576]{0,1:T(8,128)(2,1)S(1)} %bitcast.82), channel_id=1, source_target_pairs={{0,64},{64,128},{128,192},{192,0},{1,65},{65,129},{129,193},{193,1... | collective-permute-start | bytes 442376 | tf_op jit(solution)/shard_map/ppermute | solution.py:81
  13.1 7.8 %collective-permute-start.1 = (bf16[128,576]{0,1:T(8,128)(2,1)S(1)}, bf16[128,576]{0,1:T(8,128)(2,1)S(1)}, u32[]{:S(2)}, u32[]{:S(2)}) collective-permute-start(bf16[128,576]{0,1:T(8,128)(2,1)S(1)} %bitcast.83), channel_id=1, source_target_pairs={{0,192},{64,0},{128,64},{192,128},{1,193},{65,1},{129,65},{193,129... | collective-permute-start | bytes 442376 | tf_op jit(solution)/shard_map/ppermute | solution.py:81
  14.7 8.0 %collective-permute-start.2 = (bf16[128,576]{0,1:T(8,128)(2,1)S(1)}, bf16[128,576]{0,1:T(8,128)(2,1)S(1)}, u32[]{:S(2)}, u32[]{:S(2)}) collective-permute-start(bf16[128,576]{0,1:T(8,128)(2,1)S(1)} %bitcast.84), channel_id=1, source_target_pairs={{0,128},{64,192},{128,0},{192,64},{1,129},{65,193},{129,1},{193,65... | collective-permute-start | bytes 442376 | tf_op jit(solution)/shard_map/ppermute | solution.py:81
  22.8 2.1 collective-permute-start.3
  30.7 2.2 copy-start.8
  30.7 2.3 copy-start.14
  34.9 14.8 %collective-permute-start.4 = (bf16[128,2176]{1,0:T(8,128)(2,1)S(1)}, bf16[128,2176]{1,0:T(8,128)(2,1)S(1)}, u32[]{:S(2)}, u32[]{:S(2)}) collective-permute-start(bf16[128,2176]{1,0:T(8,128)(2,1)S(1)} %fusion.30.refs_1_), channel_id=1, source_target_pairs={{0,1},{1,2},{2,3},{3,4},{4,5},{5,6},{6,7},{7,0},{8,9},{9,10},{10,1... | collective-permute-start | bytes 1671176 | tf_op jit(solution)/shard_map/ppermute | solution.py:81
  36.8 14.7 %collective-permute-start.5 = (bf16[128,2176]{1,0:T(8,128)(2,1)S(1)}, bf16[128,2176]{1,0:T(8,128)(2,1)S(1)}, u32[]{:S(2)}, u32[]{:S(2)}) collective-permute-start(bf16[128,2176]{1,0:T(8,128)(2,1)S(1)} %fusion.30.refs_1_), channel_id=1, source_target_pairs={{0,7},{1,0},{2,1},{3,2},{4,3},{5,4},{6,5},{7,6},{8,15},{9,8},{10,9... | collective-permute-start | bytes 1671176 | tf_op jit(solution)/shard_map/ppermute | solution.py:81
  49.6 16.7 %collective-permute-start.6 = (bf16[128,2176]{1,0:T(8,128)(2,1)S(1)}, bf16[128,2176]{1,0:T(8,128)(2,1)S(1)}, u32[]{:S(2)}, u32[]{:S(2)}) collective-permute-start(bf16[128,2176]{1,0:T(8,128)(2,1)S(1)} %collective-permute-done.4.refs_0_), channel_id=1, source_target_pairs={{0,1},{1,2},{2,3},{3,4},{4,5},{5,6},{6,7},{7,0},{8,9},{9,10},{10,1... | collective-permute-start | bytes 1671176 | tf_op jit(solution)/shard_map/ppermute | solution.py:81
  51.5 15.2 %collective-permute-start.7 = (bf16[128,2176]{1,0:T(8,128)(2,1)S(1)}, bf16[128,2176]{1,0:T(8,128)(2,1)S(1)}, u32[]{:S(2)}, u32[]{:S(2)}) collective-permute-start(bf16[128,2176]{1,0:T(8,128)(2,1)S(1)} %collective-permute-done.5.refs_2_), channel_id=1, source_target_pairs={{0,7},{1,0},{2,1},{3,2},{4,3},{5,4},{6,5},{7,6},{8,15},{9,8},{10,9... | collective-permute-start | bytes 1671176 | tf_op jit(solution)/shard_map/ppermute | solution.py:81
  55.9 29.1 %all-to-all-start = ((bf16[4,80,2048]{2,1,0:T(8,128)(2,1)}), bf16[4,80,2048]{2,1,0:T(8,128)(2,1)}, u32[]{:S(2)}, u32[]{:S(2)}) async-start(bf16[4,80,2048]{2,1,0:T(8,128)(2,1)} %bitcast.14), calls=%async_computation | async-start | bytes 2621440 | tf_op jit(solution)/shard_map/all_to_all | solution.py:354
  66.8 14.3 %collective-permute-start.9 = (bf16[128,2176]{1,0:T(8,128)(2,1)S(1)}, bf16[128,2176]{1,0:T(8,128)(2,1)S(1)}, u32[]{:S(2)}, u32[]{:S(2)}) collective-permute-start(bf16[128,2176]{1,0:T(8,128)(2,1)S(1)} %collective-permute-done.6.refs_0_), channel_id=1, source_target_pairs={{0,1},{1,2},{2,3},{3,4},{4,5},{5,6},{6,7},{7,0},{8,9},{9,10},{10,1... | collective-permute-start | bytes 1671176 | tf_op jit(solution)/shard_map/ppermute | solution.py:81
  69.8 19.6 %collective-permute-start.8 = (bf16[128,2176]{1,0:T(8,128)(2,1)S(1)}, bf16[128,2176]{1,0:T(8,128)(2,1)S(1)}, u32[]{:S(2)}, u32[]{:S(2)}) collective-permute-start(bf16[128,2176]{1,0:T(8,128)(2,1)S(1)} %collective-permute-done.7.refs_1_), channel_id=1, source_target_pairs={{0,7},{1,0},{2,1},{3,2},{4,3},{5,4},{6,5},{7,6},{8,15},{9,8},{10,9... | collective-permute-start | bytes 1671176 | tf_op jit(solution)/shard_map/ppermute | solution.py:81
  81.1 9.4 %collective-permute-start.10 = (bf16[64,2176]{1,0:T(8,128)(2,1)S(1)}, bf16[64,2176]{1,0:T(8,128)(2,1)S(1)}, u32[]{:S(2)}, u32[]{:S(2)}) collective-permute-start(bf16[64,2176]{1,0:T(8,128)(2,1)S(1)} %slice.60), channel_id=1, source_target_pairs={{0,1},{1,2},{2,3},{3,4},{4,5},{5,6},{6,7},{7,0},{8,9},{9,10},{10,1... | collective-permute-start | bytes 835592 | tf_op jit(solution)/shard_map/ppermute | solution.py:81
  85.0 15.7 %all-to-all-start.1 = ((bf16[4,56,2048]{2,1,0:T(8,128)(2,1)}), bf16[4,56,2048]{2,1,0:T(8,128)(2,1)}, u32[]{:S(2)}, u32[]{:S(2)}) async-start(bf16[4,56,2048]{2,1,0:T(8,128)(2,1)} %bitcast.16), calls=%async_computation.1 | async-start | bytes 1835008 | tf_op jit(solution)/shard_map/all_to_all | solution.py:354
  89.4 7.1 %collective-permute-start.11 = (bf16[64,2176]{1,0:T(8,128)(2,1)S(1)}, bf16[64,2176]{1,0:T(8,128)(2,1)S(1)}, u32[]{:S(2)}, u32[]{:S(2)}) collective-permute-start(bf16[64,2176]{1,0:T(8,128)(2,1)S(1)} %slice.61), channel_id=1, source_target_pairs={{0,7},{1,0},{2,1},{3,2},{4,3},{5,4},{6,5},{7,6},{8,15},{9,8},{10,9... | collective-permute-start | bytes 835592 | tf_op jit(solution)/shard_map/ppermute | solution.py:81
  100.8 12.2 %all-to-all-start.2 = ((bf16[4,40,2048]{2,1,0:T(8,128)(2,1)}), bf16[4,40,2048]{2,1,0:T(8,128)(2,1)S(1)}, u32[]{:S(2)}, u32[]{:S(2)}) async-start(bf16[4,40,2048]{2,1,0:T(8,128)(2,1)} %bitcast.18), calls=%async_computation.2 | async-start | bytes 1310720 | tf_op jit(solution)/shard_map/all_to_all | solution.py:354
  113.0 5.2 %copy-start.9 = (bf16[4,40,2048]{2,1,0:T(8,128)(2,1)}, bf16[4,40,2048]{2,1,0:T(8,128)(2,1)S(1)}, u32[]{:S(2)}) copy-start(bf16[4,40,2048]{2,1,0:T(8,128)(2,1)S(1)} %all-to-all-done.2) | copy-start | bytes 1966084
  113.0 18.6 %all-to-all-start.3 = ((bf16[4,40,2048]{2,1,0:T(8,128)(2,1)}), bf16[4,40,2048]{2,1,0:T(8,128)(2,1)S(1)}, u32[]{:S(2)}, u32[]{:S(2)}) async-start(bf16[4,40,2048]{2,1,0:T(8,128)(2,1)} %bitcast.20), calls=%async_computation.3 | async-start | bytes 1310720 | tf_op jit(solution)/shard_map/all_to_all | solution.py:354
  132.5 47.1 %all-to-all-start.5 = ((bf16[32,104,256]{2,1,0:T(8,128)(2,1)}), bf16[32,104,256]{2,1,0:T(8,128)(2,1)S(1)}, u32[]{:S(2)}, u32[]{:S(2)}) async-start(bf16[32,104,256]{2,1,0:T(8,128)(2,1)} %bitcast.76), calls=%async_computation.5 | async-start | bytes 3407872 | tf_op jit(solution)/shard_map/all_to_all | solution.py:44
  179.7 5.6 %copy-start.17 = (f32[1,128,6]{1,0,2:T(1,128)S(1)}, f32[1,128,6]{1,0,2:T(1,128)}, u32[]{:S(2)}) copy-start(f32[1,128,6]{1,0,2:T(1,128)} %param.23) | copy-start | bytes 9220
  179.7 42.4 %all-to-all-start.4 = ((bf16[32,104,256]{2,1,0:T(8,128)(2,1)}), bf16[32,104,256]{2,1,0:T(8,128)(2,1)S(1)}, u32[]{:S(2)}, u32[]{:S(2)}) async-start(bf16[32,104,256]{2,1,0:T(8,128)(2,1)} %bitcast.75), calls=%async_computation.4 | async-start | bytes 3407872 | tf_op jit(solution)/shard_map/all_to_all | solution.py:44
  189.1 4.4 %copy-start.3 = (bf16[128,2048]{1,0:T(8,128)(2,1)S(1)}, bf16[128,2048]{1,0:T(8,128)(2,1)}, u32[]{:S(2)}) copy-start(bf16[128,2048]{1,0:T(8,128)(2,1)} %copy-done.2) | copy-start | bytes 1572868
  222.1 5.2 %copy-start.1 = (bf16[512,1024]{1,0:T(8,128)(2,1)S(1)}, bf16[512,1024]{1,0:T(8,128)(2,1)}, u32[]{:S(2)}) copy-start(bf16[512,1024]{1,0:T(8,128)(2,1)} %param.18) | copy-start | bytes 3145732
  (8 other events, 8.7 us)
Sparse Core Ops, SparseCore 0:
  10.1 72.5 all-gather.6
  84.5 70.2 all-gather.4

commit v7 on v6

--- a/solution.py
+++ b/solution.py
@@ -29,15 +29,20 @@
 DISTANCES = ((-1, 0, 1), (-2, 2), (3, 4, -3))
 
 
-def gather_latent(own):
+def gather_latent(own, ready):
     near = [own, shifted(own, "y", 1), shifted(own, "y", -1), shifted(own, "y", 2)]
-    mine = jnp.concatenate(near, axis=0)
+    mine, ready = held(jnp.concatenate(near, axis=0), ready)
     whole = jnp.concatenate([mine, shifted(mine, "core", 1)], axis=0)
     length, cores = lax.axis_size("y"), lax.axis_size("core")
     along = (lax.axis_index("y") + jnp.array([0, -1, 1, -2], jnp.int32)) % length
     core = lax.axis_index("core")
     places = [along * cores + (core + i) % cores for i in range(cores)]
-    return whole, jnp.concatenate(places)
+    return whole, jnp.concatenate(places), ready
+
+
+def gather_weights(shares, local):
+    stack = jnp.concatenate([w[local : local + 1] for w in shares])
+    return lax.all_gather(stack, ("y", "core"), axis=0)
 
 
 def exchanged(rows, peers):
@@ -142,7 +147,7 @@
     )(*plan, *blocks)
 
 
-def unpick_matrix(distances, rows, offset, ring):
+def unpick_places(distances, rows, offset, ring):
     out = jnp.arange(2 * ring * CAP, dtype=jnp.int32)
     distance = ((out // CAP) % ring - lax.axis_index("z")) % ring
     inside, listed = jnp.zeros(out.shape, bool), jnp.zeros_like(out)
@@ -150,8 +155,7 @@
         here = distance == d % ring
         inside, listed = inside | here, jnp.where(here, i, listed)
     at = (out // (ring * CAP)) * rows + offset + listed * CAP + out % CAP
-    col = jnp.arange(2 * rows, dtype=jnp.int32)
-    return (inside[:, None] & (at[:, None] == col[None, :])).astype(jnp.bfloat16)
+    return jnp.where(inside, at, -1)
 
 
 def pack_matrix():
@@ -163,8 +167,8 @@
 
 def expert_kernel(*refs):
     groups = len(DISTANCES)
-    received, orders = refs[:groups], refs[groups : 2 * groups]
-    gate_ref, up_ref, down_ref, out_ref, x_ref, acc_ref = refs[2 * groups :]
+    received, order_ref = refs[:groups], refs[groups]
+    gate_ref, up_ref, down_ref, out_ref, x_ref, acc_ref = refs[groups + 1 :]
     part = pl.program_id(0)
     parts = pl.num_programs(0)
     side = PACK * CHUNKS
@@ -172,13 +176,19 @@
 
     @pl.when(part == 0)
     def _():
-        rows = orders[0].shape[0]
-        for i in range(x_ref.shape[0] // rows):
+        rows = order_ref.shape[0]
+        repeats = x_ref.shape[0] // rows
+        orders = []
+        for g, ref in enumerate(received):
+            col = lax.broadcasted_iota(jnp.int32, (rows, ref.shape[0] // repeats), 1)
+            same = order_ref[:, g : g + 1] == col
+            orders.append(same.astype(jnp.float32).astype(jnp.bfloat16))
+        for i in range(repeats):
             got = 0.0
             for ref, order in zip(received, orders):
                 cols = order.shape[1]
                 got = got + jnp.dot(
-                    order[...],
+                    order,
                     ref[i * cols : (i + 1) * cols, :],
                     preferred_element_type=jnp.float32,
                 )
@@ -215,7 +225,7 @@
             ).astype(jnp.bfloat16)
 
 
-def run_expert(received, orders, weights, items):
+def run_expert(received, order, weights, items):
     total = items * CHUNKS
     shares, _, _, width = weights.shape
     step = FF_BLOCK // width
@@ -225,7 +235,7 @@
         out_shape=jax.ShapeDtypeStruct((total, WIDTH), jnp.bfloat16),
         grid=(shares // step,),
         in_specs=[
-            *(once(a) for a in (*received, *orders)),
+            *(once(a) for a in (*received, order)),
             pl.BlockSpec((step, 1, D, width), lambda f: (f, 0, 0, 0)),
             pl.BlockSpec((step, 1, D, width), lambda f: (f, 1, 0, 0)),
             pl.BlockSpec((step, 1, D, width), lambda f: (f, 2, 0, 0)),
@@ -237,7 +247,7 @@
         ],
         compiler_params=pltpu.CompilerParams(vmem_limit_bytes=54 * MIB),
         name="run_expert",
-    )(*received, *orders, weights, weights, weights)
+    )(*received, order, weights, weights, weights)
 
 
 def combine_kernel(combine_ref, rows_ref, base_ref, out_ref):
@@ -286,11 +296,9 @@
     peers = columns * ring
     block_rows = hidden.shape[1]
     half_rows = block_rows // 2
-    whole, places = gather_latent(latent[0])
-    weights = []
-    for k in range(LOCAL):
-        stack = jnp.concatenate([w[k : k + 1] for w in (w_gate, w_up, w_down)])
-        weights.append(lax.all_gather(stack, ("y", "core"), axis=0))
+    whole, places, query_rows = gather_latent(latent[0], queries[0].T)
+    shares = (w_gate, w_up, w_down)
+    weights = [gather_weights(shares, k) for k in range(LOCAL)]
     seq_rows = whole.shape[0]
     inside = jnp.arange(half_rows, dtype=jnp.int32)
 
@@ -311,21 +319,22 @@
         rows = group_rows(count * (LOCAL if together else 1))
         for k in both:
             offset = k * count * CAP if together else 0
-            orders[k].append(unpick_matrix(distances, rows, offset, ring))
+            orders[k].append(unpick_places(distances, rows, offset, ring))
+    orders = [jnp.stack(places_of, axis=1) for places_of in orders]
     table = jnp.pad(rank_of, ((0, 0), (0, EXTRA - EXPERTS)))
     content = whole[:, :KVR]
     key_rope = whole[:, KVR:]
     key_nope = jnp.dot(content, w_uk, preferred_element_type=jnp.float32).astype(jnp.bfloat16)
     values = jnp.dot(content, w_uv, preferred_element_type=jnp.float32).astype(jnp.bfloat16)
-    query_full = queries[0].reshape(block_rows, HEADS, NOPE + ROPE)
+    query_full = query_rows.reshape(HEADS, NOPE + ROPE, block_rows)
     scores = jnp.einsum(
-        "qhd,khd->hqk",
-        query_full[:, :, :NOPE],
+        "hdq,khd->hqk",
+        query_full[:, :NOPE],
         key_nope.reshape(seq_rows, HEADS, NOPE),
         preferred_element_type=jnp.float32,
     )
     scores = scores + jnp.einsum(
-        "qhr,kr->hqk", query_full[:, :, NOPE:], key_rope, preferred_element_type=jnp.float32
+        "hrq,kr->hqk", query_full[:, NOPE:], key_rope, preferred_element_type=jnp.float32
     )
     scores = scores * (NOPE + ROPE) ** (-0.5)
     visible = positions[None, :] <= own_positions[:, None]
@@ -360,7 +369,7 @@
     second = pick_rows(plans[1][0], [up2, down2])
     _, up2, down2 = held(first, up2, down2)
     up3, down3 = shifted(up2, "z", 1), shifted(down2, "z", -1)
-    second, _ = held(second, from_first)
+    second, _, orders = held(second, from_first, orders)
     from_second = along_x(second)
     half = block_rows // 2
     across = jnp.concatenate(

time: 235 us -> 234 us (level)
    convert_element_type x3 -> x0, other arithmetic: 2.4 us -> none  [unpick_matrix(): (inside[:, None] & (at[:, None] == col[None, :])).astype(jnp.bfloat16)]
    unnamed x48 -> x47, local copies, waits for them, and re-layouts: 9.22 us -> 7.44 us
  transfers between devices with their start and end apart: 20 -> 20, of which waited for: 13 -> 13; matrix products, arithmetic and copies ran while one was open for 11% -> 10% of each run, Pallas kernels for 15% -> 15%
where the time goes in v7:
time: 234 us; the launch traced here: 233 us
  waiting for transfers between devices  99.2 us (42%)
  starting transfers between devices  49.2 us (21%)
  Pallas kernels  37.2 us (16%)
  matrix products  14.7 us (6%)
  between operations  14 us (6%)
  local copies, waits for them, and re-layouts  13.1 us (6%)
  other arithmetic  5.44 us (2%)
    ppermute x12, waiting for transfers between devices, shifted(): lax.ppermute(rows, axis, [(i, (i + by) % length) for i in range(length)])  40.9 us
    all_to_all x2, waiting for transfers between devices, exchanged(): lax.all_to_all(rows.reshape(peers, BLOCK, WIDTH), ('x', 'z'), split_axis=...  35.9 us
    pallas_call x2, Pallas kernels, run_expert(): pl.pallas_call(expert_kernel, out_shape=jax.ShapeDtypeStruct((total, WIDT...  26.7 us
    ppermute x12, starting transfers between devices, shifted(): lax.ppermute(rows, axis, [(i, (i + by) % length) for i in range(length)])  18 us
    all_to_all x4, starting transfers between devices, along_x(): lax.all_to_all(picked, 'x', split_axis=0, concat_axis=0, tiled=True)  15.6 us
    all_to_all x2, starting transfers between devices, exchanged(): lax.all_to_all(rows.reshape(peers, BLOCK, WIDTH), ('x', 'z'), split_axis=...  15.5 us
    all_gather x2, waiting for transfers between devices, gather_weights(): return lax.all_gather(stack, ('y', 'core'), axis=0)  12.4 us
    all_to_all x4, waiting for transfers between devices, along_x(): lax.all_to_all(picked, 'x', split_axis=0, concat_axis=0, tiled=True)  9.98 us
  transfers between devices with their start and end apart: 20, of which 13 were waited for; matrix products, arithmetic and copies ran while one was open for 10% of the time, Pallas kernels for 15%

profile of v7, /device:TPU:32, one launch (start us, length us, event | category | flops | bytes accessed | tf_op | source)
XLA Modules:
  0.0 232.9 jit_solution(16834941102307630917)
XLA Ops:
  14.7 2.0 collective-permute-start.2
  18.9 2.0 collective-permute-done.1
  20.9 1.8 collective-permute-done.2
  35.0 2.2 collective-permute-start.4
  37.5 12.4 %collective-permute-done.4.refs_0_ = bf16[128,2176]{1,0:T(8,128)(2,1)S(1)} collective-permute-done((bf16[128,2176]{1,0:T(8,128)(2,1)S(1)}, bf16[128,2176]{1,0:T(8,128)(2,1)S(1)}, u32[]{:S(2)}, u32[]{:S(2)}) %collective-permute-start.4) | collective-permute-done | bytes 557088 | tf_op jit(solution)/shard_map/ppermute | solution.py:86
  49.9 1.9 collective-permute-start.6
  51.8 2.2 collective-permute-start.7
  54.3 1.8 pick_rows.4
  56.1 4.3 %all-to-all-start = ((bf16[4,80,2048]{2,1,0:T(8,128)(2,1)}), bf16[4,80,2048]{2,1,0:T(8,128)(2,1)}, u32[]{:S(2)}, u32[]{:S(2)}) async-start(bf16[4,80,2048]{2,1,0:T(8,128)(2,1)} %bitcast.14), calls=%async_computation | async-start | bytes 2621440 | tf_op jit(solution)/shard_map/all_to_all | solution.py:363
  60.5 6.1 %collective-permute-done.6.refs_0_ = bf16[128,2176]{1,0:T(8,128)(2,1)S(1)} collective-permute-done((bf16[128,2176]{1,0:T(8,128)(2,1)S(1)}, bf16[128,2176]{1,0:T(8,128)(2,1)S(1)}, u32[]{:S(2)}, u32[]{:S(2)}) %collective-permute-start.6) | collective-permute-done | bytes 557088 | tf_op jit(solution)/shard_map/ppermute | solution.py:86
  67.0 3.0 %collective-permute-start.9 = (bf16[128,2176]{1,0:T(8,128)(2,1)S(1)}, bf16[128,2176]{1,0:T(8,128)(2,1)S(1)}, u32[]{:S(2)}, u32[]{:S(2)}) collective-permute-start(bf16[128,2176]{1,0:T(8,128)(2,1)S(1)} %collective-permute-done.6.refs_0_), channel_id=1, source_target_pairs={{0,1},{1,2},{2,3},{3,4},{4,5},{5,6},{6,7},{7,0},{8,9},{9,10},{10,1... | collective-permute-start | bytes 1671176 | tf_op jit(solution)/shard_map/ppermute | solution.py:86
  70.2 11.0 %collective-permute-done.9.refs_2_ = bf16[128,2176]{1,0:T(8,128)(2,1)S(1)} collective-permute-done((bf16[128,2176]{1,0:T(8,128)(2,1)S(1)}, bf16[128,2176]{1,0:T(8,128)(2,1)S(1)}, u32[]{:S(2)}, u32[]{:S(2)}) %collective-permute-start.9) | collective-permute-done | bytes 557088 | tf_op jit(solution)/shard_map/ppermute | solution.py:86
  81.3 2.1 collective-permute-start.10
  85.3 4.3 %all-to-all-start.1 = ((bf16[4,56,2048]{2,1,0:T(8,128)(2,1)}), bf16[4,56,2048]{2,1,0:T(8,128)(2,1)}, u32[]{:S(2)}, u32[]{:S(2)}) async-start(bf16[4,56,2048]{2,1,0:T(8,128)(2,1)} %bitcast.16), calls=%async_computation.1 | async-start | bytes 1835008 | tf_op jit(solution)/shard_map/all_to_all | solution.py:363
  90.6 6.1 %collective-permute-done.11 = bf16[64,2176]{1,0:T(8,128)(2,1)S(1)} collective-permute-done((bf16[64,2176]{1,0:T(8,128)(2,1)S(1)}, bf16[64,2176]{1,0:T(8,128)(2,1)S(1)}, u32[]{:S(2)}, u32[]{:S(2)}) %collective-permute-start.11) | collective-permute-done | bytes 278560 | tf_op jit(solution)/shard_map/ppermute | solution.py:86
  98.2 2.8 %all-to-all-done.1 = bf16[4,56,2048]{2,1,0:T(8,128)(2,1)} async-done(((bf16[4,56,2048]{2,1,0:T(8,128)(2,1)}), bf16[4,56,2048]{2,1,0:T(8,128)(2,1)}, u32[]{:S(2)}, u32[]{:S(2)}) %all-to-all-start.1) | async-done | bytes 917536 | tf_op jit(solution)/shard_map/all_to_all | solution.py:363
  101.0 3.5 %all-to-all-start.2 = ((bf16[4,40,2048]{2,1,0:T(8,128)(2,1)}), bf16[4,40,2048]{2,1,0:T(8,128)(2,1)S(1)}, u32[]{:S(2)}, u32[]{:S(2)}) async-start(bf16[4,40,2048]{2,1,0:T(8,128)(2,1)} %bitcast.18), calls=%async_computation.2 | async-start | bytes 1310720 | tf_op jit(solution)/shard_map/all_to_all | solution.py:363
  106.0 7.2 %all-to-all-done.2 = bf16[4,40,2048]{2,1,0:T(8,128)(2,1)S(1)} async-done(((bf16[4,40,2048]{2,1,0:T(8,128)(2,1)}), bf16[4,40,2048]{2,1,0:T(8,128)(2,1)S(1)}, u32[]{:S(2)}, u32[]{:S(2)}) %all-to-all-start.2) | async-done | bytes 655392 | tf_op jit(solution)/shard_map/all_to_all | solution.py:363
  113.2 3.5 %all-to-all-start.3 = ((bf16[4,40,2048]{2,1,0:T(8,128)(2,1)}), bf16[4,40,2048]{2,1,0:T(8,128)(2,1)S(1)}, u32[]{:S(2)}, u32[]{:S(2)}) async-start(bf16[4,40,2048]{2,1,0:T(8,128)(2,1)} %bitcast.20), calls=%async_computation.3 | async-start | bytes 1310720 | tf_op jit(solution)/shard_map/all_to_all | solution.py:363
  117.5 13.4 %run_expert.3 = bf16[3328,256]{1,0:T(8,128)(2,1)} custom-call(bf16[320,2048]{1,0:T(8,128)(2,1)} %bitcast.15.refs_0_, bf16[224,2048]{1,0:T(8,128)(2,1)} %bitcast.17.refs_1_, bf16[160,2048]{1,0:T(8,128)(2,1)} %bitcast.72, s32[208,3]{1,0:T(8,128)} %copy.40.refs_3_, bf16[8,3,2048,128]{3,2,1,0:T(8,128)(2,1)} %bitcast.66, bf16[8,3,2048,128]{3,2,1,0:T(8,128)(2,1)} %bitcast.67, ...), custom_call_target="tpu_custom_call" | custom-call | tf_op jit(solution)/shard_map/run_expert/pallas_call | solution.py:233
  131.7 9.9 %all-to-all-start.5 = ((bf16[32,104,256]{2,1,0:T(8,128)(2,1)}), bf16[32,104,256]{2,1,0:T(8,128)(2,1)S(1)}, u32[]{:S(2)}, u32[]{:S(2)}) async-start(bf16[32,104,256]{2,1,0:T(8,128)(2,1)} %bitcast.70), calls=%async_computation.5 | async-start | bytes 3407872 | tf_op jit(solution)/shard_map/all_to_all | solution.py:49
  142.5 12.4 %all-gather.5.cloned.1.call-done = bf16[24,2048,128]{2,1,0:T(8,128)(2,1)} async-done(((bf16[3,2048,128]{2,1,0:T(8,128)(2,1)}), bf16[24,2048,128]{2,1,0:T(8,128)(2,1)}) %all-gather.5.cloned.1.call-update) | async-done | bytes 12582928 | tf_op jit(solution)/shard_map/all_gather | solution.py:45
  154.8 13.3 %run_expert.2 = bf16[3328,256]{1,0:T(8,128)(2,1)} custom-call(bf16[320,2048]{1,0:T(8,128)(2,1)} %bitcast.15.refs_0_, bf16[224,2048]{1,0:T(8,128)(2,1)} %bitcast.17.refs_1_, bf16[160,2048]{1,0:T(8,128)(2,1)} %bitcast.71, s32[208,3]{1,0:T(8,128)} %copy.39.refs_3_, bf16[8,3,2048,128]{3,2,1,0:T(8,128)(2,1)} %bitcast.63, bf16[8,3,2048,128]{3,2,1,0:T(8,128)(2,1)} %bitcast.64, ...), custom_call_target="tpu_custom_call" | custom-call | tf_op jit(solution)/shard_map/run_expert/pallas_call | solution.py:233
  168.1 10.7 %all-to-all-done.5 = bf16[32,104,256]{2,1,0:T(8,128)(2,1)S(1)} async-done(((bf16[32,104,256]{2,1,0:T(8,128)(2,1)}), bf16[32,104,256]{2,1,0:T(8,128)(2,1)S(1)}, u32[]{:S(2)}, u32[]{:S(2)}) %all-to-all-start.5) | async-done | bytes 1703968 | tf_op jit(solution)/shard_map/all_to_all | solution.py:49
  178.8 5.6 %all-to-all-start.4 = ((bf16[32,104,256]{2,1,0:T(8,128)(2,1)}), bf16[32,104,256]{2,1,0:T(8,128)(2,1)S(1)}, u32[]{:S(2)}, u32[]{:S(2)}) async-start(bf16[32,104,256]{2,1,0:T(8,128)(2,1)} %bitcast.69), calls=%async_computation.4 | async-start | bytes 3407872 | tf_op jit(solution)/shard_map/all_to_all | solution.py:49
  184.5 1.9 convolution_compare_fusion
  186.4 1.9 convolution_compare_fusion.1
  188.3 1.8 fusion.1.combine_ref
  190.1 2.6 %fusion.combine_ref = bf16[128,3328]{1,0:T(8,128)(2,1)} fusion(pred[128,3328]{1,0:T(32,128)(4,1)S(1)} %convolution_compare_fusion.1, s32[3328]{0:T(1024)S(1)} %broadcast_add_fusion, bf16[128,64]{0,1:T(8,128)(2,1)S(1)} %select_reduce_fusion), kind=kOutput, calls=%fused_computation.4 | convolution fusion | flops 55590912 | bytes 1307648 | tf_op jit(solution)/shard_map/dot_general | solution.py:75
  192.8 1.9 combine_rows.2.base_ref
  195.7 25.2 %all-to-all-done.4 = bf16[32,104,256]{2,1,0:T(8,128)(2,1)S(1)} async-done(((bf16[32,104,256]{2,1,0:T(8,128)(2,1)}), bf16[32,104,256]{2,1,0:T(8,128)(2,1)S(1)}, u32[]{:S(2)}, u32[]{:S(2)}) %all-to-all-start.4) | async-done | bytes 1703968 | tf_op jit(solution)/shard_map/all_to_all | solution.py:49
  223.4 2.7 %combine_rows.3 = bf16[128,2048]{1,0:T(8,128)(2,1)} custom-call(bf16[128,3328]{1,0:T(8,128)(2,1)S(1)} %copy-done.6, bf16[3328,256]{1,0:T(8,128)(2,1)S(1)} %bitcast.62, f32[128,2048]{1,0:T(8,128)S(1)} %copy-done.5), custom_call_target="tpu_custom_call" | custom-call | tf_op jit(solution)/shard_map/combine_rows/pallas_call | solution.py:270
  (145 shorter events, 35.6 us)
Async XLA Ops:
  6.5 18.4 %copy-start = (bf16[512,1024]{1,0:T(8,128)(2,1)S(1)}, bf16[512,1024]{1,0:T(8,128)(2,1)}, u32[]{:S(2)}) copy-start(bf16[512,1024]{1,0:T(8,128)(2,1)} %param.18) | copy-start | bytes 3145732
  6.5 111.0 %all-gather.7.cloned.1.call-start = ((), (), s32[]{:S(2)}) async-start(), calls=%async_computation.7 | async-start | bytes 14155776 | tf_op jit(solution)/shard_map/all_gather | solution.py:45
  6.5 1.9 copy-start.12
  10.0 144.9 %all-gather.5.cloned.1.call-start = ((), (), s32[]{:S(2)}) async-start(), calls=%async_computation.6 | async-start | bytes 14155776 | tf_op jit(solution)/shard_map/all_gather | solution.py:45
  10.0 6.7 %copy-start.19 = (s32[4]{0:T(128)S(1)}, s32[4]{0:T(128)}, u32[]{:S(2)}) copy-start(s32[4]{0:T(128)} %constant.320.clone) | copy-start | bytes 52
  10.1 7.0 %copy-start.7 = (s32[16]{0:T(128)S(1)}, s32[16]{0:T(128)}, u32[]{:S(2)}) copy-start(s32[16]{0:T(128)} %param.17) | copy-start | bytes 196
  11.4 7.3 %copy-start.14 = (bf16[1,128,1536]{2,1,0:T(8,128)(2,1)S(1)}, bf16[1,128,1536]{2,1,0:T(8,128)(2,1)}, u32[]{:S(2)}) copy-start(bf16[1,128,1536]{2,1,0:T(8,128)(2,1)} %param.15) | copy-start | bytes 1179652
  11.4 7.5 %copy-start.17 = (s32[1,128,6]{1,0,2:T(1,128)S(1)}, s32[1,128,6]{1,0,2:T(1,128)}, u32[]{:S(2)}) copy-start(s32[1,128,6]{1,0,2:T(1,128)} %param.22) | copy-start | bytes 9220
  11.4 7.5 %collective-permute-start = (bf16[128,576]{0,1:T(8,128)(2,1)S(1)}, bf16[128,576]{0,1:T(8,128)(2,1)S(1)}, u32[]{:S(2)}, u32[]{:S(2)}) collective-permute-start(bf16[128,576]{0,1:T(8,128)(2,1)S(1)} %bitcast.77), channel_id=1, source_target_pairs={{0,64},{64,128},{128,192},{192,0},{1,65},{65,129},{129,193},{193,1... | collective-permute-start | bytes 442376 | tf_op jit(solution)/shard_map/ppermute | solution.py:86
  13.1 7.8 %collective-permute-start.1 = (bf16[128,576]{0,1:T(8,128)(2,1)S(1)}, bf16[128,576]{0,1:T(8,128)(2,1)S(1)}, u32[]{:S(2)}, u32[]{:S(2)}) collective-permute-start(bf16[128,576]{0,1:T(8,128)(2,1)S(1)} %bitcast.78), channel_id=1, source_target_pairs={{0,192},{64,0},{128,64},{192,128},{1,193},{65,1},{129,65},{193,129... | collective-permute-start | bytes 442376 | tf_op jit(solution)/shard_map/ppermute | solution.py:86
  14.7 8.0 %collective-permute-start.2 = (bf16[128,576]{0,1:T(8,128)(2,1)S(1)}, bf16[128,576]{0,1:T(8,128)(2,1)S(1)}, u32[]{:S(2)}, u32[]{:S(2)}) collective-permute-start(bf16[128,576]{0,1:T(8,128)(2,1)S(1)} %bitcast.79), channel_id=1, source_target_pairs={{0,128},{64,192},{128,0},{192,64},{1,129},{65,193},{129,1},{193,65... | collective-permute-start | bytes 442376 | tf_op jit(solution)/shard_map/ppermute | solution.py:86
  22.8 2.1 collective-permute-start.3
  30.8 2.2 copy-start.8
  30.8 2.3 copy-start.13
  35.0 14.9 %collective-permute-start.4 = (bf16[128,2176]{1,0:T(8,128)(2,1)S(1)}, bf16[128,2176]{1,0:T(8,128)(2,1)S(1)}, u32[]{:S(2)}, u32[]{:S(2)}) collective-permute-start(bf16[128,2176]{1,0:T(8,128)(2,1)S(1)} %fusion.28.refs_1_), channel_id=1, source_target_pairs={{0,1},{1,2},{2,3},{3,4},{4,5},{5,6},{6,7},{7,0},{8,9},{9,10},{10,1... | collective-permute-start | bytes 1671176 | tf_op jit(solution)/shard_map/ppermute | solution.py:86
  37.1 14.7 %collective-permute-start.5 = (bf16[128,2176]{1,0:T(8,128)(2,1)S(1)}, bf16[128,2176]{1,0:T(8,128)(2,1)S(1)}, u32[]{:S(2)}, u32[]{:S(2)}) collective-permute-start(bf16[128,2176]{1,0:T(8,128)(2,1)S(1)} %fusion.28.refs_1_), channel_id=1, source_target_pairs={{0,7},{1,0},{2,1},{3,2},{4,3},{5,4},{6,5},{7,6},{8,15},{9,8},{10,9... | collective-permute-start | bytes 1671176 | tf_op jit(solution)/shard_map/ppermute | solution.py:86
  49.9 16.6 %collective-permute-start.6 = (bf16[128,2176]{1,0:T(8,128)(2,1)S(1)}, bf16[128,2176]{1,0:T(8,128)(2,1)S(1)}, u32[]{:S(2)}, u32[]{:S(2)}) collective-permute-start(bf16[128,2176]{1,0:T(8,128)(2,1)S(1)} %collective-permute-done.4.refs_0_), channel_id=1, source_target_pairs={{0,1},{1,2},{2,3},{3,4},{4,5},{5,6},{6,7},{7,0},{8,9},{9,10},{10,1... | collective-permute-start | bytes 1671176 | tf_op jit(solution)/shard_map/ppermute | solution.py:86
  51.8 15.2 %collective-permute-start.7 = (bf16[128,2176]{1,0:T(8,128)(2,1)S(1)}, bf16[128,2176]{1,0:T(8,128)(2,1)S(1)}, u32[]{:S(2)}, u32[]{:S(2)}) collective-permute-start(bf16[128,2176]{1,0:T(8,128)(2,1)S(1)} %collective-permute-done.5.refs_2_), channel_id=1, source_target_pairs={{0,7},{1,0},{2,1},{3,2},{4,3},{5,4},{6,5},{7,6},{8,15},{9,8},{10,9... | collective-permute-start | bytes 1671176 | tf_op jit(solution)/shard_map/ppermute | solution.py:86
  56.1 29.1 %all-to-all-start = ((bf16[4,80,2048]{2,1,0:T(8,128)(2,1)}), bf16[4,80,2048]{2,1,0:T(8,128)(2,1)}, u32[]{:S(2)}, u32[]{:S(2)}) async-start(bf16[4,80,2048]{2,1,0:T(8,128)(2,1)} %bitcast.14), calls=%async_computation | async-start | bytes 2621440 | tf_op jit(solution)/shard_map/all_to_all | solution.py:363
  67.0 14.2 %collective-permute-start.9 = (bf16[128,2176]{1,0:T(8,128)(2,1)S(1)}, bf16[128,2176]{1,0:T(8,128)(2,1)S(1)}, u32[]{:S(2)}, u32[]{:S(2)}) collective-permute-start(bf16[128,2176]{1,0:T(8,128)(2,1)S(1)} %collective-permute-done.6.refs_0_), channel_id=1, source_target_pairs={{0,1},{1,2},{2,3},{3,4},{4,5},{5,6},{6,7},{7,0},{8,9},{9,10},{10,1... | collective-permute-start | bytes 1671176 | tf_op jit(solution)/shard_map/ppermute | solution.py:86
  70.1 19.5 %collective-permute-start.8 = (bf16[128,2176]{1,0:T(8,128)(2,1)S(1)}, bf16[128,2176]{1,0:T(8,128)(2,1)S(1)}, u32[]{:S(2)}, u32[]{:S(2)}) collective-permute-start(bf16[128,2176]{1,0:T(8,128)(2,1)S(1)} %collective-permute-done.7.refs_1_), channel_id=1, source_target_pairs={{0,7},{1,0},{2,1},{3,2},{4,3},{5,4},{6,5},{7,6},{8,15},{9,8},{10,9... | collective-permute-start | bytes 1671176 | tf_op jit(solution)/shard_map/ppermute | solution.py:86
  81.3 9.4 %collective-permute-start.10 = (bf16[64,2176]{1,0:T(8,128)(2,1)S(1)}, bf16[64,2176]{1,0:T(8,128)(2,1)S(1)}, u32[]{:S(2)}, u32[]{:S(2)}) collective-permute-start(bf16[64,2176]{1,0:T(8,128)(2,1)S(1)} %slice.60), channel_id=1, source_target_pairs={{0,1},{1,2},{2,3},{3,4},{4,5},{5,6},{6,7},{7,0},{8,9},{9,10},{10,1... | collective-permute-start | bytes 835592 | tf_op jit(solution)/shard_map/ppermute | solution.py:86
  85.3 15.7 %all-to-all-start.1 = ((bf16[4,56,2048]{2,1,0:T(8,128)(2,1)}), bf16[4,56,2048]{2,1,0:T(8,128)(2,1)}, u32[]{:S(2)}, u32[]{:S(2)}) async-start(bf16[4,56,2048]{2,1,0:T(8,128)(2,1)} %bitcast.16), calls=%async_computation.1 | async-start | bytes 1835008 | tf_op jit(solution)/shard_map/all_to_all | solution.py:363
  89.6 7.1 %collective-permute-start.11 = (bf16[64,2176]{1,0:T(8,128)(2,1)S(1)}, bf16[64,2176]{1,0:T(8,128)(2,1)S(1)}, u32[]{:S(2)}, u32[]{:S(2)}) collective-permute-start(bf16[64,2176]{1,0:T(8,128)(2,1)S(1)} %slice.61), channel_id=1, source_target_pairs={{0,7},{1,0},{2,1},{3,2},{4,3},{5,4},{6,5},{7,6},{8,15},{9,8},{10,9... | collective-permute-start | bytes 835592 | tf_op jit(solution)/shard_map/ppermute | solution.py:86
  101.0 12.2 %all-to-all-start.2 = ((bf16[4,40,2048]{2,1,0:T(8,128)(2,1)}), bf16[4,40,2048]{2,1,0:T(8,128)(2,1)S(1)}, u32[]{:S(2)}, u32[]{:S(2)}) async-start(bf16[4,40,2048]{2,1,0:T(8,128)(2,1)} %bitcast.18), calls=%async_computation.2 | async-start | bytes 1310720 | tf_op jit(solution)/shard_map/all_to_all | solution.py:363
  113.2 4.3 %copy-start.10 = (bf16[4,40,2048]{2,1,0:T(8,128)(2,1)}, bf16[4,40,2048]{2,1,0:T(8,128)(2,1)S(1)}, u32[]{:S(2)}) copy-start(bf16[4,40,2048]{2,1,0:T(8,128)(2,1)S(1)} %all-to-all-done.2) | copy-start | bytes 1966084
  113.2 17.7 %all-to-all-start.3 = ((bf16[4,40,2048]{2,1,0:T(8,128)(2,1)}), bf16[4,40,2048]{2,1,0:T(8,128)(2,1)S(1)}, u32[]{:S(2)}, u32[]{:S(2)}) async-start(bf16[4,40,2048]{2,1,0:T(8,128)(2,1)} %bitcast.20), calls=%async_computation.3 | async-start | bytes 1310720 | tf_op jit(solution)/shard_map/all_to_all | solution.py:363
  131.7 47.1 %all-to-all-start.5 = ((bf16[32,104,256]{2,1,0:T(8,128)(2,1)}), bf16[32,104,256]{2,1,0:T(8,128)(2,1)S(1)}, u32[]{:S(2)}, u32[]{:S(2)}) async-start(bf16[32,104,256]{2,1,0:T(8,128)(2,1)} %bitcast.70), calls=%async_computation.5 | async-start | bytes 3407872 | tf_op jit(solution)/shard_map/all_to_all | solution.py:49
  178.8 5.6 %copy-start.18 = (f32[1,128,6]{1,0,2:T(1,128)S(1)}, f32[1,128,6]{1,0,2:T(1,128)}, u32[]{:S(2)}) copy-start(f32[1,128,6]{1,0,2:T(1,128)} %param.23) | copy-start | bytes 9220
  178.8 42.1 %all-to-all-start.4 = ((bf16[32,104,256]{2,1,0:T(8,128)(2,1)}), bf16[32,104,256]{2,1,0:T(8,128)(2,1)S(1)}, u32[]{:S(2)}, u32[]{:S(2)}) async-start(bf16[32,104,256]{2,1,0:T(8,128)(2,1)} %bitcast.69), calls=%async_computation.4 | async-start | bytes 3407872 | tf_op jit(solution)/shard_map/all_to_all | solution.py:49
  188.3 4.5 %copy-start.3 = (bf16[128,2048]{1,0:T(8,128)(2,1)S(1)}, bf16[128,2048]{1,0:T(8,128)(2,1)}, u32[]{:S(2)}) copy-start(bf16[128,2048]{1,0:T(8,128)(2,1)} %copy-done.2) | copy-start | bytes 1572868
  220.9 5.2 %copy-start.1 = (bf16[512,1024]{1,0:T(8,128)(2,1)S(1)}, bf16[512,1024]{1,0:T(8,128)(2,1)}, u32[]{:S(2)}) copy-start(bf16[512,1024]{1,0:T(8,128)(2,1)} %param.18) | copy-start | bytes 3145732
  (9 other events, 10.3 us)
Sparse Core Ops, SparseCore 0:
  10.1 72.5 all-gather.6
  84.5 70.3 all-gather.4

commit v8 on v7

--- a/solution.py
+++ b/solution.py
@@ -40,9 +40,30 @@
     return whole, jnp.concatenate(places), ready
 
 
-def gather_weights(shares, local):
-    stack = jnp.concatenate([w[local : local + 1] for w in shares])
-    return lax.all_gather(stack, ("y", "core"), axis=0)
+def pack_kernel(*refs):
+    shares, packed, sems = refs[:3], refs[3:-1], refs[-1]
+    copies = [
+        pltpu.make_async_copy(share.at[k], packed[k].at[i], sems.at[k, i])
+        for k in range(len(packed))
+        for i, share in enumerate(shares)
+    ]
+    for copy in copies:
+        copy.start()
+    for copy in copies:
+        copy.wait()
+
+
+def pack_weights(shares):
+    hbm = pl.BlockSpec(memory_space=pltpu.HBM)
+    one = jax.ShapeDtypeStruct((len(shares), *shares[0].shape[1:]), shares[0].dtype)
+    return pl.pallas_call(
+        pack_kernel,
+        out_shape=[one] * LOCAL,
+        in_specs=[hbm] * len(shares),
+        out_specs=[hbm] * LOCAL,
+        scratch_shapes=[pltpu.SemaphoreType.DMA((LOCAL, len(shares)))],
+        name="pack_weights",
+    )(*shares)
 
 
 def exchanged(rows, peers):
@@ -297,8 +318,8 @@
     block_rows = hidden.shape[1]
     half_rows = block_rows // 2
     whole, places, query_rows = gather_latent(latent[0], queries[0].T)
-    shares = (w_gate, w_up, w_down)
-    weights = [gather_weights(shares, k) for k in range(LOCAL)]
+    packed = pack_weights((w_gate, w_up, w_down))
+    weights = [lax.all_gather(one, ("y", "core"), axis=0) for one in packed]
     seq_rows = whole.shape[0]
     inside = jnp.arange(half_rows, dtype=jnp.int32)
 

time: 234 us -> 327 us (1.40)
  Pallas kernels: 37.2 us -> 134 us
    pallas_call x0 -> x1, Pallas kernels: none -> 96.4 us  [pack_weights(): pl.pallas_call(pack_kernel, out_shape=[one] * LOCAL, in_specs=[hbm] * len...]
    unnamed x47 -> x43, local copies, waits for them, and re-layouts: 7.44 us -> 7.2 us
  transfers between devices with their start and end apart: 20 -> 20, of which waited for: 13 -> 13; matrix products, arithmetic and copies ran while one was open for 10% -> 7% of each run, Pallas kernels for 15% -> 11%
where the time goes in v8:
time: 327 us; the launch traced here: 326 us
  Pallas kernels  134 us (41%)
  waiting for transfers between devices  101 us (31%)
  starting transfers between devices  48.6 us (15%)
  matrix products  14.7 us (4%)
  between operations  14 us (4%)
  local copies, waits for them, and re-layouts  11.4 us (3%)
    pallas_call x1, Pallas kernels, pack_weights(): pl.pallas_call(pack_kernel, out_shape=[one] * LOCAL, in_specs=[hbm] * len...  96.4 us
    ppermute x12, waiting for transfers between devices, shifted(): lax.ppermute(rows, axis, [(i, (i + by) % length) for i in range(length)])  41 us
    all_to_all x2, waiting for transfers between devices, exchanged(): lax.all_to_all(rows.reshape(peers, BLOCK, WIDTH), ('x', 'z'), split_axis=...  35.9 us
    pallas_call x2, Pallas kernels, run_expert(): pl.pallas_call(expert_kernel, out_shape=jax.ShapeDtypeStruct((total, WIDT...  26.7 us
    ppermute x12, starting transfers between devices, shifted(): lax.ppermute(rows, axis, [(i, (i + by) % length) for i in range(length)])  17.5 us
    all_to_all x4, starting transfers between devices, along_x(): lax.all_to_all(picked, 'x', split_axis=0, concat_axis=0, tiled=True)  15.6 us
    all_to_all x2, starting transfers between devices, exchanged(): lax.all_to_all(rows.reshape(peers, BLOCK, WIDTH), ('x', 'z'), split_axis=...  15.5 us
    all_gather x2, waiting for transfers between devices, body(): weights = [lax.all_gather(one, ('y', 'core'), axis=0) for one in packed]  13.2 us
  transfers between devices with their start and end apart: 20, of which 13 were waited for; matrix products, arithmetic and copies ran while one was open for 7% of the time, Pallas kernels for 11%

profile of v8, /device:TPU:32, one launch (start us, length us, event | category | flops | bytes accessed | tf_op | source)
XLA Modules:
  0.0 326.1 jit_solution(14151058918499181598)
XLA Ops:
  6.5 96.4 %pack_weights.1 = (bf16[3,2048,128]{2,1,0:T(8,128)(2,1)}, bf16[3,2048,128]{2,1,0:T(8,128)(2,1)}) custom-call(bf16[2,2048,128]{2,1,0:T(8,128)(2,1)} %refs_0_.1, bf16[2,2048,128]{2,1,0:T(8,128)(2,1)} %refs_1_.1, bf16[2,2048,128]{2,1,0:T(8,128)(2,1)} %refs_2_.1), custom_call_target="tpu_custom_call" | custom-call | tf_op jit(solution)/shard_map/pack_weights/pallas_call | solution.py:59
  107.1 2.0 collective-permute-start.2
  111.3 2.0 collective-permute-done.1
  127.6 1.8 collective-permute-start.4
  130.0 12.4 %collective-permute-done.4.refs_0_ = bf16[128,2176]{1,0:T(8,128)(2,1)S(1)} collective-permute-done((bf16[128,2176]{1,0:T(8,128)(2,1)S(1)}, bf16[128,2176]{1,0:T(8,128)(2,1)S(1)}, u32[]{:S(2)}, u32[]{:S(2)}) %collective-permute-start.4) | collective-permute-done | bytes 557088 | tf_op jit(solution)/shard_map/ppermute | solution.py:107
  142.4 1.8 collective-permute-start.6
  144.2 2.1 collective-permute-start.7
  146.6 1.8 pick_rows.4
  148.4 4.3 %all-to-all-start = ((bf16[4,80,2048]{2,1,0:T(8,128)(2,1)}), bf16[4,80,2048]{2,1,0:T(8,128)(2,1)}, u32[]{:S(2)}, u32[]{:S(2)}) async-start(bf16[4,80,2048]{2,1,0:T(8,128)(2,1)} %bitcast.14), calls=%async_computation | async-start | bytes 2621440 | tf_op jit(solution)/shard_map/all_to_all | solution.py:384
  152.7 6.1 %collective-permute-done.6.refs_0_ = bf16[128,2176]{1,0:T(8,128)(2,1)S(1)} collective-permute-done((bf16[128,2176]{1,0:T(8,128)(2,1)S(1)}, bf16[128,2176]{1,0:T(8,128)(2,1)S(1)}, u32[]{:S(2)}, u32[]{:S(2)}) %collective-permute-start.6) | collective-permute-done | bytes 557088 | tf_op jit(solution)/shard_map/ppermute | solution.py:107
  159.3 3.0 collective-permute-start.9
  162.5 11.0 %collective-permute-done.9.refs_2_ = bf16[128,2176]{1,0:T(8,128)(2,1)S(1)} collective-permute-done((bf16[128,2176]{1,0:T(8,128)(2,1)S(1)}, bf16[128,2176]{1,0:T(8,128)(2,1)S(1)}, u32[]{:S(2)}, u32[]{:S(2)}) %collective-permute-start.9) | collective-permute-done | bytes 557088 | tf_op jit(solution)/shard_map/ppermute | solution.py:107
  173.5 2.1 collective-permute-start.10
  177.6 4.3 %all-to-all-start.1 = ((bf16[4,56,2048]{2,1,0:T(8,128)(2,1)}), bf16[4,56,2048]{2,1,0:T(8,128)(2,1)}, u32[]{:S(2)}, u32[]{:S(2)}) async-start(bf16[4,56,2048]{2,1,0:T(8,128)(2,1)} %bitcast.16), calls=%async_computation.1 | async-start | bytes 1835008 | tf_op jit(solution)/shard_map/all_to_all | solution.py:384
  182.9 6.1 %collective-permute-done.11 = bf16[64,2176]{1,0:T(8,128)(2,1)S(1)} collective-permute-done((bf16[64,2176]{1,0:T(8,128)(2,1)S(1)}, bf16[64,2176]{1,0:T(8,128)(2,1)S(1)}, u32[]{:S(2)}, u32[]{:S(2)}) %collective-permute-start.11) | collective-permute-done | bytes 278560 | tf_op jit(solution)/shard_map/ppermute | solution.py:107
  190.4 2.8 all-to-all-done.1
  193.3 3.5 %all-to-all-start.2 = ((bf16[4,40,2048]{2,1,0:T(8,128)(2,1)}), bf16[4,40,2048]{2,1,0:T(8,128)(2,1)S(1)}, u32[]{:S(2)}, u32[]{:S(2)}) async-start(bf16[4,40,2048]{2,1,0:T(8,128)(2,1)} %bitcast.18), calls=%async_computation.2 | async-start | bytes 1310720 | tf_op jit(solution)/shard_map/all_to_all | solution.py:384
  198.4 7.2 %all-to-all-done.2 = bf16[4,40,2048]{2,1,0:T(8,128)(2,1)S(1)} async-done(((bf16[4,40,2048]{2,1,0:T(8,128)(2,1)}), bf16[4,40,2048]{2,1,0:T(8,128)(2,1)S(1)}, u32[]{:S(2)}, u32[]{:S(2)}) %all-to-all-start.2) | async-done | bytes 655392 | tf_op jit(solution)/shard_map/all_to_all | solution.py:384
  205.5 3.5 %all-to-all-start.3 = ((bf16[4,40,2048]{2,1,0:T(8,128)(2,1)}), bf16[4,40,2048]{2,1,0:T(8,128)(2,1)S(1)}, u32[]{:S(2)}, u32[]{:S(2)}) async-start(bf16[4,40,2048]{2,1,0:T(8,128)(2,1)} %bitcast.20), calls=%async_computation.3 | async-start | bytes 1310720 | tf_op jit(solution)/shard_map/all_to_all | solution.py:384
  209.8 13.4 %run_expert.3 = bf16[3328,256]{1,0:T(8,128)(2,1)} custom-call(bf16[320,2048]{1,0:T(8,128)(2,1)} %bitcast.15.refs_0_, bf16[224,2048]{1,0:T(8,128)(2,1)} %bitcast.17.refs_1_, bf16[160,2048]{1,0:T(8,128)(2,1)} %bitcast.72, s32[208,3]{1,0:T(8,128)} %copy.40.refs_3_, bf16[8,3,2048,128]{3,2,1,0:T(8,128)(2,1)} %bitcast.66, bf16[8,3,2048,128]{3,2,1,0:T(8,128)(2,1)} %bitcast.67, ...), custom_call_target="tpu_custom_call" | custom-call | tf_op jit(solution)/shard_map/run_expert/pallas_call | solution.py:254
  224.0 9.9 %all-to-all-start.5 = ((bf16[32,104,256]{2,1,0:T(8,128)(2,1)}), bf16[32,104,256]{2,1,0:T(8,128)(2,1)S(1)}, u32[]{:S(2)}, u32[]{:S(2)}) async-start(bf16[32,104,256]{2,1,0:T(8,128)(2,1)} %bitcast.70), calls=%async_computation.5 | async-start | bytes 3407872 | tf_op jit(solution)/shard_map/all_to_all | solution.py:70
  234.7 13.2 %all-gather.5.cloned.1.call-done = bf16[24,2048,128]{2,1,0:T(8,128)(2,1)} async-done(((bf16[3,2048,128]{2,1,0:T(8,128)(2,1)}), bf16[24,2048,128]{2,1,0:T(8,128)(2,1)}) %all-gather.5.cloned.1.call-update) | async-done | bytes 12582928 | tf_op jit(solution)/shard_map/all_gather | solution.py:322
  248.0 13.3 %run_expert.2 = bf16[3328,256]{1,0:T(8,128)(2,1)} custom-call(bf16[320,2048]{1,0:T(8,128)(2,1)} %bitcast.15.refs_0_, bf16[224,2048]{1,0:T(8,128)(2,1)} %bitcast.17.refs_1_, bf16[160,2048]{1,0:T(8,128)(2,1)} %bitcast.71, s32[208,3]{1,0:T(8,128)} %copy.39.refs_3_, bf16[8,3,2048,128]{3,2,1,0:T(8,128)(2,1)} %bitcast.63, bf16[8,3,2048,128]{3,2,1,0:T(8,128)(2,1)} %bitcast.64, ...), custom_call_target="tpu_custom_call" | custom-call | tf_op jit(solution)/shard_map/run_expert/pallas_call | solution.py:254
  261.2 10.0 %all-to-all-done.5 = bf16[32,104,256]{2,1,0:T(8,128)(2,1)S(1)} async-done(((bf16[32,104,256]{2,1,0:T(8,128)(2,1)}), bf16[32,104,256]{2,1,0:T(8,128)(2,1)S(1)}, u32[]{:S(2)}, u32[]{:S(2)}) %all-to-all-start.5) | async-done | bytes 1703968 | tf_op jit(solution)/shard_map/all_to_all | solution.py:70
  271.2 5.6 %all-to-all-start.4 = ((bf16[32,104,256]{2,1,0:T(8,128)(2,1)}), bf16[32,104,256]{2,1,0:T(8,128)(2,1)S(1)}, u32[]{:S(2)}, u32[]{:S(2)}) async-start(bf16[32,104,256]{2,1,0:T(8,128)(2,1)} %bitcast.69), calls=%async_computation.4 | async-start | bytes 3407872 | tf_op jit(solution)/shard_map/all_to_all | solution.py:70
  276.9 1.9 convolution_compare_fusion
  278.8 1.9 convolution_compare_fusion.1
  280.7 1.8 fusion.1.combine_ref
  282.5 2.6 fusion.combine_ref
  285.2 1.9 combine_rows.2.base_ref
  288.1 26.0 %all-to-all-done.4 = bf16[32,104,256]{2,1,0:T(8,128)(2,1)S(1)} async-done(((bf16[32,104,256]{2,1,0:T(8,128)(2,1)}), bf16[32,104,256]{2,1,0:T(8,128)(2,1)S(1)}, u32[]{:S(2)}, u32[]{:S(2)}) %all-to-all-start.4) | async-done | bytes 1703968 | tf_op jit(solution)/shard_map/all_to_all | solution.py:70
  316.5 2.7 combine_rows.3
  (138 shorter events, 33.7 us)
Async XLA Ops:
  6.5 110.8 %copy-start = (bf16[512,1024]{1,0:T(8,128)(2,1)S(1)}, bf16[512,1024]{1,0:T(8,128)(2,1)}, u32[]{:S(2)}) copy-start(bf16[512,1024]{1,0:T(8,128)(2,1)} %param.18) | copy-start | bytes 3145732
  6.5 203.3 %all-gather.7.cloned.1.call-start = ((), (), s32[]{:S(2)}) async-start(), calls=%async_computation.7 | async-start | bytes 14155776 | tf_op jit(solution)/shard_map/all_gather | solution.py:322
  103.0 6.1 %copy-start.17 = (s32[4]{0:T(128)S(1)}, s32[4]{0:T(128)}, u32[]{:S(2)}) copy-start(s32[4]{0:T(128)} %constant.320.clone) | copy-start | bytes 52
  103.0 6.5 %copy-start.7 = (s32[16]{0:T(128)S(1)}, s32[16]{0:T(128)}, u32[]{:S(2)}) copy-start(s32[16]{0:T(128)} %param.17) | copy-start | bytes 196
  103.1 8.0 %copy-start.12 = (bf16[1,128,1536]{2,1,0:T(8,128)(2,1)S(1)}, bf16[1,128,1536]{2,1,0:T(8,128)(2,1)}, u32[]{:S(2)}) copy-start(bf16[1,128,1536]{2,1,0:T(8,128)(2,1)} %param.15) | copy-start | bytes 1179652
  103.1 144.9 %all-gather.5.cloned.1.call-start = ((), (), s32[]{:S(2)}) async-start(), calls=%async_computation.6 | async-start | bytes 14155776 | tf_op jit(solution)/shard_map/all_gather | solution.py:322
  103.1 8.2 %copy-start.15 = (s32[1,128,6]{1,0,2:T(1,128)S(1)}, s32[1,128,6]{1,0,2:T(1,128)}, u32[]{:S(2)}) copy-start(s32[1,128,6]{1,0,2:T(1,128)} %param.22) | copy-start | bytes 9220
  103.9 7.4 %collective-permute-start = (bf16[128,576]{0,1:T(8,128)(2,1)S(1)}, bf16[128,576]{0,1:T(8,128)(2,1)S(1)}, u32[]{:S(2)}, u32[]{:S(2)}) collective-permute-start(bf16[128,576]{0,1:T(8,128)(2,1)S(1)} %bitcast.77), channel_id=1, source_target_pairs={{0,64},{64,128},{128,192},{192,0},{1,65},{65,129},{129,193},{193,1... | collective-permute-start | bytes 442376 | tf_op jit(solution)/shard_map/ppermute | solution.py:107
  105.5 7.8 %collective-permute-start.1 = (bf16[128,576]{0,1:T(8,128)(2,1)S(1)}, bf16[128,576]{0,1:T(8,128)(2,1)S(1)}, u32[]{:S(2)}, u32[]{:S(2)}) collective-permute-start(bf16[128,576]{0,1:T(8,128)(2,1)S(1)} %bitcast.78), channel_id=1, source_target_pairs={{0,192},{64,0},{128,64},{192,128},{1,193},{65,1},{129,65},{193,129... | collective-permute-start | bytes 442376 | tf_op jit(solution)/shard_map/ppermute | solution.py:107
  107.1 8.0 %collective-permute-start.2 = (bf16[128,576]{0,1:T(8,128)(2,1)S(1)}, bf16[128,576]{0,1:T(8,128)(2,1)S(1)}, u32[]{:S(2)}, u32[]{:S(2)}) collective-permute-start(bf16[128,576]{0,1:T(8,128)(2,1)S(1)} %bitcast.79), channel_id=1, source_target_pairs={{0,128},{64,192},{128,0},{192,64},{1,129},{65,193},{129,1},{193,65... | collective-permute-start | bytes 442376 | tf_op jit(solution)/shard_map/ppermute | solution.py:107
  115.2 2.1 collective-permute-start.3
  120.5 1.5 copy-start.18
  123.4 2.2 copy-start.8
  123.4 2.3 copy-start.11
  127.6 14.8 %collective-permute-start.4 = (bf16[128,2176]{1,0:T(8,128)(2,1)S(1)}, bf16[128,2176]{1,0:T(8,128)(2,1)S(1)}, u32[]{:S(2)}, u32[]{:S(2)}) collective-permute-start(bf16[128,2176]{1,0:T(8,128)(2,1)S(1)} %fusion.28.refs_1_), channel_id=1, source_target_pairs={{0,1},{1,2},{2,3},{3,4},{4,5},{5,6},{6,7},{7,0},{8,9},{9,10},{10,1... | collective-permute-start | bytes 1671176 | tf_op jit(solution)/shard_map/ppermute | solution.py:107
  129.4 14.7 %collective-permute-start.5 = (bf16[128,2176]{1,0:T(8,128)(2,1)S(1)}, bf16[128,2176]{1,0:T(8,128)(2,1)S(1)}, u32[]{:S(2)}, u32[]{:S(2)}) collective-permute-start(bf16[128,2176]{1,0:T(8,128)(2,1)S(1)} %fusion.28.refs_1_), channel_id=1, source_target_pairs={{0,7},{1,0},{2,1},{3,2},{4,3},{5,4},{6,5},{7,6},{8,15},{9,8},{10,9... | collective-permute-start | bytes 1671176 | tf_op jit(solution)/shard_map/ppermute | solution.py:107
  142.4 16.4 %collective-permute-start.6 = (bf16[128,2176]{1,0:T(8,128)(2,1)S(1)}, bf16[128,2176]{1,0:T(8,128)(2,1)S(1)}, u32[]{:S(2)}, u32[]{:S(2)}) collective-permute-start(bf16[128,2176]{1,0:T(8,128)(2,1)S(1)} %collective-permute-done.4.refs_0_), channel_id=1, source_target_pairs={{0,1},{1,2},{2,3},{3,4},{4,5},{5,6},{6,7},{7,0},{8,9},{9,10},{10,1... | collective-permute-start | bytes 1671176 | tf_op jit(solution)/shard_map/ppermute | solution.py:107
  144.2 15.1 %collective-permute-start.7 = (bf16[128,2176]{1,0:T(8,128)(2,1)S(1)}, bf16[128,2176]{1,0:T(8,128)(2,1)S(1)}, u32[]{:S(2)}, u32[]{:S(2)}) collective-permute-start(bf16[128,2176]{1,0:T(8,128)(2,1)S(1)} %collective-permute-done.5.refs_2_), channel_id=1, source_target_pairs={{0,7},{1,0},{2,1},{3,2},{4,3},{5,4},{6,5},{7,6},{8,15},{9,8},{10,9... | collective-permute-start | bytes 1671176 | tf_op jit(solution)/shard_map/ppermute | solution.py:107
  148.4 29.2 %all-to-all-start = ((bf16[4,80,2048]{2,1,0:T(8,128)(2,1)}), bf16[4,80,2048]{2,1,0:T(8,128)(2,1)}, u32[]{:S(2)}, u32[]{:S(2)}) async-start(bf16[4,80,2048]{2,1,0:T(8,128)(2,1)} %bitcast.14), calls=%async_computation | async-start | bytes 2621440 | tf_op jit(solution)/shard_map/all_to_all | solution.py:384
  159.3 14.2 %collective-permute-start.9 = (bf16[128,2176]{1,0:T(8,128)(2,1)S(1)}, bf16[128,2176]{1,0:T(8,128)(2,1)S(1)}, u32[]{:S(2)}, u32[]{:S(2)}) collective-permute-start(bf16[128,2176]{1,0:T(8,128)(2,1)S(1)} %collective-permute-done.6.refs_0_), channel_id=1, source_target_pairs={{0,1},{1,2},{2,3},{3,4},{4,5},{5,6},{6,7},{7,0},{8,9},{9,10},{10,1... | collective-permute-start | bytes 1671176 | tf_op jit(solution)/shard_map/ppermute | solution.py:107
  162.3 19.5 %collective-permute-start.8 = (bf16[128,2176]{1,0:T(8,128)(2,1)S(1)}, bf16[128,2176]{1,0:T(8,128)(2,1)S(1)}, u32[]{:S(2)}, u32[]{:S(2)}) collective-permute-start(bf16[128,2176]{1,0:T(8,128)(2,1)S(1)} %collective-permute-done.7.refs_1_), channel_id=1, source_target_pairs={{0,7},{1,0},{2,1},{3,2},{4,3},{5,4},{6,5},{7,6},{8,15},{9,8},{10,9... | collective-permute-start | bytes 1671176 | tf_op jit(solution)/shard_map/ppermute | solution.py:107
  173.5 9.3 %collective-permute-start.10 = (bf16[64,2176]{1,0:T(8,128)(2,1)S(1)}, bf16[64,2176]{1,0:T(8,128)(2,1)S(1)}, u32[]{:S(2)}, u32[]{:S(2)}) collective-permute-start(bf16[64,2176]{1,0:T(8,128)(2,1)S(1)} %slice.36), channel_id=1, source_target_pairs={{0,1},{1,2},{2,3},{3,4},{4,5},{5,6},{6,7},{7,0},{8,9},{9,10},{10,1... | collective-permute-start | bytes 835592 | tf_op jit(solution)/shard_map/ppermute | solution.py:107
  177.6 15.7 %all-to-all-start.1 = ((bf16[4,56,2048]{2,1,0:T(8,128)(2,1)}), bf16[4,56,2048]{2,1,0:T(8,128)(2,1)}, u32[]{:S(2)}, u32[]{:S(2)}) async-start(bf16[4,56,2048]{2,1,0:T(8,128)(2,1)} %bitcast.16), calls=%async_computation.1 | async-start | bytes 1835008 | tf_op jit(solution)/shard_map/all_to_all | solution.py:384
  181.9 7.1 %collective-permute-start.11 = (bf16[64,2176]{1,0:T(8,128)(2,1)S(1)}, bf16[64,2176]{1,0:T(8,128)(2,1)S(1)}, u32[]{:S(2)}, u32[]{:S(2)}) collective-permute-start(bf16[64,2176]{1,0:T(8,128)(2,1)S(1)} %slice.37), channel_id=1, source_target_pairs={{0,7},{1,0},{2,1},{3,2},{4,3},{5,4},{6,5},{7,6},{8,15},{9,8},{10,9... | collective-permute-start | bytes 835592 | tf_op jit(solution)/shard_map/ppermute | solution.py:107
  193.3 12.2 %all-to-all-start.2 = ((bf16[4,40,2048]{2,1,0:T(8,128)(2,1)}), bf16[4,40,2048]{2,1,0:T(8,128)(2,1)S(1)}, u32[]{:S(2)}, u32[]{:S(2)}) async-start(bf16[4,40,2048]{2,1,0:T(8,128)(2,1)} %bitcast.18), calls=%async_computation.2 | async-start | bytes 1310720 | tf_op jit(solution)/shard_map/all_to_all | solution.py:384
  205.5 4.3 %copy-start.10 = (bf16[4,40,2048]{2,1,0:T(8,128)(2,1)}, bf16[4,40,2048]{2,1,0:T(8,128)(2,1)S(1)}, u32[]{:S(2)}) copy-start(bf16[4,40,2048]{2,1,0:T(8,128)(2,1)S(1)} %all-to-all-done.2) | copy-start | bytes 1966084
  205.5 17.6 %all-to-all-start.3 = ((bf16[4,40,2048]{2,1,0:T(8,128)(2,1)}), bf16[4,40,2048]{2,1,0:T(8,128)(2,1)S(1)}, u32[]{:S(2)}, u32[]{:S(2)}) async-start(bf16[4,40,2048]{2,1,0:T(8,128)(2,1)} %bitcast.20), calls=%async_computation.3 | async-start | bytes 1310720 | tf_op jit(solution)/shard_map/all_to_all | solution.py:384
  224.0 47.2 %all-to-all-start.5 = ((bf16[32,104,256]{2,1,0:T(8,128)(2,1)}), bf16[32,104,256]{2,1,0:T(8,128)(2,1)S(1)}, u32[]{:S(2)}, u32[]{:S(2)}) async-start(bf16[32,104,256]{2,1,0:T(8,128)(2,1)} %bitcast.70), calls=%async_computation.5 | async-start | bytes 3407872 | tf_op jit(solution)/shard_map/all_to_all | solution.py:70
  271.2 5.6 %copy-start.16 = (f32[1,128,6]{1,0,2:T(1,128)S(1)}, f32[1,128,6]{1,0,2:T(1,128)}, u32[]{:S(2)}) copy-start(f32[1,128,6]{1,0,2:T(1,128)} %param.23) | copy-start | bytes 9220
  271.2 42.8 %all-to-all-start.4 = ((bf16[32,104,256]{2,1,0:T(8,128)(2,1)}), bf16[32,104,256]{2,1,0:T(8,128)(2,1)S(1)}, u32[]{:S(2)}, u32[]{:S(2)}) async-start(bf16[32,104,256]{2,1,0:T(8,128)(2,1)} %bitcast.69), calls=%async_computation.4 | async-start | bytes 3407872 | tf_op jit(solution)/shard_map/all_to_all | solution.py:70
  280.7 4.5 %copy-start.3 = (bf16[128,2048]{1,0:T(8,128)(2,1)S(1)}, bf16[128,2048]{1,0:T(8,128)(2,1)}, u32[]{:S(2)}) copy-start(bf16[128,2048]{1,0:T(8,128)(2,1)} %copy-done.2) | copy-start | bytes 1572868
  314.0 5.2 %copy-start.1 = (bf16[512,1024]{1,0:T(8,128)(2,1)S(1)}, bf16[512,1024]{1,0:T(8,128)(2,1)}, u32[]{:S(2)}) copy-start(bf16[512,1024]{1,0:T(8,128)(2,1)} %param.18) | copy-start | bytes 3145732
  (7 other events, 6.9 us)
Sparse Core Ops, SparseCore 0:
  103.2 72.5 all-gather.6
  177.6 70.2 all-gather.4
